TPU v7x, 32 devices: a whole 2x2x4 slice. The times are simulated.
32 devices in a mesh: fsdp: 8 (over z, x), mp: 4 (over y, core).
Axes of the slice: x: 2, y: 2, z: 4, core: 2. Of those that a mesh axis runs over, the one named last changes fastest.
Arguments:
- hidden_in: bfloat16 [16, 832, 768], P('fsdp'), may hold values from -6 to 6
- segment_ids: int32 [16, 832], P('fsdp'), may hold values from 0 to 16, never falling along the last dimension, each value on 1 to 128 neighbouring positions
- pad_flags: int32 [16, 832], P('fsdp'), may hold values 0 or 1
- gain1: bfloat16 [768], P('fsdp'), may hold values from 0.5 to 1.5
- shift1: bfloat16 [768], P('fsdp'), may hold values from -3 to 3
- w_query: bfloat16 [768, 768], P('fsdp', 'mp'), may hold values from -0.21875 to 0.21875
- b_query: bfloat16 [768], P('mp'), may hold values from -3 to 3
- w_key: bfloat16 [768, 768], P('fsdp', 'mp'), may hold values from -0.21875 to 0.21875
- w_value: bfloat16 [768, 768], P('fsdp', 'mp'), may hold values from -0.21875 to 0.21875
- b_value: bfloat16 [768], P('mp'), may hold values from -3 to 3
- w_out: bfloat16 [768, 768], P('mp', 'fsdp'), may hold values from -1.25 to 1.25
- b_out: bfloat16 [768], P('fsdp'), may hold values from -3 to 3
- gain2: bfloat16 [768], P('fsdp'), may hold values from 0.5 to 1.5
- shift2: bfloat16 [768], P('fsdp'), may hold values from -3 to 3
- w_up: bfloat16 [768, 768], P('fsdp', 'mp'), may hold values from -0.21875 to 0.21875
- b_up: bfloat16 [768], P('mp'), may hold values from -3 to 3
- w_down: bfloat16 [768, 768], P('mp', 'fsdp'), may hold values from -0.3125 to 0.3125
- b_down: bfloat16 [768], P('fsdp'), may hold values from -3 to 3
- cotangent: bfloat16 [16, 832, 768], P('fsdp'), may hold values from -6 to 6
Outputs:
- out_hidden: bfloat16 [16, 832, 768], P('fsdp')
- grad_hidden: bfloat16 [16, 832, 768], P('fsdp')
- grad_gain1: float32 [768], P('fsdp')
- grad_shift1: float32 [768], P('fsdp')
- grad_w_query: float32 [768, 768], P('fsdp', 'mp')
- grad_b_query: float32 [768], P('mp')
- grad_w_key: float32 [768, 768], P('fsdp', 'mp')
- grad_w_value: float32 [768, 768], P('fsdp', 'mp')
- grad_b_value: float32 [768], P('mp')
- grad_w_out: float32 [768, 768], P('mp', 'fsdp')
- grad_b_out: float32 [768], P('fsdp')
- grad_gain2: float32 [768], P('fsdp')
- grad_shift2: float32 [768], P('fsdp')
- grad_w_up: float32 [768, 768], P('fsdp', 'mp')
- grad_b_up: float32 [768], P('mp')
- grad_w_down: float32 [768, 768], P('mp', 'fsdp')
- grad_b_down: float32 [768], P('fsdp')
Inputs may be any that keep to these rules, and one draw needn't show every extreme that they name: `segment_ids`: within a row, segment numbers never fall, and each molecule of a row has 1 to 128 tokens.
All inputs are finite; a program needn't handle non-finite values. No bound on the sum of `pad_flags` on one device may be relied on, other than what follows from the above.
Results may differ from a plain program's by a relative error of at most 0.015.
Values may be sent and summed in bfloat16 or wider, within the bound.
No kernel may reach another device: no remote copies, remote signals or barrier semaphores. Data moves between devices by JAX's collectives and lax.ppermute only.
A program may use at most 192 MiB of HBM per device.

v0:
```python
import functools
import math

import jax
import jax.numpy as jnp
from jax import lax
from jax.experimental import pallas as pl
from jax.experimental.pallas import tpu as pltpu
from jax.sharding import PartitionSpec as P

HD = 24
PAD = 32
MOST = 128
BOTH = ("fsdp", "mp")
EPS = 1e-05
F32 = jnp.float32
BF16 = jnp.bfloat16
LOG2 = math.log2(math.e) / math.sqrt(HD)
SCALE = 1.0 / math.sqrt(HD)
GELU = math.sqrt(2.0 / math.pi)


def send(value, fs, mp, flip_f, flip_m):
    pairs = [(f * mp + m, (f ^ flip_f) * mp + (m ^ flip_m)) for f in range(fs) for m in range(mp)]
    return lax.ppermute(value, BOTH, pairs)


def dot_nn(left, right):
    return lax.dot_general(left, right, (((1,), (0,)), ((), ())), preferred_element_type=F32)


def dot_nt(left, right):
    return lax.dot_general(left, right, (((1,), (1,)), ((), ())), preferred_element_type=F32)


def dot_tn(left, right):
    return lax.dot_general(left, right, (((0,), (0,)), ((), ())), preferred_element_type=F32)


def norm_parts(values):
    centre = jnp.mean(values, axis=-1, keepdims=True)
    centered = values - centre
    inverse = lax.rsqrt(jnp.mean(centered * centered, axis=-1, keepdims=True) + EPS)
    return centered * inverse, inverse


def norm_back(grad, normed, inverse, gain):
    scaled = grad * gain
    return inverse * (
        scaled
        - jnp.mean(scaled, axis=-1, keepdims=True)
        - normed * jnp.mean(scaled * normed, axis=-1, keepdims=True)
    )


def call(body, outs, operands, scratch=(), scalars=0, us=0.1, mib=6):
    whole = pl.BlockSpec(memory_space=pltpu.VMEM)
    few = pl.BlockSpec(memory_space=pltpu.SMEM)
    return pl.pallas_call(
        body,
        out_shape=tuple(jax.ShapeDtypeStruct(s, d) for s, d in outs),
        in_specs=[few] * scalars + [whole] * (len(operands) - scalars),
        out_specs=tuple(whole for _ in outs),
        scratch_shapes=list(scratch),
        name=getattr(body, "func", body).__name__,
        compiler_params=pltpu.CompilerParams(vmem_limit_bytes=mib << 20),
        cost_estimate=pl.CostEstimate(
            flops=int(us * 2e9), transcendentals=0, bytes_accessed=int(us * 3e6)
        ),
    )(*operands)


def fence(*values):
    return lax.optimization_barrier(values)


def tiles(window):
    made = []
    for q0 in range(0, window, 256):
        qn = min(256, window - q0)
        k0 = max(0, q0 - MOST)
        made.append((q0, qn, k0, min(window, q0 + qn + MOST)))
    return made


def permutation(target):
    width = target.shape[1]
    return (lax.broadcasted_iota(jnp.int32, (width, width), 0) == target).astype(BF16)


def cuts_of(segments):
    middle = segments.shape[1] // 2
    held = segments[:, middle : middle + 1]
    first = jnp.sum((segments < held).astype(F32), axis=1, keepdims=True)
    last = jnp.sum((segments <= held).astype(F32), axis=1, keepdims=True)
    return jnp.where(middle - first <= last - middle, first, last)


def start_body(info, hidden, cotangent, segment_ids, pad_flags, target, x_o, c_o, xhat_o, bias_o):
    core, y = info[0], info[1]
    window = x_o.shape[0]
    gap = hidden.shape[1] - window
    start = pl.multiple_of(core * gap, 16)
    segments = segment_ids[...]
    cuts = cuts_of(segments)
    cut = jnp.where(y == 0, cuts[0:1], cuts[1:2])
    here = (start + lax.broadcasted_iota(jnp.int32, (window, 1), 0)).astype(F32)
    before = (here < cut).astype(F32)
    owned = jnp.where(core == 0, before, 1.0 - before)
    perm = permutation(target[...])
    x = dot_nn(hidden[y, pl.ds(start, window), :], perm)
    x_o[...] = x.astype(BF16)
    c_o[...] = (dot_nn(cotangent[y, pl.ds(start, window), :], perm) * owned).astype(BF16)
    xhat_o[...] = norm_parts(x)[0]
    segs = jnp.where(y == 0, segments[0:1], segments[1:2]).astype(F32)
    pads = pad_flags[...]
    pads = jnp.where(y == 0, pads[0:1], pads[1:2])
    code = jnp.where(pads == 0, segs, -1.0)
    segs = jnp.where(core == 0, segs[:, :window], segs[:, gap:])
    code = jnp.where(core == 0, code[:, :window], code[:, gap:])
    column = jnp.broadcast_to(code, (8, window)).T[:, 0:1]
    key = lax.broadcasted_iota(jnp.int32, (window, window), 0)
    query = lax.broadcasted_iota(jnp.int32, (window, window), 1)
    bias_o[...] = jnp.where((column == segs) | (key == query), 0.0, -1e30)


def assemble(blocks, places, high, weights):
    for block, rows in zip(blocks, places):
        for z, row in enumerate(rows):
            for w in range(3):
                weights[w, row : row + high] = block[z, w * high : (w + 1) * high]


def disassemble(value, outs, pick):
    value = value.astype(BF16)
    if len(outs) == 1:
        outs[0][pick] = value
        return
    _, deep, high, _ = outs[0].shape[-4:]
    half = high // 3
    yr, w = pick[:-1], pick[-1]
    for x in range(2):
        for z in range(deep):
            for c in range(2):
                at = ((z * 2 + x) * 2 + c) * half
                outs[c][yr + (x, z, pl.ds(w * half, half))] = value[at : at + half]


def common_order(rows, perm):
    high = rows.astype(BF16)
    rest = rows - high.astype(F32)
    mid = rest.astype(BF16)
    last = (rest - mid.astype(F32)).astype(BF16)
    return dot_nn(high, perm) + dot_nn(mid, perm) + dot_nn(last, perm)


def by_head(value, fill=0.0):
    tokens, columns = value.shape
    parts = value.T.reshape(columns // HD, HD, tokens)
    row = lax.broadcasted_iota(jnp.int32, (columns // HD, PAD - HD, tokens), 1)
    extra = jnp.where(row == 0, fill, 0.0)
    return jnp.concatenate([parts, extra], axis=1).astype(BF16)


def flat_heads(value):
    heads, _, tokens = value.shape
    return value[:, :HD, :].reshape(heads * HD, tokens)


def project_body(places, high, unpack, first, given, *refs):
    blocks = refs[: len(places)]
    refs = refs[len(places) :]
    if not unpack:
        small_i, shift_i = refs[:2]
        refs = refs[2:]
    qt, kt, vt, shift_o = refs[:4]
    weights = refs[-1]
    assemble(blocks, places, high, weights)
    if unpack:
        shifts = blocks[0][0, 3 * high : 3 * high + 16].astype(F32)[0:8]
    else:
        shifts = shift_i[...]
    shift_o[...] = shifts
    if first:
        small_o, n_o, nt_o = refs[4:7]
        if unpack:
            deep = blocks[0].shape[0]
            wide = blocks[0].shape[2] // 4
            rows = [
                [blocks[2 * x][z, 3 * high : 3 * high + 16].astype(F32) for x in range(2)]
                for z in range(deep)
            ]
            made = []
            for p in range(6):
                r, at = 8 + p // 4, p % 4 * wide
                made.append(
                    jnp.concatenate(
                        [rows[z][x][r : r + 1, at : at + wide] for z in range(deep) for x in range(2)],
                        axis=1,
                    )
                )
            made += [jnp.zeros_like(made[0])] * 2
            small = jnp.concatenate(made, axis=0)
        else:
            small = small_i[...]
        small_o[...] = small
        exact = given[...] * small[0:1] + small[1:2]
        normed = exact.astype(BF16)
        n_o[...] = normed
        nt_o[...] = exact.T.astype(BF16)
    else:
        normed = given[...]
    qt[...] = by_head(dot_nn(normed, weights[0]) + shifts[0:1])
    kt[...] = by_head(dot_nn(normed, weights[1]))
    vt[...] = by_head(dot_nn(normed, weights[2]) + shifts[1:2], 1.0)


def forward_body(first, qt, kt, vt, bias, ot, lse):
    heads, _, window = ot.shape

    def head(i, carry):
        h = first + i
        for q0, qn, k0, k1 in tiles(window):
            scores = dot_tn(kt[h, :, k0:k1], qt[h, :, q0 : q0 + qn])
            scores = scores * LOG2 + bias[k0:k1, q0 : q0 + qn]
            top = jnp.max(scores, axis=0, keepdims=True)
            weight = jnp.exp2(scores - top).astype(BF16)
            mixed = dot_nn(vt[h, :, k0:k1], weight)
            total = mixed[HD : HD + 1]
            ot[i, :, q0 : q0 + qn] = mixed / total
            lse[i, :, q0 : q0 + qn] = top + jnp.log2(total)
        return carry

    lax.fori_loop(0, heads, head, 0, unroll=2)


def feed_body(places, high, x_r, o00, o01, o10, o11, small, cols0, cols1, target, *refs):
    count = len(places)
    blocks = refs[: 2 * count]
    refs = refs[2 * count :]
    out_o, xhat_o, inv_o, n_o = refs[:4]
    atts, acts, slopes, weights = refs[4:6], refs[6:8], refs[8:10], refs[10:]
    for yr in range(2):
        assemble(blocks[yr * count : (yr + 1) * count], places, high, weights[yr])
    for out, a, b in zip(atts, (o00, o10), (o01, o11)):
        out[...] = jnp.concatenate([flat_heads(a[...]), flat_heads(b[...])], axis=0).T.astype(BF16)
    x = x_r[...].astype(F32)
    middle = x + dot_nt(atts[0][...], weights[0][0]) + dot_nt(atts[1][...], weights[1][0]) + small[2:3]
    xhat, inverse = norm_parts(middle)
    xhat_o[...] = xhat
    inv_o[...] = inverse
    normed = (xhat * small[3:4] + small[4:5]).astype(BF16)
    n_o[...] = normed
    result = middle + small[5:6]
    for yr, cols in enumerate((cols0, cols1)):
        pre = dot_nn(normed, weights[yr][1]) + cols[2:3]
        square = pre * pre
        bent = jnp.tanh(GELU * (pre + 0.044715 * (pre * square)))
        act = (0.5 * pre * (1.0 + bent)).astype(BF16)
        acts[yr][...] = act
        slopes[yr][...] = 0.5 * (1.0 + bent) + 0.5 * pre * (1.0 - bent * bent) * (
            GELU * (1.0 + 3.0 * 0.044715 * square)
        )
        result = result + dot_nt(act, weights[yr][2])
    out_o[...] = dot_nn(result.astype(BF16), permutation(target[...])).astype(BF16)


def rows_of(info, feats, units):
    width = feats.shape[1]
    cols = width // 2
    made = []
    for i in range(feats.shape[0]):
        made += [feats[i : i + 1, :cols], feats[i : i + 1, cols:]]
    for own, other in units:
        made += [jnp.where(info[1] == 0, own, other), jnp.where(info[1] == 0, other, own)]
    return jnp.concatenate(made, axis=0)


def feed_back_body(places, high, parts, info, c_r, xhat_r, inv_r, n_r, a0, a1, act0, act1, slope0, slope1, small, target, *refs):
    count = len(places)
    blocks = refs[: 2 * count]
    refs = refs[2 * count :]
    mid_o, d0, d1, sum_o = refs[:4]
    outs = refs[4 : 4 + parts]
    weights = refs[4 + parts :]
    for yr in range(2):
        assemble(blocks[yr * count : (yr + 1) * count], places, high, weights[yr])
    ct_low, normed = c_r[...], n_r[...]
    dnorm, ups = None, []
    for yr, (act, slope) in enumerate(((act0, slope0), (act1, slope1))):
        disassemble(dot_tn(ct_low, act[...]), outs, (yr, 2))
        dpre = (dot_nn(ct_low, weights[yr][2]) * slope[...]).astype(BF16)
        disassemble(dot_tn(normed, dpre), outs, (yr, 1))
        ups.append(jnp.sum(dpre.astype(F32), axis=0, keepdims=True))
        part = dot_nt(dpre, weights[yr][1])
        dnorm = part if dnorm is None else dnorm + part
    ct, xhat = ct_low.astype(F32), xhat_r[...]
    dmiddle = ct + norm_back(dnorm, xhat, inv_r[...], small[3:4])
    mid_o[...] = dmiddle
    sums = [jnp.sum(part, axis=0, keepdims=True) for part in (dmiddle, dnorm * xhat, dnorm, ct)]
    sums = common_order(
        jnp.concatenate(sums + [jnp.zeros((4, dnorm.shape[1]), F32)], axis=0), permutation(target[...])
    )
    sums = rows_of(info, sums[0:4], [ups])
    sum_o[...] = jnp.concatenate([sums, jnp.zeros_like(sums[0:6])], axis=0)
    low = dmiddle.astype(BF16)
    for yr, att in enumerate((a0, a1)):
        disassemble(dot_tn(low, att[...]), outs, (yr, 0))
        (d0, d1)[yr][...] = by_head(dot_nn(low, weights[yr][0]))


def backward_body(first, qt, kt, vt, dt, ot, lse, bias, dq_o, dk_o, dv_o, dq, dk, dv):
    heads, _, window = ot.shape
    made = tiles(window)

    def head(i, carry):
        h = first + i
        delta = jnp.sum(dt[h].astype(F32) * ot[i], axis=0, keepdims=True)
        for ref in (dk, dv):
            ref[i] = jnp.zeros_like(ref[i])
        for q0, qn, k0, k1 in made:
            query, grad = qt[h, :, q0 : q0 + qn], dt[h, :, q0 : q0 + qn]
            scores = dot_tn(kt[h, :, k0:k1], query)
            dprobs = dot_tn(vt[h, :, k0:k1], grad)
            probs = jnp.exp2(scores * LOG2 + (bias[k0:k1, q0 : q0 + qn] - lse[i, :, q0 : q0 + qn]))
            dscores = (probs * (dprobs - delta[:, q0 : q0 + qn])).astype(BF16)
            dq[i, :, q0 : q0 + qn] = dot_nn(kt[h, :, k0:k1], dscores)
            dk[i, :, k0:k1] += dot_nt(query, dscores)
            dv[i, :, k0:k1] += dot_nt(grad, probs.astype(BF16))
        return carry

    lax.fori_loop(0, heads, head, 0, unroll=1)
    for ref, out, factor in ((dq, dq_o, SCALE), (dk, dk_o, SCALE), (dv, dv_o, 1.0)):
        out[...] = (flat_heads(ref[...]) * factor).astype(BF16)


def weigh_body(places, high, parts, nt_r, qa, ka, va, qb, kb, vb, *refs):
    blocks = refs[: len(places)]
    refs = refs[len(places) :]
    dn, sums = refs[:2]
    outs = refs[2 : 2 + parts]
    weights = refs[2 + parts]
    assemble(blocks, places, high, weights)
    normed = nt_r[...]
    ones = jnp.ones((8, normed.shape[1]), BF16)
    total = None
    for w, (a, b) in enumerate(((qa, qb), (ka, kb), (va, vb))):
        low = jnp.concatenate([a[...], b[...]], axis=0)
        disassemble(dot_nt(normed, low), outs, (w,))
        part = dot_nn(weights[w], low)
        total = part if total is None else total + part
        if w != 1:
            sums[w // 2 : w // 2 + 1] = dot_nt(ones, low)[0:1]
    dn[...] = total


def finish_body(info, dn0, dn1, x_r, mid, small, target, qv0, qv1, out_o, sum_o):
    perm = permutation(target[...])
    grad = (dn0[...] + dn1[...]).T
    xhat, inverse = norm_parts(x_r[...].astype(F32))
    dx = mid[...] + norm_back(grad, xhat, inverse, small[0:1])
    out_o[...] = dot_nn(dx.astype(BF16), perm).astype(BF16)
    sums = [jnp.sum(part, axis=0, keepdims=True) for part in (grad * xhat, grad)]
    sums = common_order(jnp.concatenate(sums + [jnp.zeros((6, grad.shape[1]), F32)], axis=0), perm)
    sum_o[...] = rows_of(info, sums[0:2], [(qv0[w : w + 1], qv1[w : w + 1]) for w in range(2)])


def deal_body(info, wo, wu, wd, mine, theirs):
    half = mine.shape[1]
    values = [wo[...].astype(F32).T.astype(BF16), wu[...], wd[...].astype(F32).T.astype(BF16)]

    @pl.when(info[0] == 0)
    def _():
        for w, value in enumerate(values):
            mine[w], theirs[w] = value[:half], value[half:]

    @pl.when(info[0] != 0)
    def _():
        for w, value in enumerate(values):
            theirs[w], mine[w] = value[:half], value[half:]


def meet_a_body(info, mine, got, small, units, units_pair, first):
    half = got.shape[1]
    wr, wc = small.shape[1], units.shape[1]
    zeros = jnp.zeros((8, 4 * wr), F32)

    def meet(own_first):
        def pair(own, other):
            return jnp.concatenate([own, other] if own_first else [other, own], axis=1)

        for w in range(3):
            first[0, w * half : (w + 1) * half, :] = pair(mine[w], got[w])
        params = small[...].astype(F32)
        if not own_first:
            params = jnp.concatenate([params[:, half:], params[:, :half]], axis=1)
        above = jnp.concatenate([params[p : p + 1] for p in range(4)], axis=1)
        below = jnp.concatenate([params[4:5], params[5:6], zeros[0:1, : 2 * wr]], axis=1)
        both = pair(units[...], units_pair[...]).astype(F32)
        extra = jnp.concatenate([both, zeros[:5], above, below, zeros[:6]], axis=0)
        first[0, 3 * half : 3 * half + 16, :] = extra.astype(BF16)

    @pl.when(info[0] == 0)
    def _():
        meet(True)

    @pl.when(info[0] != 0)
    def _():
        meet(False)


def meet_b_body(info, mine, got, second):
    half = got.shape[1]

    def meet(low, high):
        for w in range(3):
            second[0, w * half : (w + 1) * half, :] = jnp.concatenate([low[w], high[w]], axis=1)

    @pl.when(info[0] == 0)
    def _():
        meet(mine, got)

    @pl.when(info[0] != 0)
    def _():
        meet(got, mine)


def stack_body(*refs):
    out = refs[-1]
    for at, ref in enumerate(refs[:-1]):
        out[at] = ref[0]


def pack(out, row, sums):
    count = sums.shape[0]
    high = sums.astype(BF16)
    out[row : row + count] = high
    out[row + count : row + 2 * count] = (sums - high.astype(F32)).astype(BF16)


def unpack_sums(ref, row, count):
    both = ref[row : row + 2 * count].astype(F32)
    return both[:count] + both[count:]


def block_sums(keep, got, out, row):
    deep, high, _ = keep.shape
    for z in range(deep):
        total = keep[z].astype(F32) + got[z].astype(F32)
        out[row + z * high : row + (z + 1) * high] = total.astype(BF16)


def far_b_body(keep, got, sums, sums_got, out, sum_o):
    total = sums[...] + sums_got[...]
    sum_o[...] = total
    for x in range(2):
        block_sums(keep.at[1, x], got.at[1, x], out, x * (out.shape[0] - 32) // 2)
    pack(out, out.shape[0] - 32, total)


def far_a_body(keep, got, out0, out1):
    block_sums(keep.at[0], got.at[0], out0, 0)
    block_sums(keep.at[1], got.at[1], out1, 0)


def pass_on(keep, got, far, out):
    deep, high, _ = keep.shape
    for z in range(deep):
        rows = slice(z * high, (z + 1) * high)
        total = keep[z].astype(F32) + got[z].astype(F32) + far[rows].astype(F32)
        out[rows] = total.astype(BF16)


def near_b_body(keep, got, far, sums, out, sum_o):
    count = out.shape[0] - 32
    pass_on(keep.at[0, 1], got.at[0, 1], far.at[count : 2 * count], out)
    total = sums[...] + unpack_sums(far, 2 * count, 16)
    sum_o[...] = total
    pack(out, count, total)


def near_a_body(keep, got, far, sums, sums_got, out, sum_o):
    pass_on(keep.at[1], got.at[1], far, out)
    total = sums[...] + sums_got[...]
    sum_o[...] = total
    pack(out, out.shape[0] - 16, total)


def block_total(keep, got, far, passed, z):
    rows = slice(z * keep.shape[1], (z + 1) * keep.shape[1])
    return keep[z].astype(F32) + got[z].astype(F32) + far[rows].astype(F32) + passed[rows].astype(F32)


def high_b_body(keep, got, far, passed, sums, own, out, sum_o):
    kept, given = keep.at[0, 0], got.at[0, 0]
    deep, high, _ = kept.shape
    total = sums[...] + unpack_sums(passed, deep * high, sums.shape[0])
    sum_o[...] = total
    for z in range(deep):
        value = block_total(kept, given, far, passed, z)
        if z < deep // 2:
            own[z] = value
        else:
            out[(z - deep // 2) * high : (z - deep // 2 + 1) * high] = value.astype(BF16)
    pack(out, deep // 2 * high, total)


def middle_b_body(own, got, sums, own_o, out, sum_o):
    _, high, _ = own.shape
    total = sums[...] + unpack_sums(got, 2 * high, sums.shape[0])
    sum_o[...] = total
    own_o[...] = own[0] + got[0:high].astype(F32)
    out[0:high] = (own[1] + got[high : 2 * high].astype(F32)).astype(BF16)
    pack(out, high, total)


def high_a_body(keep, got, far, passed, sums, *outs):
    kept, given = keep.at[0], got.at[0]
    deep, high, _ = kept.shape
    total = sums[...] + unpack_sums(passed, deep * high, sums.shape[0])
    outs[-1][...] = total
    for z in range(deep):
        value = block_total(kept, given, far, passed, z)
        if z == 0:
            outs[0][...] = value
        else:
            outs[z][0:high] = value.astype(BF16)
            pack(outs[z], high, total)


def last_body(info, own, sums, *refs):
    parts, (mine, theirs, sum_o) = refs[:-3], refs[-3:]
    high = own.shape[0]
    half = high // 3
    total, wide = own[...], sums[...]
    for part in parts:
        total = total + part[0:high].astype(F32)
        wide = wide + unpack_sums(part, high, sums.shape[0])
    sum_o[...] = wide
    wc = mine.shape[2]

    def give(low, upper):
        for w in range(3):
            low[w] = total[w * half : (w + 1) * half, :wc]
            upper[w] = total[w * half : (w + 1) * half, wc:]

    @pl.when(info[0] == 0)
    def _():
        give(mine, theirs)

    @pl.when(info[0] != 0)
    def _():
        give(theirs, mine)


def deliver_body(turned, info, mine, got, *outs):
    half = mine.shape[1]

    def deliver(low, high):
        for w, out in enumerate(outs):
            if turned[w]:
                out[...] = jnp.concatenate([low[w], high[w]], axis=0).T
            else:
                out[0:half] = low[w]
                out[half:] = high[w]

    @pl.when(info[0] == 0)
    def _():
        deliver(mine, got)

    @pl.when(info[0] != 0)
    def _():
        deliver(got, mine)


def join_body(info, segment_ids, own, beside, across, corner, out):
    core, y = info[0], info[1]
    length, window = out.shape[1], own.shape[0]
    gap = length - window
    cuts = cuts_of(segment_ids[...])
    own_cut = jnp.where(y == 0, cuts[0:1], cuts[1:2])
    other_cut = jnp.where(y == 0, cuts[1:2], cuts[0:1])

    def row(low, high, place, cut):
        out[place, 0:gap] = low[0:gap]
        at = (gap + lax.broadcasted_iota(jnp.int32, (window - gap, 1), 0)).astype(F32)
        seam = jnp.where(at < cut, low[gap:window].astype(F32), high[0 : window - gap].astype(F32))
        out[place, gap:window] = seam.astype(BF16)
        out[place, window:length] = high[window - gap : window]

    @pl.when(core == 0)
    def _():
        row(own, beside, y, own_cut)
        row(across, corner, 1 - y, other_cut)

    @pl.when(core != 0)
    def _():
        row(beside, own, y, own_cut)
        row(corner, across, 1 - y, other_cut)


def per_device(
    hidden_in,
    segment_ids,
    pad_flags,
    gain1,
    shift1,
    w_query,
    b_query,
    w_key,
    w_value,
    b_value,
    w_out,
    b_out,
    gain2,
    shift2,
    w_up,
    b_up,
    w_down,
    b_down,
    cotangent,
):
    fs, mp = lax.axis_size("fsdp"), lax.axis_size("mp")
    rows, length, width = hidden_in.shape
    wr, wc = w_query.shape
    half, cols = wr // 2, 2 * wc
    heads = cols // HD
    f, m = lax.axis_index("fsdp"), lax.axis_index("mp")
    core, y = m % 2, m // 2
    side = jnp.stack([core, y])
    window = length // 2 + MOST // 2
    deep = fs // 2
    flips = [2 * z for z in range(1, deep)]
    staged = half % 16 == 0 and deep == 4
    if staged:
        places = [[((z * 2 + x) * 2 + c) * half for z in range(deep)] for x in range(2) for c in range(2)]
        high, parts = half, 2
    else:
        places, high, parts = [[0]], width, 1
    wide, tall = (window, width), (width, window)
    by_heads, by_few = (heads, PAD, window), (heads // 2, PAD, window)
    weights = pltpu.VMEM((3, width, cols), BF16)

    def to(value, flip_f, flip_m):
        return send(value, fs, mp, flip_f, flip_m)

    def begin(target):
        return call(
            start_body,
            [(wide, BF16), (wide, BF16), (wide, F32), ((window, window), F32)],
            [side, hidden_in, cotangent, segment_ids, pad_flags, target],
            (),
            1,
            us=3,
            mib=4,
        )

    def project(given, blocks, first, extra=()):
        outs = [(by_heads, BF16)] * 3 + [((8, cols), F32)]
        if first:
            outs += [((8, width), F32), (wide, BF16), (tall, BF16)]
        return call(
            functools.partial(project_body, places, high, not extra, first),
            outs,
            [given] + blocks + list(extra),
            [weights],
            us=2,
            mib=4,
        )

    def attend(part, qkv_heads, bias):
        return call(
            functools.partial(forward_body, part * (heads // 2)),
            [(by_few, F32), ((heads // 2, 1, window), F32)],
            list(qkv_heads) + [bias],
            us=5,
        )

    def feed(x, mixed, small, shifts, target, blocks):
        units_shape = (window, cols)
        return call(
            functools.partial(feed_body, places, high),
            [(wide, BF16), (wide, F32), ((window, 1), F32), (wide, BF16)]
            + [(units_shape, BF16)] * 4
            + [(units_shape, F32)] * 2,
            [x] + mixed + [small] + shifts + [target] + blocks,
            [weights, weights],
            us=5,
            mib=7,
        )

    def feed_back(side, ct, made, small, target, blocks):
        if staged:
            grads = [((2, 2, deep, 3 * half, cols), BF16)] * 2
        else:
            grads = [((2, 3, width, cols), BF16)]
        return call(
            functools.partial(feed_back_body, places, high, parts),
            [(wide, F32), (by_heads, BF16), (by_heads, BF16), ((16, cols), F32)] + grads,
            [side, ct] + list(made) + [small, target] + blocks,
            [weights, weights],
            1,
            us=7,
            mib=7,
        )

    def backward(part, qkv_heads, da, o, lse, bias):
        return call(
            functools.partial(backward_body, part * (heads // 2)),
            [((heads // 2 * HD, window), BF16)] * 3,
            list(qkv_heads) + [da, o, lse, bias],
            [pltpu.VMEM(by_few, F32)] * 3,
            us=15,
        )

    def weigh(normed_t, blocks, low_a, low_b):
        if staged:
            grads = [((2, deep, 3 * half, cols), BF16)] * 2
        else:
            grads = [((3, width, cols), BF16)]
        return call(
            functools.partial(weigh_body, places, high, parts),
            [(tall, F32), ((2, cols), F32)] + grads,
            [normed_t] + list(low_a) + list(low_b) + blocks,
            [weights],
            us=0.1,
        )

    def finish(side, dn0, dn1, x, dmiddle, small, target, qv0, qv1):
        return call(
            finish_body,
            [(wide, BF16), ((8, cols), F32)],
            [side, dn0, dn1, x, dmiddle, small, target, qv0, qv1],
            (),
            1,
            us=20,
            mib=5,
        )

    def join(own, beside, across, corner):
        operands = [side, segment_ids, own, beside, across, corner]
        return call(join_body, [((rows, length, width), BF16)], operands, (), 1, us=20)[0]

    if not staged:

        def gathered(blocks):
            full = []
            for block in blocks:
                block = lax.all_gather(block, "fsdp", axis=0, tiled=True)
                full.append(lax.all_gather(block, "mp", axis=1, tiled=True))
            full = jnp.stack(full)
            return [full[:, :, yr * cols : (yr + 1) * cols].reshape(1, 3 * width, cols) for yr in range(2)]

        target = lax.iota(jnp.int32, width)[None]
        wa = gathered([w_query, w_key, w_value])
        wb = gathered([w_out.T, w_up, w_down.T])
        small = jnp.stack([gain1, shift1, b_out, gain2, shift2, b_down] + [jnp.zeros_like(gain1)] * 2)
        small = lax.all_gather(small, "fsdp", axis=1, tiled=True).astype(F32)
        units = jnp.stack([b_query, b_value, b_up] + [jnp.zeros_like(b_up)] * 5)
        units = lax.all_gather(units, "mp", axis=1, tiled=True).astype(F32)
        units = [units[:, :cols], units[:, cols:]]
        x, ct, xhat, bias = begin(target)
        *heads0, _, _, normed, normed_t = project(xhat, [wa[0]], True, (small, units[0]))
        *heads1, _ = project(normed, [wa[1]], False, (small, units[1]))
        both = (heads0, heads1)
        mixed = [attend(part, both[yr], bias) for yr in range(2) for part in range(2)]
        made = feed(x, [o for o, _ in mixed], small, units, target, wb)
        result = made[0]
        none = jnp.zeros_like(side)
        dmiddle, da0, da1, sums_b, grads_b = feed_back(none, ct, made[1:], small, target, wb)
        dn, qv, grads_a = [], [], []
        for yr, da in enumerate((da0, da1)):
            lows = [backward(part, both[yr], da, *mixed[2 * yr + part], bias) for part in range(2)]
            got = weigh(normed_t, [wa[yr]], *lows)
            dn.append(got[0])
            qv.append(got[1])
            grads_a.append(got[2])
        grad_window, sums_a = finish(none, dn[0], dn[1], x, dmiddle, small, target, *qv)

        def scattered(pair):
            full = jnp.concatenate(pair, axis=2).astype(F32)
            full = lax.psum_scatter(full, "mp", scatter_dimension=2, tiled=True)
            return lax.psum_scatter(full, "fsdp", scatter_dimension=1, tiled=True)

        grad_q, grad_k, grad_v = scattered(grads_a)
        grad_out, grad_up, grad_down = scattered([grads_b[0], grads_b[1]])
        grad_out, grad_down = grad_out.T, grad_down.T
        sums_a, sums_b = sums_a.reshape(4, width), sums_b.reshape(8, width)
        sums = jnp.concatenate([sums_a[0:2], sums_b[0:4], sums_a[2:4], sums_b[4:5]])
        sums = lax.psum(sums, BOTH)
        mine_f = lax.dynamic_slice(sums, (0, f * wr), (6, wr))
        mine_u = lax.dynamic_slice(sums, (6, m * wc), (3, wc))

        def shared(value):
            across = to(value, 0, 2)
            return join(value, to(value, 0, 1), across, to(across, 0, 1))

        out_hidden, grad_hidden = shared(result), shared(grad_window)
    else:
        piece_a, piece_b = (1, 3 * half + 16, cols), (1, 3 * half, cols)

        def stacked(pieces):
            return call(stack_body, [((deep,) + pieces[0].shape[1:], BF16)], pieces)[0]

        def part(block, of):
            return lax.dynamic_slice(block, (of * half, 0), (half, wc))

        theirs = jnp.stack([part(w, 1 - core) for w in (w_query, w_key, w_value)])
        got = to(theirs, 0, 1)
        theirs, gain1, b_query, w_query, w_key, w_value = fence(theirs, gain1, b_query, w_query, w_key, w_value)
        mine = jnp.stack([part(w, core) for w in (w_query, w_key, w_value)])
        small = jnp.stack([gain1, shift1, b_out, gain2, shift2, b_down])
        units = jnp.stack([b_query, b_value, b_up])
        units_pair = to(units, 0, 1)
        feature = lax.iota(jnp.int32, width)
        target = (((feature // half) ^ (f * 2 + core)) * half + feature % half)[None]
        got, units_pair, small, mine = fence(got, units_pair, small, mine)

        first = call(
            meet_a_body, [(piece_a, BF16)], [side, mine, got, small, units, units_pair], (), 1
        )[0]
        first_parts = [to(first, flip, 0) for flip in flips]
        first, w_out, w_up, w_down = fence(first, w_out, w_up, w_down)
        mine, theirs = call(deal_body, [((3, half, wc), BF16)] * 2, [side, w_out, w_up, w_down], (), 1)
        got = to(theirs, 0, 1)
        second = call(meet_b_body, [(piece_b, BF16)], [side, mine, got], (), 1)[0]
        first, first_parts, second, hidden_in, target = fence(first, first_parts, second, hidden_in, target)

        qkv = stacked([first] + first_parts)
        qkv_x, qkv_y = to(qkv, 1, 0), to(qkv, 0, 2)
        second_parts = [to(second, flip, 0) for flip in flips]
        x, ct, xhat, bias = begin(target)
        second_parts, second, qkv, qkv_x, qkv_y, xhat = fence(second_parts, second, qkv, qkv_x, qkv_y, xhat)
        qkv_xy = to(qkv, 1, 2)

        qkv_c, qkv_xc = to(qkv, 0, 1), to(qkv_x, 0, 1)
        odu = stacked([second] + second_parts)
        near = [qkv, qkv_c, qkv_x, qkv_xc]
        *heads0, shift0, small, normed, normed_t = project(xhat, near, True)
        heads0, qkv_y, odu = fence(heads0, qkv_y, odu)
        qkv_yc, odu_x, odu_y = to(qkv_y, 0, 1), to(odu, 1, 0), to(odu, 0, 2)
        o00, l00 = attend(0, heads0, bias)
        o00, heads0, qkv_yc, qkv_xy, odu = fence(o00, heads0, qkv_yc, qkv_xy, odu)
        qkv_xyc, odu_xy, odu_c = to(qkv_xy, 0, 1), to(odu, 1, 2), to(odu, 0, 1)
        o01, l01 = attend(1, heads0, bias)
        o01, qkv_xyc, odu_c, normed = fence(o01, qkv_xyc, odu_c, normed)
        far = [qkv_y, qkv_yc, qkv_xy, qkv_xyc]
        *heads1, shift1u = project(normed, far, False)
        o10, l10 = attend(0, heads1, bias)
        o10, heads1, odu_x, odu_y = fence(o10, heads1, odu_x, odu_y)
        odu_xc, odu_yc = to(odu_x, 0, 1), to(odu_y, 0, 1)
        o11, l11 = attend(1, heads1, bias)
        o11, odu_xc, odu_yc, odu_xy = fence(o11, odu_xc, odu_yc, odu_xy)
        odu_xyc = to(odu_xy, 0, 1)

        odu_blocks = [odu, odu_c, odu_x, odu_xc, odu_y, odu_yc, odu_xy, odu_xyc]
        made = fence(*feed(x, [o00, o01, o10, o11], small, [shift0, shift1u], target, odu_blocks))
        result = made[0]
        res_c, res_y = to(result, 0, 1), to(result, 0, 2)
        made = feed_back(side, ct, made[1:], small, target, odu_blocks)
        dmiddle, da0, da1, b_sums, b_keep, b_send, res_c = fence(*made, res_c)

        n_far, n_near = 2 * deep * 3 * half, deep * 3 * half
        f32_16, f32_8 = ((16, cols), F32), ((8, cols), F32)
        b_got, b_sums_got = to(b_send, 0, 1), to(b_sums, 0, 1)
        low10 = backward(0, heads1, da1, o10, l10, bias)
        low10, heads1, b_got, b_sums_got = fence(low10, heads1, b_got, b_sums_got)
        b_far, b_sums = call(
            far_b_body,
            [((n_far + 32, cols), BF16), f32_16],
            [b_keep, b_got, b_sums, b_sums_got],
        )
        b_far = to(b_far, 0, 2)
        low11 = backward(1, heads1, da1, o11, l11, bias)
        low11, normed_t = fence(low11, normed_t)
        dn1, qv1, keep1, send1 = weigh(normed_t, far, low10, low11)
        dn1, keep1, send1, da0, res_y = fence(dn1, keep1, send1, da0, res_y)
        got1, res_yc = to(send1, 0, 1), to(res_y, 0, 1)
        low00 = backward(0, heads0, da0, o00, l00, bias)
        low00, heads0, got1, res_yc = fence(low00, heads0, got1, res_yc)
        a_far0, a_far1 = call(far_a_body, [((n_near, cols), BF16)] * 2, [keep1, got1])
        a_far0, a_far1, heads0 = fence(a_far0, a_far1, heads0)
        a_far1, a_far0 = to(a_far1, 0, 2), to(a_far0, 0, 2)
        low01 = backward(1, heads0, da0, o01, l01, bias)
        low01, normed_t, b_far = fence(low01, normed_t, b_far)
        b_x, b_sums = call(
            near_b_body, [((n_near + 32, cols), BF16), f32_16], [b_keep, b_got, b_far, b_sums]
        )
        b_x = to(b_x, 1, 0)
        dn0, qv0, keep0, send0 = weigh(normed_t, near, low00, low01)
        dn0, keep0, send0, dmiddle = fence(dn0, keep0, send0, dmiddle)
        got0 = to(send0, 0, 1)
        n_two = 2 * 3 * half
        grad_window, a_sums = finish(side, dn0, dn1, x, dmiddle, small, target, qv0, qv1)
        grad_window, a_sums, got0, a_far1, b_x = fence(grad_window, a_sums, got0, a_far1, b_x)

        gw_y, gw_c, a_sums_got = to(grad_window, 0, 2), to(grad_window, 0, 1), to(a_sums, 0, 1)
        a_sums_got, gw_c, keep0 = fence(a_sums_got, gw_c, keep0)
        a_x, a_sums = call(
            near_a_body, [((n_near + 16, cols), BF16), f32_8], [keep0, got0, a_far1, a_sums, a_sums_got]
        )
        a_x, b_keep = fence(a_x, b_keep)
        a_x = to(a_x, 1, 0)
        b_own, b_z2, b_sums = call(
            high_b_body,
            [((2, 3 * half, cols), F32), ((n_two + 32, cols), BF16), f32_16],
            [b_keep, b_got, b_far, b_x, b_sums],
        )
        b_z2, result = fence(b_z2, result)
        b_z2 = to(b_z2, 4, 0)
        out_hidden = join(result, res_c, res_y, res_yc)
        b_z2, out_hidden = fence(b_z2, out_hidden)

        def last(own, sums, got, kind):
            return call(last_body, [((3, half, wc), F32)] * 2 + [kind], [side, own, sums] + got, (), 1, us=20)

        def deliver(mine, got, turned):
            shapes = [((wc, wr) if t else (wr, wc), F32) for t in turned]
            return call(functools.partial(deliver_body, turned), shapes, [side, mine, got], (), 1)

        b_own, b_z1, b_sums = call(
            middle_b_body,
            [((3 * half, cols), F32), ((3 * half + 32, cols), BF16), f32_16],
            [b_own, b_z2, b_sums],
            us=20,
        )
        b_z1, a_x, a_far0, keep0 = fence(b_z1, a_x, a_far0, keep0)
        a_split = call(
            high_a_body,
            [((3 * half, cols), F32)] + [((3 * half + 16, cols), BF16)] * (deep - 1) + [f32_8],
            [keep0, got0, a_far0, a_x, a_sums],
        )
        a_split, b_z1, b_own = fence(a_split, b_z1, b_own)
        a_high = [to(part, flip, 0) for part, flip in zip(a_split[1:-1], flips)]
        b_z1 = to(b_z1, 2, 0)
        b_z1, gw_y = fence(b_z1, gw_y)
        b_mine, b_theirs, b_sums = last(b_own, b_sums, [b_z1], f32_16)
        b_last, gw_yc = to(b_theirs, 0, 1), to(gw_y, 0, 1)
        grad_hidden = join(grad_window, gw_c, gw_y, gw_yc)
        b_last, grad_hidden = fence(b_last, grad_hidden)
        grad_out, grad_up, grad_down = deliver(b_mine, b_last, (True, False, True))
        a_own, a_high, grad_out, grad_hidden = fence(a_split[0], a_high, grad_out, grad_hidden)
        a_mine, a_theirs, a_sums = last(a_own, a_split[-1], a_high, f32_8)
        a_last = to(a_theirs, 0, 1)
        a_sums = a_sums + to(a_sums, 0, 2)
        grad_q, grad_k, grad_v = deliver(a_mine, a_last, (False, False, False))
        sums = jnp.concatenate(
            [
                a_sums.reshape(4, width)[0:2],
                b_sums.reshape(8, width)[0:4],
                a_sums.reshape(4, width)[2:4],
                b_sums.reshape(8, width)[4:5],
            ]
        )
        mine_f = lax.dynamic_slice(sums, (0, f * wr), (6, wr))
        mine_u = lax.dynamic_slice(sums, (6, m * wc), (3, wc))
    return (
        out_hidden,
        grad_hidden,
        mine_f[0],
        mine_f[1],
        grad_q,
        mine_u[0],
        grad_k,
        grad_v,
        mine_u[1],
        grad_out,
        mine_f[2],
        mine_f[3],
        mine_f[4],
        grad_up,
        mine_u[2],
        grad_down,
        mine_f[5],
    )


def solution(mesh):
    return jax.shard_map(
        per_device,
        mesh=mesh,
        in_specs=(
            P("fsdp", None, None),
            P("fsdp", None),
            P("fsdp", None),
            P("fsdp"),
            P("fsdp"),
            P("fsdp", "mp"),
            P("mp"),
            P("fsdp", "mp"),
            P("fsdp", "mp"),
            P("mp"),
            P("mp", "fsdp"),
            P("fsdp"),
            P("fsdp"),
            P("fsdp"),
            P("fsdp", "mp"),
            P("mp"),
            P("mp", "fsdp"),
            P("fsdp"),
            P("fsdp", None, None),
        ),
        out_specs=(
            P("fsdp", None, None),
            P("fsdp", None, None),
            P("fsdp"),
            P("fsdp"),
            P("fsdp", "mp"),
            P("mp"),
            P("fsdp", "mp"),
            P("fsdp", "mp"),
            P("mp"),
            P("mp", "fsdp"),
            P("fsdp"),
            P("fsdp"),
            P("fsdp"),
            P("fsdp", "mp"),
            P("mp"),
            P("mp", "fsdp"),
            P("fsdp"),
        ),
        check_vma=False,
    )
```

profile of v0, /device:TPU:0, one launch (start us, length us, event | category | flops | bytes accessed | tf_op | source)
XLA Modules:
  0.0 178.2 jit_solution(2666515487763739032)
XLA Ops:
  8.0 3.1 %collective-permute-start.2 = (bf16[1,160,384]{2,1,0:T(8,128)(2,1)S(1)}, bf16[1,160,384]{2,1,0:T(8,128)(2,1)S(1)}, u32[]{:S(2)}, u32[]{:S(2)}) collective-permute-start(bf16[1,160,384]{2,1,0:T(8,128)(2,1)S(1)} %meet_a_body.1.refs_0_), channel_id=1, source_target_pairs={{0,8},{1,9},{2,10},{3,11},{4,12},{5,13},{6,14},{7,15},{8,0},{9,1},... | collective-permute-start | bytes 368648 | tf_op jit(solution)/shard_map/ppermute | solution.py:25
  11.1 2.6 %collective-permute-start.3 = (bf16[1,160,384]{2,1,0:T(8,128)(2,1)S(1)}, bf16[1,160,384]{2,1,0:T(8,128)(2,1)S(1)}, u32[]{:S(2)}, u32[]{:S(2)}) collective-permute-start(bf16[1,160,384]{2,1,0:T(8,128)(2,1)S(1)} %meet_a_body.1.refs_0_), channel_id=1, source_target_pairs={{0,16},{1,17},{2,18},{3,19},{4,20},{5,21},{6,22},{7,23},{8,24},{9,... | collective-permute-start | bytes 368648 | tf_op jit(solution)/shard_map/ppermute | solution.py:25
  18.8 4.8 %collective-permute-done.3.refs_2_ = bf16[1,160,384]{2,1,0:T(8,128)(2,1)S(1)} collective-permute-done((bf16[1,160,384]{2,1,0:T(8,128)(2,1)S(1)}, bf16[1,160,384]{2,1,0:T(8,128)(2,1)S(1)}, u32[]{:S(2)}, u32[]{:S(2)}) %collective-permute-start.3) | collective-permute-done | bytes 122912 | tf_op jit(solution)/shard_map/ppermute | solution.py:25
  35.1 3.6 %collective-permute-done.7.refs_2_ = bf16[1,144,384]{2,1,0:T(8,128)(2,1)S(1)} collective-permute-done((bf16[1,144,384]{2,1,0:T(8,128)(2,1)S(1)}, bf16[1,144,384]{2,1,0:T(8,128)(2,1)S(1)}, u32[]{:S(2)}, u32[]{:S(2)}) %collective-permute-start.7) | collective-permute-done | bytes 110624 | tf_op jit(solution)/shard_map/ppermute | solution.py:25
  44.6 5.5 %forward_body.4 = (f32[8,32,480]{2,1,0:T(8,128)S(1)}, f32[8,1,480]{2,1,0:T(1,128)S(1)}) custom-call(bf16[16,32,480]{2,1,0:T(8,128)(2,1)S(1)} %get-tuple-element.376.qt, bf16[16,32,480]{2,1,0:T(8,128)(2,1)S(1)} %get-tuple-element.377.kt, bf16[16,32,480]{2,1,0:T(8,128)(2,1)S(1)} %get-tuple-element.378.vt, f32[480,480]{1,0:T(8,128)S(1)} %get-tuple-element.283.bias), custom_call_target="tpu_custom_call" | custom-call | flops 10000000000 | bytes 15000000 | tf_op jit(solution)/shard_map/forward_body/pallas_call | solution.py:59
  50.1 4.2 %collective-permute-done.14.refs_2_ = bf16[4,160,384]{2,1,0:T(8,128)(2,1)S(1)} collective-permute-done((bf16[4,160,384]{2,1,0:T(8,128)(2,1)S(1)}, bf16[4,160,384]{2,1,0:T(8,128)(2,1)S(1)}, u32[]{:S(2)}, u32[]{:S(2)}) %collective-permute-start.14) | collective-permute-done | bytes 491552 | tf_op jit(solution)/shard_map/ppermute | solution.py:25
  55.0 5.5 %forward_body.5 = (f32[8,32,480]{2,1,0:T(8,128)S(1)}, f32[8,1,480]{2,1,0:T(1,128)S(1)}) custom-call(bf16[16,32,480]{2,1,0:T(8,128)(2,1)S(1)} %get-tuple-element.376.qt, bf16[16,32,480]{2,1,0:T(8,128)(2,1)S(1)} %get-tuple-element.377.kt, bf16[16,32,480]{2,1,0:T(8,128)(2,1)S(1)} %get-tuple-element.378.vt, f32[480,480]{1,0:T(8,128)S(1)} %get-tuple-element.283.bias), custom_call_target="tpu_custom_call" | custom-call | flops 10000000000 | bytes 15000000 | tf_op jit(solution)/shard_map/forward_body/pallas_call | solution.py:59
  62.0 5.5 %forward_body.6 = (f32[8,32,480]{2,1,0:T(8,128)S(1)}, f32[8,1,480]{2,1,0:T(1,128)S(1)}) custom-call(bf16[16,32,480]{2,1,0:T(8,128)(2,1)S(1)} %get-tuple-element.343.qt, bf16[16,32,480]{2,1,0:T(8,128)(2,1)S(1)} %get-tuple-element.344.kt, bf16[16,32,480]{2,1,0:T(8,128)(2,1)S(1)} %get-tuple-element.345.vt, f32[480,480]{1,0:T(8,128)S(1)} %get-tuple-element.283.bias), custom_call_target="tpu_custom_call" | custom-call | flops 10000000000 | bytes 15000000 | tf_op jit(solution)/shard_map/forward_body/pallas_call | solution.py:59
  68.1 5.7 %forward_body.7 = (f32[8,32,480]{2,1,0:T(8,128)S(1)}, f32[8,1,480]{2,1,0:T(1,128)S(1)}) custom-call(bf16[16,32,480]{2,1,0:T(8,128)(2,1)S(1)} %get-tuple-element.343.qt, bf16[16,32,480]{2,1,0:T(8,128)(2,1)S(1)} %get-tuple-element.344.kt, bf16[16,32,480]{2,1,0:T(8,128)(2,1)S(1)} %get-tuple-element.345.vt, f32[480,480]{1,0:T(8,128)S(1)} %get-tuple-element.283.bias), custom_call_target="tpu_custom_call" | custom-call | flops 10000000000 | bytes 15000000 | tf_op jit(solution)/shard_map/forward_body/pallas_call | solution.py:59
  75.7 4.9 %feed_body.1 = (bf16[480,768]{1,0:T(8,128)(2,1)S(1)}, f32[480,768]{1,0:T(8,128)S(1)}, f32[480,1]{1,0:T(8,128)S(1)}, bf16[480,768]{1,0:T(8,128)(2,1)S(1)}, bf16[4...) custom-call(bf16[480,768]{1,0:T(8,128)(2,1)S(1)} %get-tuple-element., ...), custom_call_target="tpu_custom_call" | custom-call | flops 10000000000 | bytes 15000000 | tf_op jit(solution)/shard_map/feed_body/pallas_call | solution.py:59
  82.5 7.9 %feed_back_body.1 = (f32[480,768]{1,0:T(8,128)S(1)}, bf16[16,32,480]{2,1,0:T(8,128)(2,1)S(1)}, bf16[16,32,480]{2,1,0:T(8,128)(2,1)S(1)}, f32[16,384]{1,0:T(8,128...) custom-call(s32[2]{0:T(128)S(1)} %pad_add_fusion.info, ...), custom_call_target="tpu_custom_call" | custom-call | flops 14000000000 | bytes 21000000 | tf_op jit(solution)/shard_map/feed_back_body/pallas_call | solution.py:59
  91.8 6.5 %backward_body.4 = (bf16[192,480]{1,0:T(8,128)(2,1)S(1)}, bf16[192,480]{1,0:T(8,128)(2,1)S(1)}, bf16[192,480]{1,0:T(8,128)(2,1)S(1)}) custom-call(bf16[16,32,480]{2,1,0:T(8,128)(2,1)S(1)} %get-tuple-element.343.qt, bf16[16,32,480]{2,1,0:T(8,128)(2,1)S(1)} %get-tuple-element.344.kt, bf16[16,32,480]{2,1,0:T(8,128)(2,1)S(1)} %get-tuple-element.345.vt, ...), custom_call_target="tpu_custom_call" | custom-call | flops 30000001024 | bytes 45000000 | tf_op jit(solution)/shard_map/backward_body/pallas_call | solution.py:59
  99.1 6.5 %backward_body.5 = (bf16[192,480]{1,0:T(8,128)(2,1)S(1)}, bf16[192,480]{1,0:T(8,128)(2,1)S(1)}, bf16[192,480]{1,0:T(8,128)(2,1)S(1)}) custom-call(bf16[16,32,480]{2,1,0:T(8,128)(2,1)S(1)} %get-tuple-element.343.qt, bf16[16,32,480]{2,1,0:T(8,128)(2,1)S(1)} %get-tuple-element.344.kt, bf16[16,32,480]{2,1,0:T(8,128)(2,1)S(1)} %get-tuple-element.345.vt, ...), custom_call_target="tpu_custom_call" | custom-call | flops 30000001024 | bytes 45000000 | tf_op jit(solution)/shard_map/backward_body/pallas_call | solution.py:59
  105.7 2.8 %weigh_body.2 = (f32[768,480]{1,0:T(8,128)S(1)}, f32[2,384]{1,0:T(2,128)S(1)}, bf16[2,4,144,384]{3,2,1,0:T(8,128)(2,1)S(1)}, bf16[2,4,144,384]{3,2,1,0:T(8,128)(2,1)S(1)}) custom-call(bf16[768,480]{1,0:T(8,128)(2,1)S(1)} %get-tuple-element.387.nt_r, bf16[192,480]{1,0:T(8,128)(2,1)S(1)} %get-tuple-element.352.qa, bf16[192,480]{1,0:T(8,128)(2,1)S(1)} %get-tuple-element.353.ka, ...), custom_call_target="tpu_custom_call" | custom-call | flops 200000000 | bytes 300000 | tf_op jit(solution)/shard_map/weigh_body/pallas_call | solution.py:59
  109.1 6.5 %backward_body.6 = (bf16[192,480]{1,0:T(8,128)(2,1)S(1)}, bf16[192,480]{1,0:T(8,128)(2,1)S(1)}, bf16[192,480]{1,0:T(8,128)(2,1)S(1)}) custom-call(bf16[16,32,480]{2,1,0:T(8,128)(2,1)S(1)} %get-tuple-element.376.qt, bf16[16,32,480]{2,1,0:T(8,128)(2,1)S(1)} %get-tuple-element.377.kt, bf16[16,32,480]{2,1,0:T(8,128)(2,1)S(1)} %get-tuple-element.378.vt, ...), custom_call_target="tpu_custom_call" | custom-call | flops 30000001024 | bytes 45000000 | tf_op jit(solution)/shard_map/backward_body/pallas_call | solution.py:59
  117.4 6.5 %backward_body.7 = (bf16[192,480]{1,0:T(8,128)(2,1)S(1)}, bf16[192,480]{1,0:T(8,128)(2,1)S(1)}, bf16[192,480]{1,0:T(8,128)(2,1)S(1)}) custom-call(bf16[16,32,480]{2,1,0:T(8,128)(2,1)S(1)} %get-tuple-element.376.qt, bf16[16,32,480]{2,1,0:T(8,128)(2,1)S(1)} %get-tuple-element.377.kt, bf16[16,32,480]{2,1,0:T(8,128)(2,1)S(1)} %get-tuple-element.378.vt, ...), custom_call_target="tpu_custom_call" | custom-call | flops 30000001024 | bytes 45000000 | tf_op jit(solution)/shard_map/backward_body/pallas_call | solution.py:59
  125.7 2.8 %weigh_body.3 = (f32[768,480]{1,0:T(8,128)S(1)}, f32[2,384]{1,0:T(2,128)S(1)}, bf16[2,4,144,384]{3,2,1,0:T(8,128)(2,1)S(1)}, bf16[2,4,144,384]{3,2,1,0:T(8,128)(2,1)S(1)}) custom-call(bf16[768,480]{1,0:T(8,128)(2,1)S(1)} %get-tuple-element.387.nt_r, bf16[192,480]{1,0:T(8,128)(2,1)S(1)} %get-tuple-element.388.qa, bf16[192,480]{1,0:T(8,128)(2,1)S(1)} %get-tuple-element.389.ka, ...), custom_call_target="tpu_custom_call" | custom-call | flops 200000000 | bytes 300000 | tf_op jit(solution)/shard_map/weigh_body/pallas_call | solution.py:59
  128.6 3.0 %finish_body.1 = (bf16[480,768]{1,0:T(8,128)(2,1)S(1)}, f32[8,384]{1,0:T(8,128)S(1)}) custom-call(s32[2]{0:T(128)S(1)} %pad_add_fusion.info, f32[768,480]{1,0:T(8,128)S(1)} %get-tuple-element.398.dn0, f32[768,480]{1,0:T(8,128)S(1)} %get-tuple-element.399.dn1, bf16[480,768]{1,0:T(8,128)(2,1)S(1)} %get-tuple-element.305.x_r, ...), custom_call_target="tpu_custom_call" | custom-call | flops 40000000000 | bytes 60000000 | tf_op jit(solution)/shard_map/finish_body/pallas_call | solution.py:59
  131.7 4.9 %collective-permute-done.32.passed = bf16[608,384]{1,0:T(8,128)(2,1)S(1)} collective-permute-done((bf16[608,384]{1,0:T(8,128)(2,1)S(1)}, bf16[608,384]{1,0:T(8,128)(2,1)S(1)}, u32[]{:S(2)}, u32[]{:S(2)}) %collective-permute-start.32) | collective-permute-done | bytes 466976 | tf_op jit(solution)/shard_map/ppermute | solution.py:25
  139.6 2.7 %collective-permute-start.35 = (bf16[320,384]{1,0:T(8,128)(2,1)S(1)}, bf16[320,384]{1,0:T(8,128)(2,1)S(1)}, u32[]{:S(2)}, u32[]{:S(2)}) collective-permute-start(bf16[320,384]{1,0:T(8,128)(2,1)S(1)} %get-tuple-element.422), channel_id=1, source_target_pairs={{0,16},{1,17},{2,18},{3,19},{4,20},{5,21},{6,22},{7,23},{8,24},{9,... | collective-permute-start | bytes 737288 | tf_op jit(solution)/shard_map/ppermute | solution.py:25
  146.3 7.3 %collective-permute-done.35.got = bf16[320,384]{1,0:T(8,128)(2,1)S(1)} collective-permute-done((bf16[320,384]{1,0:T(8,128)(2,1)S(1)}, bf16[320,384]{1,0:T(8,128)(2,1)S(1)}, u32[]{:S(2)}, u32[]{:S(2)}) %collective-permute-start.35) | collective-permute-done | bytes 245792 | tf_op jit(solution)/shard_map/ppermute | solution.py:25
  159.0 6.0 %collective-permute-done.42.across = bf16[480,768]{1,0:T(8,128)(2,1)S(1)} collective-permute-done((bf16[480,768]{1,0:T(8,128)(2,1)S(1)}, bf16[480,768]{1,0:T(8,128)(2,1)S(1)}, u32[]{:S(2)}, u32[]{:S(2)}) %collective-permute-start.42) | collective-permute-done | bytes 737312 | tf_op jit(solution)/shard_map/ppermute | solution.py:25
  167.2 2.5 %join_body.3 = bf16[2,832,768]{2,1,0:T(8,128)(2,1)} custom-call(s32[2]{0:T(128)S(1)} %pad_add_fusion.info, s32[2,832]{1,0:T(2,128)S(1)} %copy-done.19, bf16[480,768]{1,0:T(8,128)(2,1)S(1)} %get-tuple-element.411.own, bf16[480,768]{1,0:T(8,128)(2,1)S(1)} %collective-permute-done.34.beside, bf16[480,768]{1,0:T(8,128)(2,1)S(1)} %collective-permute-done.42.across, ...), custom_call_target="tpu_custom_call" | custom-call | flops 40000000000 | bytes 60000000 | tf_op jit(solution)/shard_map/join_body/pallas_call | solution.py:59
  172.5 3.1 %collective-permute-done.45 = f32[8,384]{1,0:T(8,128)S(1)} collective-permute-done((f32[8,384]{1,0:T(8,128)S(1)}, f32[8,384]{1,0:T(8,128)S(1)}, u32[]{:S(2)}, u32[]{:S(2)}) %collective-permute-start.45) | collective-permute-done | bytes 12320 | tf_op jit(solution)/shard_map/ppermute | solution.py:25
  (170 shorter events, 62.6 us)
Async XLA Ops:
  8.0 10.7 %collective-permute-start.2 = (bf16[1,160,384]{2,1,0:T(8,128)(2,1)S(1)}, bf16[1,160,384]{2,1,0:T(8,128)(2,1)S(1)}, u32[]{:S(2)}, u32[]{:S(2)}) collective-permute-start(bf16[1,160,384]{2,1,0:T(8,128)(2,1)S(1)} %meet_a_body.1.refs_0_), channel_id=1, source_target_pairs={{0,8},{1,9},{2,10},{3,11},{4,12},{5,13},{6,14},{7,15},{8,0},{9,1},... | collective-permute-start | bytes 368648 | tf_op jit(solution)/shard_map/ppermute | solution.py:25
  11.1 12.4 %collective-permute-start.3 = (bf16[1,160,384]{2,1,0:T(8,128)(2,1)S(1)}, bf16[1,160,384]{2,1,0:T(8,128)(2,1)S(1)}, u32[]{:S(2)}, u32[]{:S(2)}) collective-permute-start(bf16[1,160,384]{2,1,0:T(8,128)(2,1)S(1)} %meet_a_body.1.refs_0_), channel_id=1, source_target_pairs={{0,16},{1,17},{2,18},{3,19},{4,20},{5,21},{6,22},{7,23},{8,24},{9,... | collective-permute-start | bytes 368648 | tf_op jit(solution)/shard_map/ppermute | solution.py:25
  13.7 9.8 %collective-permute-start.4 = (bf16[1,160,384]{2,1,0:T(8,128)(2,1)S(1)}, bf16[1,160,384]{2,1,0:T(8,128)(2,1)S(1)}, u32[]{:S(2)}, u32[]{:S(2)}) collective-permute-start(bf16[1,160,384]{2,1,0:T(8,128)(2,1)S(1)} %meet_a_body.1.refs_0_), channel_id=1, source_target_pairs={{0,24},{1,25},{2,26},{3,27},{4,28},{5,29},{6,30},{7,31},{8,16},{9,... | collective-permute-start | bytes 368648 | tf_op jit(solution)/shard_map/ppermute | solution.py:25
  23.6 15.1 %collective-permute-start.10 = (bf16[4,160,384]{2,1,0:T(8,128)(2,1)S(1)}, bf16[4,160,384]{2,1,0:T(8,128)(2,1)S(1)}, u32[]{:S(2)}, u32[]{:S(2)}) collective-permute-start(bf16[4,160,384]{2,1,0:T(8,128)(2,1)S(1)} %stack_body.2.refs_0_), channel_id=1, source_target_pairs={{0,2},{1,3},{2,0},{3,1},{4,6},{5,7},{6,4},{7,5},{8,10},{9,11},{10,... | collective-permute-start | bytes 1474568 | tf_op jit(solution)/shard_map/ppermute | solution.py:25
  25.2 13.5 %collective-permute-start.9 = (bf16[4,160,384]{2,1,0:T(8,128)(2,1)S(1)}, bf16[4,160,384]{2,1,0:T(8,128)(2,1)S(1)}, u32[]{:S(2)}, u32[]{:S(2)}) collective-permute-start(bf16[4,160,384]{2,1,0:T(8,128)(2,1)S(1)} %stack_body.2.refs_0_), channel_id=1, source_target_pairs={{0,4},{1,5},{2,6},{3,7},{4,0},{5,1},{6,2},{7,3},{8,12},{9,13},{10,... | collective-permute-start | bytes 1474568 | tf_op jit(solution)/shard_map/ppermute | solution.py:25
  28.7 9.9 %collective-permute-start.7 = (bf16[1,144,384]{2,1,0:T(8,128)(2,1)S(1)}, bf16[1,144,384]{2,1,0:T(8,128)(2,1)S(1)}, u32[]{:S(2)}, u32[]{:S(2)}) collective-permute-start(bf16[1,144,384]{2,1,0:T(8,128)(2,1)S(1)} %meet_b_body.1.refs_0_), channel_id=1, source_target_pairs={{0,16},{1,17},{2,18},{3,19},{4,20},{5,21},{6,22},{7,23},{8,24},{9,... | collective-permute-start | bytes 331784 | tf_op jit(solution)/shard_map/ppermute | solution.py:25
  39.2 15.0 %collective-permute-start.14 = (bf16[4,160,384]{2,1,0:T(8,128)(2,1)S(1)}, bf16[4,160,384]{2,1,0:T(8,128)(2,1)S(1)}, u32[]{:S(2)}, u32[]{:S(2)}) collective-permute-start(bf16[4,160,384]{2,1,0:T(8,128)(2,1)S(1)} %stack_body.2.refs_0_), channel_id=1, source_target_pairs={{0,6},{1,7},{2,4},{3,5},{4,2},{5,3},{6,0},{7,1},{8,14},{9,15},{10,... | collective-permute-start | bytes 1474568 | tf_op jit(solution)/shard_map/ppermute | solution.py:25
  43.0 24.6 %collective-permute-start.17 = (bf16[4,144,384]{2,1,0:T(8,128)(2,1)S(1)}, bf16[4,144,384]{2,1,0:T(8,128)(2,1)S(1)}, u32[]{:S(2)}, u32[]{:S(2)}) collective-permute-start(bf16[4,144,384]{2,1,0:T(8,128)(2,1)S(1)} %stack_body.3.refs_0_), channel_id=1, source_target_pairs={{0,4},{1,5},{2,6},{3,7},{4,0},{5,1},{6,2},{7,3},{8,12},{9,13},{10,... | collective-permute-start | bytes 1327112 | tf_op jit(solution)/shard_map/ppermute | solution.py:25
  43.6 24.0 %collective-permute-start.18 = (bf16[4,144,384]{2,1,0:T(8,128)(2,1)S(1)}, bf16[4,144,384]{2,1,0:T(8,128)(2,1)S(1)}, u32[]{:S(2)}, u32[]{:S(2)}) collective-permute-start(bf16[4,144,384]{2,1,0:T(8,128)(2,1)S(1)} %stack_body.3.refs_0_), channel_id=1, source_target_pairs={{0,2},{1,3},{2,0},{3,1},{4,6},{5,7},{6,4},{7,5},{8,10},{9,11},{10,... | collective-permute-start | bytes 1327112 | tf_op jit(solution)/shard_map/ppermute | solution.py:25
  44.5 9.7 %collective-permute-start.13 = (bf16[4,160,384]{2,1,0:T(8,128)(2,1)S(1)}, bf16[4,160,384]{2,1,0:T(8,128)(2,1)S(1)}, u32[]{:S(2)}, u32[]{:S(2)}) collective-permute-start(bf16[4,160,384]{2,1,0:T(8,128)(2,1)S(1)} %collective-permute-done.10.refs_0_), channel_id=1, source_target_pairs={{0,1},{1,0},{2,3},{3,2},{4,5},{5,4},{6,7},{7,6},{8,9},{9,8},{10,11... | collective-permute-start | bytes 1474568 | tf_op jit(solution)/shard_map/ppermute | solution.py:25
  54.2 19.6 %collective-permute-start.21 = (bf16[4,144,384]{2,1,0:T(8,128)(2,1)S(1)}, bf16[4,144,384]{2,1,0:T(8,128)(2,1)S(1)}, u32[]{:S(2)}, u32[]{:S(2)}) collective-permute-start(bf16[4,144,384]{2,1,0:T(8,128)(2,1)S(1)} %stack_body.3.refs_0_), channel_id=1, source_target_pairs={{0,6},{1,7},{2,4},{3,5},{4,2},{5,3},{6,0},{7,1},{8,14},{9,15},{10,... | collective-permute-start | bytes 1327112 | tf_op jit(solution)/shard_map/ppermute | solution.py:25
  80.6 9.8 %collective-permute-start.23 = (bf16[480,768]{1,0:T(8,128)(2,1)S(1)}, bf16[480,768]{1,0:T(8,128)(2,1)S(1)}, u32[]{:S(2)}, u32[]{:S(2)}) collective-permute-start(bf16[480,768]{1,0:T(8,128)(2,1)S(1)} %get-tuple-element.423.own), channel_id=1, source_target_pairs={{0,1},{1,0},{2,3},{3,2},{4,5},{5,4},{6,7},{7,6},{8,9},{9,8},{10,11... | collective-permute-start | bytes 2211848 | tf_op jit(solution)/shard_map/ppermute | solution.py:25
  80.9 27.6 %collective-permute-start.26 = (bf16[480,768]{1,0:T(8,128)(2,1)S(1)}, bf16[480,768]{1,0:T(8,128)(2,1)S(1)}, u32[]{:S(2)}, u32[]{:S(2)}) collective-permute-start(bf16[480,768]{1,0:T(8,128)(2,1)S(1)} %get-tuple-element.423.own), channel_id=1, source_target_pairs={{0,2},{1,3},{2,0},{3,1},{4,6},{5,7},{6,4},{7,5},{8,10},{9,11},{10,... | collective-permute-start | bytes 2211848 | tf_op jit(solution)/shard_map/ppermute | solution.py:25
  98.6 25.3 %collective-permute-start.29 = (bf16[1184,384]{1,0:T(8,128)(2,1)S(1)}, bf16[1184,384]{1,0:T(8,128)(2,1)S(1)}, u32[]{:S(2)}, u32[]{:S(2)}) collective-permute-start(bf16[1184,384]{1,0:T(8,128)(2,1)S(1)} %get-tuple-element.386), channel_id=1, source_target_pairs={{0,2},{1,3},{2,0},{3,1},{4,6},{5,7},{6,4},{7,5},{8,10},{9,11},{10,... | collective-permute-start | bytes 2727944 | tf_op jit(solution)/shard_map/ppermute | solution.py:25
  115.8 15.8 %collective-permute-start.31 = (bf16[576,384]{1,0:T(8,128)(2,1)S(1)}, bf16[576,384]{1,0:T(8,128)(2,1)S(1)}, u32[]{:S(2)}, u32[]{:S(2)}) collective-permute-start(bf16[576,384]{1,0:T(8,128)(2,1)S(1)} %get-tuple-element.406), channel_id=1, source_target_pairs={{0,2},{1,3},{2,0},{3,1},{4,6},{5,7},{6,4},{7,5},{8,10},{9,11},{10,... | collective-permute-start | bytes 1327112 | tf_op jit(solution)/shard_map/ppermute | solution.py:25
  124.1 12.5 %collective-permute-start.32 = (bf16[608,384]{1,0:T(8,128)(2,1)S(1)}, bf16[608,384]{1,0:T(8,128)(2,1)S(1)}, u32[]{:S(2)}, u32[]{:S(2)}) collective-permute-start(bf16[608,384]{1,0:T(8,128)(2,1)S(1)} %get-tuple-element.409), channel_id=1, source_target_pairs={{0,4},{1,5},{2,6},{3,7},{4,0},{5,1},{6,2},{7,3},{8,12},{9,13},{10,... | collective-permute-start | bytes 1400840 | tf_op jit(solution)/shard_map/ppermute | solution.py:25
  137.1 16.5 %collective-permute-start.37 = (bf16[576,384]{1,0:T(8,128)(2,1)S(1)}, bf16[576,384]{1,0:T(8,128)(2,1)S(1)}, u32[]{:S(2)}, u32[]{:S(2)}) collective-permute-start(bf16[576,384]{1,0:T(8,128)(2,1)S(1)} %get-tuple-element.432), channel_id=1, source_target_pairs={{0,2},{1,3},{2,0},{3,1},{4,6},{5,7},{6,4},{7,5},{8,10},{9,11},{10,... | collective-permute-start | bytes 1327112 | tf_op jit(solution)/shard_map/ppermute | solution.py:25
  137.6 27.4 %collective-permute-start.42 = (bf16[480,768]{1,0:T(8,128)(2,1)S(1)}, bf16[480,768]{1,0:T(8,128)(2,1)S(1)}, u32[]{:S(2)}, u32[]{:S(2)}) collective-permute-start(bf16[480,768]{1,0:T(8,128)(2,1)S(1)} %get-tuple-element.411.own), channel_id=1, source_target_pairs={{0,2},{1,3},{2,0},{3,1},{4,6},{5,7},{6,4},{7,5},{8,10},{9,11},{10,... | collective-permute-start | bytes 2211848 | tf_op jit(solution)/shard_map/ppermute | solution.py:25
  139.6 13.9 %collective-permute-start.35 = (bf16[320,384]{1,0:T(8,128)(2,1)S(1)}, bf16[320,384]{1,0:T(8,128)(2,1)S(1)}, u32[]{:S(2)}, u32[]{:S(2)}) collective-permute-start(bf16[320,384]{1,0:T(8,128)(2,1)S(1)} %get-tuple-element.422), channel_id=1, source_target_pairs={{0,16},{1,17},{2,18},{3,19},{4,20},{5,21},{6,22},{7,23},{8,24},{9,... | collective-permute-start | bytes 737288 | tf_op jit(solution)/shard_map/ppermute | solution.py:25
  142.3 11.9 %collective-permute-start.36 = (bf16[592,384]{1,0:T(8,128)(2,1)S(1)}, bf16[592,384]{1,0:T(8,128)(2,1)S(1)}, u32[]{:S(2)}, u32[]{:S(2)}) collective-permute-start(bf16[592,384]{1,0:T(8,128)(2,1)S(1)} %get-tuple-element.431), channel_id=1, source_target_pairs={{0,4},{1,5},{2,6},{3,7},{4,0},{5,1},{6,2},{7,3},{8,12},{9,13},{10,... | collective-permute-start | bytes 1363976 | tf_op jit(solution)/shard_map/ppermute | solution.py:25
  154.4 10.6 %collective-permute-start.41 = (bf16[176,384]{1,0:T(8,128)(2,1)S(1)}, bf16[176,384]{1,0:T(8,128)(2,1)S(1)}, u32[]{:S(2)}, u32[]{:S(2)}) collective-permute-start(bf16[176,384]{1,0:T(8,128)(2,1)S(1)} %get-tuple-element.450), channel_id=1, source_target_pairs={{0,8},{1,9},{2,10},{3,11},{4,12},{5,13},{6,14},{7,15},{8,0},{9,1},... | collective-permute-start | bytes 405512 | tf_op jit(solution)/shard_map/ppermute | solution.py:25
  154.5 16.6 %collective-permute-start.38 = (bf16[160,384]{1,0:T(8,128)(2,1)S(1)}, bf16[160,384]{1,0:T(8,128)(2,1)S(1)}, u32[]{:S(2)}, u32[]{:S(2)}) collective-permute-start(bf16[160,384]{1,0:T(8,128)(2,1)S(1)} %get-tuple-element.445), channel_id=1, source_target_pairs={{0,8},{1,9},{2,10},{3,11},{4,12},{5,13},{6,14},{7,15},{8,0},{9,1},... | collective-permute-start | bytes 368648 | tf_op jit(solution)/shard_map/ppermute | solution.py:25
  156.5 14.6 %collective-permute-start.39 = (bf16[160,384]{1,0:T(8,128)(2,1)S(1)}, bf16[160,384]{1,0:T(8,128)(2,1)S(1)}, u32[]{:S(2)}, u32[]{:S(2)}) collective-permute-start(bf16[160,384]{1,0:T(8,128)(2,1)S(1)} %get-tuple-element.446), channel_id=1, source_target_pairs={{0,16},{1,17},{2,18},{3,19},{4,20},{5,21},{6,22},{7,23},{8,24},{9,... | collective-permute-start | bytes 368648 | tf_op jit(solution)/shard_map/ppermute | solution.py:25
  156.9 14.2 %collective-permute-start.40 = (bf16[160,384]{1,0:T(8,128)(2,1)S(1)}, bf16[160,384]{1,0:T(8,128)(2,1)S(1)}, u32[]{:S(2)}, u32[]{:S(2)}) collective-permute-start(bf16[160,384]{1,0:T(8,128)(2,1)S(1)} %get-tuple-element.447), channel_id=1, source_target_pairs={{0,24},{1,25},{2,26},{3,27},{4,28},{5,29},{6,30},{7,31},{8,16},{9,... | collective-permute-start | bytes 368648 | tf_op jit(solution)/shard_map/ppermute | solution.py:25
  (43 other events, 244.5 us)
where the time goes:
time: 179 us; the launch traced here: 178 us
  Pallas kernels  87.5 us (49%)
  waiting for transfers between devices  39.7 us (22%)
  starting transfers between devices  37.4 us (21%)
  local copies, waits for them, and re-layouts  12.3 us (7%)
    pallas_call x34, Pallas kernels, call(): pl.pallas_call(body, out_shape=tuple((jax.ShapeDtypeStruct(s, d) for s, d...  87.5 us
    ppermute x47, waiting for transfers between devices, send(): return lax.ppermute(value, BOTH, pairs)  39.7 us
    ppermute x47, starting transfers between devices, send(): return lax.ppermute(value, BOTH, pairs)  37.4 us
    unnamed x42, local copies, waits for them, and re-layouts  5.82 us
  transfers between devices with their start and end apart: 47, of which 13 were waited for; matrix products, arithmetic and copies ran while one was open for 3% of the time, Pallas kernels for 45%

commit v1 on v0

--- a/solution.py
+++ b/solution.py
@@ -117,10 +117,13 @@
     pads = jnp.where(y == 0, pads[0:1], pads[1:2])
     code = jnp.where(pads == 0, segs, -1.0)
     segs = jnp.where(core == 0, segs[:, :window], segs[:, gap:])
+    wide = bias_o.shape[1]
+    if wide > window:
+        segs = jnp.concatenate([segs, jnp.full((1, wide - window), -2.0, F32)], axis=1)
     code = jnp.where(core == 0, code[:, :window], code[:, gap:])
     column = jnp.broadcast_to(code, (8, window)).T[:, 0:1]
-    key = lax.broadcasted_iota(jnp.int32, (window, window), 0)
-    query = lax.broadcasted_iota(jnp.int32, (window, window), 1)
+    key = lax.broadcasted_iota(jnp.int32, (window, wide), 0)
+    query = lax.broadcasted_iota(jnp.int32, (window, wide), 1)
     bias_o[...] = jnp.where((column == segs) | (key == query), 0.0, -1e30)
 
 
@@ -217,21 +220,34 @@
 
 def forward_body(first, qt, kt, vt, bias, ot, lse):
     heads, _, window = ot.shape
-
-    def head(i, carry):
-        h = first + i
+    rows = 4 * PAD
+
+    def four(i, carry):
+        h = first + 4 * i
         for q0, qn, k0, k1 in tiles(window):
-            scores = dot_tn(kt[h, :, k0:k1], qt[h, :, q0 : q0 + qn])
-            scores = scores * LOG2 + bias[k0:k1, q0 : q0 + qn]
-            top = jnp.max(scores, axis=0, keepdims=True)
-            weight = jnp.exp2(scores - top).astype(BF16)
-            mixed = dot_nn(vt[h, :, k0:k1], weight)
-            total = mixed[HD : HD + 1]
-            ot[i, :, q0 : q0 + qn] = mixed / total
-            lse[i, :, q0 : q0 + qn] = top + jnp.log2(total)
+            query = qt[pl.ds(h, 4), :, q0 : q0 + qn].reshape(rows, qn).astype(F32)
+            if qn < 256:
+                query = jnp.concatenate([query, jnp.zeros((rows, 256 - qn), F32)], axis=1)
+            own = lax.broadcasted_iota(jnp.int32, (rows, 256), 0) // PAD
+            block = [jnp.where(own == n, query, 0.0).astype(BF16) for n in range(4)]
+            keys = kt[pl.ds(h, 4), :, k0:k1].reshape(rows, k1 - k0)
+            values = vt[pl.ds(h, 4), :, k0:k1].reshape(rows, k1 - k0)
+            scores = dot_tn(keys, jnp.concatenate(block, axis=1))
+            tops, weights = [], []
+            for n in range(4):
+                part = scores[:, n * 256 : (n + 1) * 256] * LOG2 + bias[k0:k1, q0 : q0 + 256]
+                top = jnp.max(part, axis=0, keepdims=True)
+                tops.append(top)
+                weights.append(jnp.exp2(part - top).astype(BF16))
+            mixed = dot_nn(values, jnp.concatenate(weights, axis=1))
+            for n in range(4):
+                own_mixed = mixed[n * PAD : (n + 1) * PAD, n * 256 : n * 256 + qn]
+                total = own_mixed[HD : HD + 1]
+                ot[4 * i + n, :, q0 : q0 + qn] = own_mixed / total
+                lse[4 * i + n, :, q0 : q0 + qn] = tops[n][:, :qn] + jnp.log2(total)
         return carry
 
-    lax.fori_loop(0, heads, head, 0, unroll=2)
+    lax.fori_loop(0, heads // 4, four, 0)
 
 
 def feed_body(places, high, x_r, o00, o01, o10, o11, small, cols0, cols1, target, *refs):
@@ -286,14 +302,20 @@
     for yr in range(2):
         assemble(blocks[yr * count : (yr + 1) * count], places, high, weights[yr])
     ct_low, normed = c_r[...], n_r[...]
-    dnorm, ups = None, []
-    for yr, (act, slope) in enumerate(((act0, slope0), (act1, slope1))):
-        disassemble(dot_tn(ct_low, act[...]), outs, (yr, 2))
-        dpre = (dot_nn(ct_low, weights[yr][2]) * slope[...]).astype(BF16)
-        disassemble(dot_tn(normed, dpre), outs, (yr, 1))
-        ups.append(jnp.sum(dpre.astype(F32), axis=0, keepdims=True))
-        part = dot_nt(dpre, weights[yr][1])
-        dnorm = part if dnorm is None else dnorm + part
+    cols = act0.shape[1]
+
+    def both(left, right, w):
+        grads = dot_tn(left, jnp.concatenate(right, axis=1))
+        for yr in range(2):
+            disassemble(grads[:, yr * cols : (yr + 1) * cols], outs, (yr, w))
+
+    both(ct_low, [act0[...], act1[...]], 2)
+    dpres = [
+        (dot_nn(ct_low, weights[yr][2]) * slope[...]).astype(BF16) for yr, slope in enumerate((slope0, slope1))
+    ]
+    both(normed, dpres, 1)
+    ups = [jnp.sum(dpre.astype(F32), axis=0, keepdims=True) for dpre in dpres]
+    dnorm = dot_nt(dpres[0], weights[0][1]) + dot_nt(dpres[1], weights[1][1])
     ct, xhat = ct_low.astype(F32), xhat_r[...]
     dmiddle = ct + norm_back(dnorm, xhat, inv_r[...], small[3:4])
     mid_o[...] = dmiddle
@@ -304,8 +326,8 @@
     sums = rows_of(info, sums[0:4], [ups])
     sum_o[...] = jnp.concatenate([sums, jnp.zeros_like(sums[0:6])], axis=0)
     low = dmiddle.astype(BF16)
-    for yr, att in enumerate((a0, a1)):
-        disassemble(dot_tn(low, att[...]), outs, (yr, 0))
+    both(low, [a0[...], a1[...]], 0)
+    for yr in range(2):
         (d0, d1)[yr][...] = by_head(dot_nn(low, weights[yr][0]))
 
 
@@ -647,7 +669,7 @@
     def begin(target):
         return call(
             start_body,
-            [(wide, BF16), (wide, BF16), (wide, F32), ((window, window), F32)],
+            [(wide, BF16), (wide, BF16), (wide, F32), ((window, -(-window // 256) * 256), F32)],
             [side, hidden_in, cotangent, segment_ids, pad_flags, target],
             (),
             1,
@@ -701,7 +723,7 @@
             [weights, weights],
             1,
             us=7,
-            mib=7,
+            mib=10,
         )
 
     def backward(part, qkv_heads, da, o, lse, bias):
@@ -838,10 +860,10 @@
         near = [qkv, qkv_c, qkv_x, qkv_xc]
         *heads0, shift0, small, normed, normed_t = project(xhat, near, True)
         heads0, qkv_y, odu = fence(heads0, qkv_y, odu)
-        qkv_yc, odu_x, odu_y = to(qkv_y, 0, 1), to(odu, 1, 0), to(odu, 0, 2)
+        qkv_yc, odu_x, odu_y, odu_xy = to(qkv_y, 0, 1), to(odu, 1, 0), to(odu, 0, 2), to(odu, 1, 2)
         o00, l00 = attend(0, heads0, bias)
         o00, heads0, qkv_yc, qkv_xy, odu = fence(o00, heads0, qkv_yc, qkv_xy, odu)
-        qkv_xyc, odu_xy, odu_c = to(qkv_xy, 0, 1), to(odu, 1, 2), to(odu, 0, 1)
+        qkv_xyc, odu_c = to(qkv_xy, 0, 1), to(odu, 0, 1)
         o01, l01 = attend(1, heads0, bias)
         o01, qkv_xyc, odu_c, normed = fence(o01, qkv_xyc, odu_c, normed)
         far = [qkv_y, qkv_yc, qkv_xy, qkv_xyc]

time: 179 us -> 175 us (0.978)
  Pallas kernels: 87.5 us -> 75.6 us
  waiting for transfers between devices: 39.7 us -> 47.9 us
    pallas_call x34, Pallas kernels: 87.5 us -> 75.6 us  [call(): pl.pallas_call(body, out_shape=tuple((jax.ShapeDtypeStruct(s, d) for s, d...]
    ppermute x47, waiting for transfers between devices: 39.7 us -> 47.9 us  [send(): return lax.ppermute(value, BOTH, pairs)]
  transfers between devices with their start and end apart: 47 -> 47, of which waited for: 13 -> 16; matrix products, arithmetic and copies ran while one was open for 3% -> 3% of each run, Pallas kernels for 45% -> 39%
where the time goes in v1:
time: 175 us
  Pallas kernels  75.6 us (43%)
  waiting for transfers between devices  47.9 us (27%)
  starting transfers between devices  36.7 us (21%)
  local copies, waits for them, and re-layouts  12.9 us (7%)
    pallas_call x34, Pallas kernels, call(): pl.pallas_call(body, out_shape=tuple((jax.ShapeDtypeStruct(s, d) for s, d...  75.6 us
    ppermute x47, waiting for transfers between devices, send(): return lax.ppermute(value, BOTH, pairs)  47.9 us
    ppermute x47, starting transfers between devices, send(): return lax.ppermute(value, BOTH, pairs)  36.7 us
    unnamed x42, local copies, waits for them, and re-layouts  6.47 us
  transfers between devices with their start and end apart: 47, of which 16 were waited for; matrix products, arithmetic and copies ran while one was open for 3% of the time, Pallas kernels for 39%

profile of v1, /device:TPU:0, one launch (start us, length us, event | category | flops | bytes accessed | tf_op | source)
XLA Modules:
  0.0 174.5 jit_solution(2641643616736652924)
XLA Ops:
  8.0 3.1 %collective-permute-start.2 = (bf16[1,160,384]{2,1,0:T(8,128)(2,1)S(1)}, bf16[1,160,384]{2,1,0:T(8,128)(2,1)S(1)}, u32[]{:S(2)}, u32[]{:S(2)}) collective-permute-start(bf16[1,160,384]{2,1,0:T(8,128)(2,1)S(1)} %meet_a_body.1.refs_0_), channel_id=1, source_target_pairs={{0,8},{1,9},{2,10},{3,11},{4,12},{5,13},{6,14},{7,15},{8,0},{9,1},... | collective-permute-start | bytes 368648 | tf_op jit(solution)/shard_map/ppermute | solution.py:25
  11.1 2.6 %collective-permute-start.3 = (bf16[1,160,384]{2,1,0:T(8,128)(2,1)S(1)}, bf16[1,160,384]{2,1,0:T(8,128)(2,1)S(1)}, u32[]{:S(2)}, u32[]{:S(2)}) collective-permute-start(bf16[1,160,384]{2,1,0:T(8,128)(2,1)S(1)} %meet_a_body.1.refs_0_), channel_id=1, source_target_pairs={{0,16},{1,17},{2,18},{3,19},{4,20},{5,21},{6,22},{7,23},{8,24},{9,... | collective-permute-start | bytes 368648 | tf_op jit(solution)/shard_map/ppermute | solution.py:25
  18.8 4.8 %collective-permute-done.3.refs_2_ = bf16[1,160,384]{2,1,0:T(8,128)(2,1)S(1)} collective-permute-done((bf16[1,160,384]{2,1,0:T(8,128)(2,1)S(1)}, bf16[1,160,384]{2,1,0:T(8,128)(2,1)S(1)}, u32[]{:S(2)}, u32[]{:S(2)}) %collective-permute-start.3) | collective-permute-done | bytes 122912 | tf_op jit(solution)/shard_map/ppermute | solution.py:25
  35.0 3.6 %collective-permute-done.7.refs_2_ = bf16[1,144,384]{2,1,0:T(8,128)(2,1)S(1)} collective-permute-done((bf16[1,144,384]{2,1,0:T(8,128)(2,1)S(1)}, bf16[1,144,384]{2,1,0:T(8,128)(2,1)S(1)}, u32[]{:S(2)}, u32[]{:S(2)}) %collective-permute-start.7) | collective-permute-done | bytes 110624 | tf_op jit(solution)/shard_map/ppermute | solution.py:25
  46.5 2.8 %forward_body.4 = (f32[8,32,480]{2,1,0:T(8,128)S(1)}, f32[8,1,480]{2,1,0:T(1,128)S(1)}) custom-call(bf16[16,32,480]{2,1,0:T(8,128)(2,1)S(1)} %get-tuple-element.376.qt, bf16[16,32,480]{2,1,0:T(8,128)(2,1)S(1)} %get-tuple-element.377.kt, bf16[16,32,480]{2,1,0:T(8,128)(2,1)S(1)} %get-tuple-element.378.vt, f32[480,512]{1,0:T(8,128)S(1)} %get-tuple-element.283.bias), custom_call_target="tpu_custom_call" | custom-call | flops 10000000000 | bytes 15000000 | tf_op jit(solution)/shard_map/forward_body/pallas_call | solution.py:59
  49.3 4.9 %collective-permute-done.14.refs_2_ = bf16[4,160,384]{2,1,0:T(8,128)(2,1)S(1)} collective-permute-done((bf16[4,160,384]{2,1,0:T(8,128)(2,1)S(1)}, bf16[4,160,384]{2,1,0:T(8,128)(2,1)S(1)}, u32[]{:S(2)}, u32[]{:S(2)}) %collective-permute-start.14) | collective-permute-done | bytes 491552 | tf_op jit(solution)/shard_map/ppermute | solution.py:25
  54.8 2.8 %forward_body.5 = (f32[8,32,480]{2,1,0:T(8,128)S(1)}, f32[8,1,480]{2,1,0:T(1,128)S(1)}) custom-call(bf16[16,32,480]{2,1,0:T(8,128)(2,1)S(1)} %get-tuple-element.376.qt, bf16[16,32,480]{2,1,0:T(8,128)(2,1)S(1)} %get-tuple-element.377.kt, bf16[16,32,480]{2,1,0:T(8,128)(2,1)S(1)} %get-tuple-element.378.vt, f32[480,512]{1,0:T(8,128)S(1)} %get-tuple-element.283.bias), custom_call_target="tpu_custom_call" | custom-call | flops 10000000000 | bytes 15000000 | tf_op jit(solution)/shard_map/forward_body/pallas_call | solution.py:59
  59.1 2.8 %forward_body.6 = (f32[8,32,480]{2,1,0:T(8,128)S(1)}, f32[8,1,480]{2,1,0:T(1,128)S(1)}) custom-call(bf16[16,32,480]{2,1,0:T(8,128)(2,1)S(1)} %get-tuple-element.343.qt, bf16[16,32,480]{2,1,0:T(8,128)(2,1)S(1)} %get-tuple-element.344.kt, bf16[16,32,480]{2,1,0:T(8,128)(2,1)S(1)} %get-tuple-element.345.vt, f32[480,512]{1,0:T(8,128)S(1)} %get-tuple-element.283.bias), custom_call_target="tpu_custom_call" | custom-call | flops 10000000000 | bytes 15000000 | tf_op jit(solution)/shard_map/forward_body/pallas_call | solution.py:59
  64.1 3.0 %forward_body.7 = (f32[8,32,480]{2,1,0:T(8,128)S(1)}, f32[8,1,480]{2,1,0:T(1,128)S(1)}) custom-call(bf16[16,32,480]{2,1,0:T(8,128)(2,1)S(1)} %get-tuple-element.343.qt, bf16[16,32,480]{2,1,0:T(8,128)(2,1)S(1)} %get-tuple-element.344.kt, bf16[16,32,480]{2,1,0:T(8,128)(2,1)S(1)} %get-tuple-element.345.vt, f32[480,512]{1,0:T(8,128)S(1)} %get-tuple-element.283.bias), custom_call_target="tpu_custom_call" | custom-call | flops 10000000000 | bytes 15000000 | tf_op jit(solution)/shard_map/forward_body/pallas_call | solution.py:59
  67.1 5.2 %collective-permute-done.21.refs_6_ = bf16[4,144,384]{2,1,0:T(8,128)(2,1)S(1)} collective-permute-done((bf16[4,144,384]{2,1,0:T(8,128)(2,1)S(1)}, bf16[4,144,384]{2,1,0:T(8,128)(2,1)S(1)}, u32[]{:S(2)}, u32[]{:S(2)}) %collective-permute-start.21) | collective-permute-done | bytes 442400 | tf_op jit(solution)/shard_map/ppermute | solution.py:25
  74.1 4.9 %feed_body.1 = (bf16[480,768]{1,0:T(8,128)(2,1)S(1)}, f32[480,768]{1,0:T(8,128)S(1)}, f32[480,1]{1,0:T(8,128)S(1)}, bf16[480,768]{1,0:T(8,128)(2,1)S(1)}, bf16[4...) custom-call(bf16[480,768]{1,0:T(8,128)(2,1)S(1)} %get-tuple-element., ...), custom_call_target="tpu_custom_call" | custom-call | flops 10000000000 | bytes 15000000 | tf_op jit(solution)/shard_map/feed_body/pallas_call | solution.py:59
  79.7 6.8 %feed_back_body.1 = (f32[480,768]{1,0:T(8,128)S(1)}, bf16[16,32,480]{2,1,0:T(8,128)(2,1)S(1)}, bf16[16,32,480]{2,1,0:T(8,128)(2,1)S(1)}, f32[16,384]{1,0:T(8,128...) custom-call(s32[2]{0:T(128)S(1)} %pad_add_fusion.info, ...), custom_call_target="tpu_custom_call" | custom-call | flops 14000000000 | bytes 21000000 | tf_op jit(solution)/shard_map/feed_back_body/pallas_call | solution.py:59
  87.9 6.5 %backward_body.4 = (bf16[192,480]{1,0:T(8,128)(2,1)S(1)}, bf16[192,480]{1,0:T(8,128)(2,1)S(1)}, bf16[192,480]{1,0:T(8,128)(2,1)S(1)}) custom-call(bf16[16,32,480]{2,1,0:T(8,128)(2,1)S(1)} %get-tuple-element.343.qt, bf16[16,32,480]{2,1,0:T(8,128)(2,1)S(1)} %get-tuple-element.344.kt, bf16[16,32,480]{2,1,0:T(8,128)(2,1)S(1)} %get-tuple-element.345.vt, ...), custom_call_target="tpu_custom_call" | custom-call | flops 30000001024 | bytes 45000000 | tf_op jit(solution)/shard_map/backward_body/pallas_call | solution.py:59
  96.2 6.7 %backward_body.5 = (bf16[192,480]{1,0:T(8,128)(2,1)S(1)}, bf16[192,480]{1,0:T(8,128)(2,1)S(1)}, bf16[192,480]{1,0:T(8,128)(2,1)S(1)}) custom-call(bf16[16,32,480]{2,1,0:T(8,128)(2,1)S(1)} %get-tuple-element.343.qt, bf16[16,32,480]{2,1,0:T(8,128)(2,1)S(1)} %get-tuple-element.344.kt, bf16[16,32,480]{2,1,0:T(8,128)(2,1)S(1)} %get-tuple-element.345.vt, ...), custom_call_target="tpu_custom_call" | custom-call | flops 30000001024 | bytes 45000000 | tf_op jit(solution)/shard_map/backward_body/pallas_call | solution.py:59
  103.0 2.8 %weigh_body.2 = (f32[768,480]{1,0:T(8,128)S(1)}, f32[2,384]{1,0:T(2,128)S(1)}, bf16[2,4,144,384]{3,2,1,0:T(8,128)(2,1)S(1)}, bf16[2,4,144,384]{3,2,1,0:T(8,128)(2,1)S(1)}) custom-call(bf16[768,480]{1,0:T(8,128)(2,1)S(1)} %get-tuple-element.387.nt_r, bf16[192,480]{1,0:T(8,128)(2,1)S(1)} %get-tuple-element.352.qa, bf16[192,480]{1,0:T(8,128)(2,1)S(1)} %get-tuple-element.353.ka, ...), custom_call_target="tpu_custom_call" | custom-call | flops 200000000 | bytes 300000 | tf_op jit(solution)/shard_map/weigh_body/pallas_call | solution.py:59
  106.4 6.5 %backward_body.6 = (bf16[192,480]{1,0:T(8,128)(2,1)S(1)}, bf16[192,480]{1,0:T(8,128)(2,1)S(1)}, bf16[192,480]{1,0:T(8,128)(2,1)S(1)}) custom-call(bf16[16,32,480]{2,1,0:T(8,128)(2,1)S(1)} %get-tuple-element.376.qt, bf16[16,32,480]{2,1,0:T(8,128)(2,1)S(1)} %get-tuple-element.377.kt, bf16[16,32,480]{2,1,0:T(8,128)(2,1)S(1)} %get-tuple-element.378.vt, ...), custom_call_target="tpu_custom_call" | custom-call | flops 30000001024 | bytes 45000000 | tf_op jit(solution)/shard_map/backward_body/pallas_call | solution.py:59
  113.7 6.5 %backward_body.7 = (bf16[192,480]{1,0:T(8,128)(2,1)S(1)}, bf16[192,480]{1,0:T(8,128)(2,1)S(1)}, bf16[192,480]{1,0:T(8,128)(2,1)S(1)}) custom-call(bf16[16,32,480]{2,1,0:T(8,128)(2,1)S(1)} %get-tuple-element.376.qt, bf16[16,32,480]{2,1,0:T(8,128)(2,1)S(1)} %get-tuple-element.377.kt, bf16[16,32,480]{2,1,0:T(8,128)(2,1)S(1)} %get-tuple-element.378.vt, ...), custom_call_target="tpu_custom_call" | custom-call | flops 30000001024 | bytes 45000000 | tf_op jit(solution)/shard_map/backward_body/pallas_call | solution.py:59
  121.7 2.8 %weigh_body.3 = (f32[768,480]{1,0:T(8,128)S(1)}, f32[2,384]{1,0:T(2,128)S(1)}, bf16[2,4,144,384]{3,2,1,0:T(8,128)(2,1)S(1)}, bf16[2,4,144,384]{3,2,1,0:T(8,128)(2,1)S(1)}) custom-call(bf16[768,480]{1,0:T(8,128)(2,1)S(1)} %get-tuple-element.387.nt_r, bf16[192,480]{1,0:T(8,128)(2,1)S(1)} %get-tuple-element.388.qa, bf16[192,480]{1,0:T(8,128)(2,1)S(1)} %get-tuple-element.389.ka, ...), custom_call_target="tpu_custom_call" | custom-call | flops 200000000 | bytes 300000 | tf_op jit(solution)/shard_map/weigh_body/pallas_call | solution.py:59
  124.6 3.0 %finish_body.1 = (bf16[480,768]{1,0:T(8,128)(2,1)S(1)}, f32[8,384]{1,0:T(8,128)S(1)}) custom-call(s32[2]{0:T(128)S(1)} %pad_add_fusion.info, f32[768,480]{1,0:T(8,128)S(1)} %get-tuple-element.398.dn0, f32[768,480]{1,0:T(8,128)S(1)} %get-tuple-element.399.dn1, bf16[480,768]{1,0:T(8,128)(2,1)S(1)} %get-tuple-element.305.x_r, ...), custom_call_target="tpu_custom_call" | custom-call | flops 40000000000 | bytes 60000000 | tf_op jit(solution)/shard_map/finish_body/pallas_call | solution.py:59
  127.6 5.3 %collective-permute-done.32.passed = bf16[608,384]{1,0:T(8,128)(2,1)S(1)} collective-permute-done((bf16[608,384]{1,0:T(8,128)(2,1)S(1)}, bf16[608,384]{1,0:T(8,128)(2,1)S(1)}, u32[]{:S(2)}, u32[]{:S(2)}) %collective-permute-start.32) | collective-permute-done | bytes 466976 | tf_op jit(solution)/shard_map/ppermute | solution.py:25
  135.9 2.7 %collective-permute-start.35 = (bf16[320,384]{1,0:T(8,128)(2,1)S(1)}, bf16[320,384]{1,0:T(8,128)(2,1)S(1)}, u32[]{:S(2)}, u32[]{:S(2)}) collective-permute-start(bf16[320,384]{1,0:T(8,128)(2,1)S(1)} %get-tuple-element.422), channel_id=1, source_target_pairs={{0,16},{1,17},{2,18},{3,19},{4,20},{5,21},{6,22},{7,23},{8,24},{9,... | collective-permute-start | bytes 737288 | tf_op jit(solution)/shard_map/ppermute | solution.py:25
  141.6 8.2 %collective-permute-done.35.got = bf16[320,384]{1,0:T(8,128)(2,1)S(1)} collective-permute-done((bf16[320,384]{1,0:T(8,128)(2,1)S(1)}, bf16[320,384]{1,0:T(8,128)(2,1)S(1)}, u32[]{:S(2)}, u32[]{:S(2)}) %collective-permute-start.35) | collective-permute-done | bytes 245792 | tf_op jit(solution)/shard_map/ppermute | solution.py:25
  155.2 6.1 %collective-permute-done.42.across = bf16[480,768]{1,0:T(8,128)(2,1)S(1)} collective-permute-done((bf16[480,768]{1,0:T(8,128)(2,1)S(1)}, bf16[480,768]{1,0:T(8,128)(2,1)S(1)}, u32[]{:S(2)}, u32[]{:S(2)}) %collective-permute-start.42) | collective-permute-done | bytes 737312 | tf_op jit(solution)/shard_map/ppermute | solution.py:25
  163.5 2.5 %join_body.3 = bf16[2,832,768]{2,1,0:T(8,128)(2,1)} custom-call(s32[2]{0:T(128)S(1)} %pad_add_fusion.info, s32[2,832]{1,0:T(2,128)S(1)} %copy-done.19, bf16[480,768]{1,0:T(8,128)(2,1)S(1)} %get-tuple-element.411.own, bf16[480,768]{1,0:T(8,128)(2,1)S(1)} %collective-permute-done.34.beside, bf16[480,768]{1,0:T(8,128)(2,1)S(1)} %collective-permute-done.42.across, ...), custom_call_target="tpu_custom_call" | custom-call | flops 40000000000 | bytes 60000000 | tf_op jit(solution)/shard_map/join_body/pallas_call | solution.py:59
  (170 shorter events, 66.6 us)
Async XLA Ops:
  8.0 10.7 %collective-permute-start.2 = (bf16[1,160,384]{2,1,0:T(8,128)(2,1)S(1)}, bf16[1,160,384]{2,1,0:T(8,128)(2,1)S(1)}, u32[]{:S(2)}, u32[]{:S(2)}) collective-permute-start(bf16[1,160,384]{2,1,0:T(8,128)(2,1)S(1)} %meet_a_body.1.refs_0_), channel_id=1, source_target_pairs={{0,8},{1,9},{2,10},{3,11},{4,12},{5,13},{6,14},{7,15},{8,0},{9,1},... | collective-permute-start | bytes 368648 | tf_op jit(solution)/shard_map/ppermute | solution.py:25
  11.1 12.4 %collective-permute-start.3 = (bf16[1,160,384]{2,1,0:T(8,128)(2,1)S(1)}, bf16[1,160,384]{2,1,0:T(8,128)(2,1)S(1)}, u32[]{:S(2)}, u32[]{:S(2)}) collective-permute-start(bf16[1,160,384]{2,1,0:T(8,128)(2,1)S(1)} %meet_a_body.1.refs_0_), channel_id=1, source_target_pairs={{0,16},{1,17},{2,18},{3,19},{4,20},{5,21},{6,22},{7,23},{8,24},{9,... | collective-permute-start | bytes 368648 | tf_op jit(solution)/shard_map/ppermute | solution.py:25
  13.7 9.8 %collective-permute-start.4 = (bf16[1,160,384]{2,1,0:T(8,128)(2,1)S(1)}, bf16[1,160,384]{2,1,0:T(8,128)(2,1)S(1)}, u32[]{:S(2)}, u32[]{:S(2)}) collective-permute-start(bf16[1,160,384]{2,1,0:T(8,128)(2,1)S(1)} %meet_a_body.1.refs_0_), channel_id=1, source_target_pairs={{0,24},{1,25},{2,26},{3,27},{4,28},{5,29},{6,30},{7,31},{8,16},{9,... | collective-permute-start | bytes 368648 | tf_op jit(solution)/shard_map/ppermute | solution.py:25
  23.6 15.1 %collective-permute-start.10 = (bf16[4,160,384]{2,1,0:T(8,128)(2,1)S(1)}, bf16[4,160,384]{2,1,0:T(8,128)(2,1)S(1)}, u32[]{:S(2)}, u32[]{:S(2)}) collective-permute-start(bf16[4,160,384]{2,1,0:T(8,128)(2,1)S(1)} %stack_body.2.refs_0_), channel_id=1, source_target_pairs={{0,2},{1,3},{2,0},{3,1},{4,6},{5,7},{6,4},{7,5},{8,10},{9,11},{10,... | collective-permute-start | bytes 1474568 | tf_op jit(solution)/shard_map/ppermute | solution.py:25
  25.2 13.5 %collective-permute-start.9 = (bf16[4,160,384]{2,1,0:T(8,128)(2,1)S(1)}, bf16[4,160,384]{2,1,0:T(8,128)(2,1)S(1)}, u32[]{:S(2)}, u32[]{:S(2)}) collective-permute-start(bf16[4,160,384]{2,1,0:T(8,128)(2,1)S(1)} %stack_body.2.refs_0_), channel_id=1, source_target_pairs={{0,4},{1,5},{2,6},{3,7},{4,0},{5,1},{6,2},{7,3},{8,12},{9,13},{10,... | collective-permute-start | bytes 1474568 | tf_op jit(solution)/shard_map/ppermute | solution.py:25
  28.7 9.9 %collective-permute-start.7 = (bf16[1,144,384]{2,1,0:T(8,128)(2,1)S(1)}, bf16[1,144,384]{2,1,0:T(8,128)(2,1)S(1)}, u32[]{:S(2)}, u32[]{:S(2)}) collective-permute-start(bf16[1,144,384]{2,1,0:T(8,128)(2,1)S(1)} %meet_b_body.1.refs_0_), channel_id=1, source_target_pairs={{0,16},{1,17},{2,18},{3,19},{4,20},{5,21},{6,22},{7,23},{8,24},{9,... | collective-permute-start | bytes 331784 | tf_op jit(solution)/shard_map/ppermute | solution.py:25
  29.7 8.9 %collective-permute-start.8 = (bf16[1,144,384]{2,1,0:T(8,128)(2,1)S(1)}, bf16[1,144,384]{2,1,0:T(8,128)(2,1)S(1)}, u32[]{:S(2)}, u32[]{:S(2)}) collective-permute-start(bf16[1,144,384]{2,1,0:T(8,128)(2,1)S(1)} %meet_b_body.1.refs_0_), channel_id=1, source_target_pairs={{0,24},{1,25},{2,26},{3,27},{4,28},{5,29},{6,30},{7,31},{8,16},{9,... | collective-permute-start | bytes 331784 | tf_op jit(solution)/shard_map/ppermute | solution.py:25
  39.2 15.0 %collective-permute-start.14 = (bf16[4,160,384]{2,1,0:T(8,128)(2,1)S(1)}, bf16[4,160,384]{2,1,0:T(8,128)(2,1)S(1)}, u32[]{:S(2)}, u32[]{:S(2)}) collective-permute-start(bf16[4,160,384]{2,1,0:T(8,128)(2,1)S(1)} %stack_body.2.refs_0_), channel_id=1, source_target_pairs={{0,6},{1,7},{2,4},{3,5},{4,2},{5,3},{6,0},{7,1},{8,14},{9,15},{10,... | collective-permute-start | bytes 1474568 | tf_op jit(solution)/shard_map/ppermute | solution.py:25
  43.0 19.8 %collective-permute-start.17 = (bf16[4,144,384]{2,1,0:T(8,128)(2,1)S(1)}, bf16[4,144,384]{2,1,0:T(8,128)(2,1)S(1)}, u32[]{:S(2)}, u32[]{:S(2)}) collective-permute-start(bf16[4,144,384]{2,1,0:T(8,128)(2,1)S(1)} %stack_body.3.refs_0_), channel_id=1, source_target_pairs={{0,4},{1,5},{2,6},{3,7},{4,0},{5,1},{6,2},{7,3},{8,12},{9,13},{10,... | collective-permute-start | bytes 1327112 | tf_op jit(solution)/shard_map/ppermute | solution.py:25
  43.6 20.1 %collective-permute-start.18 = (bf16[4,144,384]{2,1,0:T(8,128)(2,1)S(1)}, bf16[4,144,384]{2,1,0:T(8,128)(2,1)S(1)}, u32[]{:S(2)}, u32[]{:S(2)}) collective-permute-start(bf16[4,144,384]{2,1,0:T(8,128)(2,1)S(1)} %stack_body.3.refs_0_), channel_id=1, source_target_pairs={{0,2},{1,3},{2,0},{3,1},{4,6},{5,7},{6,4},{7,5},{8,10},{9,11},{10,... | collective-permute-start | bytes 1327112 | tf_op jit(solution)/shard_map/ppermute | solution.py:25
  44.5 27.8 %collective-permute-start.21 = (bf16[4,144,384]{2,1,0:T(8,128)(2,1)S(1)}, bf16[4,144,384]{2,1,0:T(8,128)(2,1)S(1)}, u32[]{:S(2)}, u32[]{:S(2)}) collective-permute-start(bf16[4,144,384]{2,1,0:T(8,128)(2,1)S(1)} %stack_body.3.refs_0_), channel_id=1, source_target_pairs={{0,6},{1,7},{2,4},{3,5},{4,2},{5,3},{6,0},{7,1},{8,14},{9,15},{10,... | collective-permute-start | bytes 1327112 | tf_op jit(solution)/shard_map/ppermute | solution.py:25
  63.6 8.7 %collective-permute-start.19 = (bf16[4,144,384]{2,1,0:T(8,128)(2,1)S(1)}, bf16[4,144,384]{2,1,0:T(8,128)(2,1)S(1)}, u32[]{:S(2)}, u32[]{:S(2)}) collective-permute-start(bf16[4,144,384]{2,1,0:T(8,128)(2,1)S(1)} %collective-permute-done.17.refs_2_), channel_id=1, source_target_pairs={{0,1},{1,0},{2,3},{3,2},{4,5},{5,4},{6,7},{7,6},{8,9},{9,8},{10,11... | collective-permute-start | bytes 1327112 | tf_op jit(solution)/shard_map/ppermute | solution.py:25
  79.2 26.6 %collective-permute-start.26 = (bf16[480,768]{1,0:T(8,128)(2,1)S(1)}, bf16[480,768]{1,0:T(8,128)(2,1)S(1)}, u32[]{:S(2)}, u32[]{:S(2)}) collective-permute-start(bf16[480,768]{1,0:T(8,128)(2,1)S(1)} %get-tuple-element.423.own), channel_id=1, source_target_pairs={{0,2},{1,3},{2,0},{3,1},{4,6},{5,7},{6,4},{7,5},{8,10},{9,11},{10,... | collective-permute-start | bytes 2211848 | tf_op jit(solution)/shard_map/ppermute | solution.py:25
  94.7 25.5 %collective-permute-start.29 = (bf16[1184,384]{1,0:T(8,128)(2,1)S(1)}, bf16[1184,384]{1,0:T(8,128)(2,1)S(1)}, u32[]{:S(2)}, u32[]{:S(2)}) collective-permute-start(bf16[1184,384]{1,0:T(8,128)(2,1)S(1)} %get-tuple-element.386), channel_id=1, source_target_pairs={{0,2},{1,3},{2,0},{3,1},{4,6},{5,7},{6,4},{7,5},{8,10},{9,11},{10,... | collective-permute-start | bytes 2727944 | tf_op jit(solution)/shard_map/ppermute | solution.py:25
  113.1 14.5 %collective-permute-start.31 = (bf16[576,384]{1,0:T(8,128)(2,1)S(1)}, bf16[576,384]{1,0:T(8,128)(2,1)S(1)}, u32[]{:S(2)}, u32[]{:S(2)}) collective-permute-start(bf16[576,384]{1,0:T(8,128)(2,1)S(1)} %get-tuple-element.406), channel_id=1, source_target_pairs={{0,2},{1,3},{2,0},{3,1},{4,6},{5,7},{6,4},{7,5},{8,10},{9,11},{10,... | collective-permute-start | bytes 1327112 | tf_op jit(solution)/shard_map/ppermute | solution.py:25
  120.4 12.5 %collective-permute-start.32 = (bf16[608,384]{1,0:T(8,128)(2,1)S(1)}, bf16[608,384]{1,0:T(8,128)(2,1)S(1)}, u32[]{:S(2)}, u32[]{:S(2)}) collective-permute-start(bf16[608,384]{1,0:T(8,128)(2,1)S(1)} %get-tuple-element.409), channel_id=1, source_target_pairs={{0,4},{1,5},{2,6},{3,7},{4,0},{5,1},{6,2},{7,3},{8,12},{9,13},{10,... | collective-permute-start | bytes 1400840 | tf_op jit(solution)/shard_map/ppermute | solution.py:25
  133.4 16.5 %collective-permute-start.37 = (bf16[576,384]{1,0:T(8,128)(2,1)S(1)}, bf16[576,384]{1,0:T(8,128)(2,1)S(1)}, u32[]{:S(2)}, u32[]{:S(2)}) collective-permute-start(bf16[576,384]{1,0:T(8,128)(2,1)S(1)} %get-tuple-element.432), channel_id=1, source_target_pairs={{0,2},{1,3},{2,0},{3,1},{4,6},{5,7},{6,4},{7,5},{8,10},{9,11},{10,... | collective-permute-start | bytes 1327112 | tf_op jit(solution)/shard_map/ppermute | solution.py:25
  134.9 26.3 %collective-permute-start.42 = (bf16[480,768]{1,0:T(8,128)(2,1)S(1)}, bf16[480,768]{1,0:T(8,128)(2,1)S(1)}, u32[]{:S(2)}, u32[]{:S(2)}) collective-permute-start(bf16[480,768]{1,0:T(8,128)(2,1)S(1)} %get-tuple-element.411.own), channel_id=1, source_target_pairs={{0,2},{1,3},{2,0},{3,1},{4,6},{5,7},{6,4},{7,5},{8,10},{9,11},{10,... | collective-permute-start | bytes 2211848 | tf_op jit(solution)/shard_map/ppermute | solution.py:25
  135.9 13.9 %collective-permute-start.35 = (bf16[320,384]{1,0:T(8,128)(2,1)S(1)}, bf16[320,384]{1,0:T(8,128)(2,1)S(1)}, u32[]{:S(2)}, u32[]{:S(2)}) collective-permute-start(bf16[320,384]{1,0:T(8,128)(2,1)S(1)} %get-tuple-element.422), channel_id=1, source_target_pairs={{0,16},{1,17},{2,18},{3,19},{4,20},{5,21},{6,22},{7,23},{8,24},{9,... | collective-permute-start | bytes 737288 | tf_op jit(solution)/shard_map/ppermute | solution.py:25
  138.6 11.9 %collective-permute-start.36 = (bf16[592,384]{1,0:T(8,128)(2,1)S(1)}, bf16[592,384]{1,0:T(8,128)(2,1)S(1)}, u32[]{:S(2)}, u32[]{:S(2)}) collective-permute-start(bf16[592,384]{1,0:T(8,128)(2,1)S(1)} %get-tuple-element.431), channel_id=1, source_target_pairs={{0,4},{1,5},{2,6},{3,7},{4,0},{5,1},{6,2},{7,3},{8,12},{9,13},{10,... | collective-permute-start | bytes 1363976 | tf_op jit(solution)/shard_map/ppermute | solution.py:25
  150.7 10.6 %collective-permute-start.41 = (bf16[176,384]{1,0:T(8,128)(2,1)S(1)}, bf16[176,384]{1,0:T(8,128)(2,1)S(1)}, u32[]{:S(2)}, u32[]{:S(2)}) collective-permute-start(bf16[176,384]{1,0:T(8,128)(2,1)S(1)} %get-tuple-element.450), channel_id=1, source_target_pairs={{0,8},{1,9},{2,10},{3,11},{4,12},{5,13},{6,14},{7,15},{8,0},{9,1},... | collective-permute-start | bytes 405512 | tf_op jit(solution)/shard_map/ppermute | solution.py:25
  150.8 16.6 %collective-permute-start.38 = (bf16[160,384]{1,0:T(8,128)(2,1)S(1)}, bf16[160,384]{1,0:T(8,128)(2,1)S(1)}, u32[]{:S(2)}, u32[]{:S(2)}) collective-permute-start(bf16[160,384]{1,0:T(8,128)(2,1)S(1)} %get-tuple-element.445), channel_id=1, source_target_pairs={{0,8},{1,9},{2,10},{3,11},{4,12},{5,13},{6,14},{7,15},{8,0},{9,1},... | collective-permute-start | bytes 368648 | tf_op jit(solution)/shard_map/ppermute | solution.py:25
  152.8 14.6 %collective-permute-start.39 = (bf16[160,384]{1,0:T(8,128)(2,1)S(1)}, bf16[160,384]{1,0:T(8,128)(2,1)S(1)}, u32[]{:S(2)}, u32[]{:S(2)}) collective-permute-start(bf16[160,384]{1,0:T(8,128)(2,1)S(1)} %get-tuple-element.446), channel_id=1, source_target_pairs={{0,16},{1,17},{2,18},{3,19},{4,20},{5,21},{6,22},{7,23},{8,24},{9,... | collective-permute-start | bytes 368648 | tf_op jit(solution)/shard_map/ppermute | solution.py:25
  153.1 14.3 %collective-permute-start.40 = (bf16[160,384]{1,0:T(8,128)(2,1)S(1)}, bf16[160,384]{1,0:T(8,128)(2,1)S(1)}, u32[]{:S(2)}, u32[]{:S(2)}) collective-permute-start(bf16[160,384]{1,0:T(8,128)(2,1)S(1)} %get-tuple-element.447), channel_id=1, source_target_pairs={{0,24},{1,25},{2,26},{3,27},{4,28},{5,29},{6,30},{7,31},{8,16},{9,... | collective-permute-start | bytes 368648 | tf_op jit(solution)/shard_map/ppermute | solution.py:25
  (43 other events, 237.9 us)

commit v2 on v1

--- a/solution.py
+++ b/solution.py
@@ -250,7 +250,7 @@
     lax.fori_loop(0, heads // 4, four, 0)
 
 
-def feed_body(places, high, x_r, o00, o01, o10, o11, small, cols0, cols1, target, *refs):
+def feed_body(places, high, x_r, o00, o01, o1, small, cols0, cols1, target, *refs):
     count = len(places)
     blocks = refs[: 2 * count]
     refs = refs[2 * count :]
@@ -258,8 +258,8 @@
     atts, acts, slopes, weights = refs[4:6], refs[6:8], refs[8:10], refs[10:]
     for yr in range(2):
         assemble(blocks[yr * count : (yr + 1) * count], places, high, weights[yr])
-    for out, a, b in zip(atts, (o00, o10), (o01, o11)):
-        out[...] = jnp.concatenate([flat_heads(a[...]), flat_heads(b[...])], axis=0).T.astype(BF16)
+    atts[0][...] = jnp.concatenate([flat_heads(o00[...]), flat_heads(o01[...])], axis=0).T.astype(BF16)
+    atts[1][...] = flat_heads(o1[...]).T.astype(BF16)
     x = x_r[...].astype(F32)
     middle = x + dot_nt(atts[0][...], weights[0][0]) + dot_nt(atts[1][...], weights[1][0]) + small[2:3]
     xhat, inverse = norm_parts(middle)
@@ -331,27 +331,27 @@
         (d0, d1)[yr][...] = by_head(dot_nn(low, weights[yr][0]))
 
 
-def backward_body(first, qt, kt, vt, dt, ot, lse, bias, dq_o, dk_o, dv_o, dq, dk, dv):
-    heads, _, window = ot.shape
+def backward_body(first, mixed, qt, kt, vt, dt, ot, lse, bias, dq_o, dk_o, dv_o, dq, dk, dv):
+    heads, _, window = dq.shape
     made = tiles(window)
 
     def head(i, carry):
         h = first + i
-        delta = jnp.sum(dt[h].astype(F32) * ot[i], axis=0, keepdims=True)
+        delta = jnp.sum(dt[h].astype(F32) * ot[mixed + i], axis=0, keepdims=True)
         for ref in (dk, dv):
             ref[i] = jnp.zeros_like(ref[i])
         for q0, qn, k0, k1 in made:
             query, grad = qt[h, :, q0 : q0 + qn], dt[h, :, q0 : q0 + qn]
             scores = dot_tn(kt[h, :, k0:k1], query)
             dprobs = dot_tn(vt[h, :, k0:k1], grad)
-            probs = jnp.exp2(scores * LOG2 + (bias[k0:k1, q0 : q0 + qn] - lse[i, :, q0 : q0 + qn]))
+            probs = jnp.exp2(scores * LOG2 + (bias[k0:k1, q0 : q0 + qn] - lse[mixed + i, :, q0 : q0 + qn]))
             dscores = (probs * (dprobs - delta[:, q0 : q0 + qn])).astype(BF16)
             dq[i, :, q0 : q0 + qn] = dot_nn(kt[h, :, k0:k1], dscores)
             dk[i, :, k0:k1] += dot_nt(query, dscores)
             dv[i, :, k0:k1] += dot_nt(grad, probs.astype(BF16))
         return carry
 
-    lax.fori_loop(0, heads, head, 0, unroll=1)
+    lax.fori_loop(0, heads, head, 0, unroll=2)
     for ref, out, factor in ((dq, dq_o, SCALE), (dk, dk_o, SCALE), (dv, dv_o, 1.0)):
         out[...] = (flat_heads(ref[...]) * factor).astype(BF16)
 
@@ -691,9 +691,10 @@
         )
 
     def attend(part, qkv_heads, bias):
+        first, count = (0, heads) if part is None else (part * (heads // 2), heads // 2)
         return call(
-            functools.partial(forward_body, part * (heads // 2)),
-            [(by_few, F32), ((heads // 2, 1, window), F32)],
+            functools.partial(forward_body, first),
+            [((count, PAD, window), F32), ((count, 1, window), F32)],
             list(qkv_heads) + [bias],
             us=5,
         )
@@ -728,7 +729,7 @@
 
     def backward(part, qkv_heads, da, o, lse, bias):
         return call(
-            functools.partial(backward_body, part * (heads // 2)),
+            functools.partial(backward_body, part * (heads // 2), part * (heads // 2) if o.shape[0] == heads else 0),
             [((heads // 2 * HD, window), BF16)] * 3,
             list(qkv_heads) + [da, o, lse, bias],
             [pltpu.VMEM(by_few, F32)] * 3,
@@ -785,8 +786,8 @@
         *heads0, _, _, normed, normed_t = project(xhat, [wa[0]], True, (small, units[0]))
         *heads1, _ = project(normed, [wa[1]], False, (small, units[1]))
         both = (heads0, heads1)
-        mixed = [attend(part, both[yr], bias) for yr in range(2) for part in range(2)]
-        made = feed(x, [o for o, _ in mixed], small, units, target, wb)
+        mixed = [attend(0, heads0, bias), attend(1, heads0, bias)] + [attend(None, heads1, bias)] * 2
+        made = feed(x, [o for o, _ in mixed[:3]], small, units, target, wb)
         result = made[0]
         none = jnp.zeros_like(side)
         dmiddle, da0, da1, sums_b, grads_b = feed_back(none, ct, made[1:], small, target, wb)
@@ -868,15 +869,14 @@
         o01, qkv_xyc, odu_c, normed = fence(o01, qkv_xyc, odu_c, normed)
         far = [qkv_y, qkv_yc, qkv_xy, qkv_xyc]
         *heads1, shift1u = project(normed, far, False)
-        o10, l10 = attend(0, heads1, bias)
-        o10, heads1, odu_x, odu_y = fence(o10, heads1, odu_x, odu_y)
+        o1, l1 = attend(None, heads1, bias)
+        o1, odu_x, odu_y = fence(o1, odu_x, odu_y)
         odu_xc, odu_yc = to(odu_x, 0, 1), to(odu_y, 0, 1)
-        o11, l11 = attend(1, heads1, bias)
-        o11, odu_xc, odu_yc, odu_xy = fence(o11, odu_xc, odu_yc, odu_xy)
+        o1, odu_xc, odu_yc, odu_xy = fence(o1, odu_xc, odu_yc, odu_xy)
         odu_xyc = to(odu_xy, 0, 1)
 
         odu_blocks = [odu, odu_c, odu_x, odu_xc, odu_y, odu_yc, odu_xy, odu_xyc]
-        made = fence(*feed(x, [o00, o01, o10, o11], small, [shift0, shift1u], target, odu_blocks))
+        made = fence(*feed(x, [o00, o01, o1], small, [shift0, shift1u], target, odu_blocks))
         result = made[0]
         res_c, res_y = to(result, 0, 1), to(result, 0, 2)
         made = feed_back(side, ct, made[1:], small, target, odu_blocks)
@@ -885,7 +885,7 @@
         n_far, n_near = 2 * deep * 3 * half, deep * 3 * half
         f32_16, f32_8 = ((16, cols), F32), ((8, cols), F32)
         b_got, b_sums_got = to(b_send, 0, 1), to(b_sums, 0, 1)
-        low10 = backward(0, heads1, da1, o10, l10, bias)
+        low10 = backward(0, heads1, da1, o1, l1, bias)
         low10, heads1, b_got, b_sums_got = fence(low10, heads1, b_got, b_sums_got)
         b_far, b_sums = call(
             far_b_body,
@@ -893,7 +893,7 @@
             [b_keep, b_got, b_sums, b_sums_got],
         )
         b_far = to(b_far, 0, 2)
-        low11 = backward(1, heads1, da1, o11, l11, bias)
+        low11 = backward(1, heads1, da1, o1, l1, bias)
         low11, normed_t = fence(low11, normed_t)
         dn1, qv1, keep1, send1 = weigh(normed_t, far, low10, low11)
         dn1, keep1, send1, da0, res_y = fence(dn1, keep1, send1, da0, res_y)

time: 175 us -> 173 us (0.989)
  Pallas kernels: 75.6 us -> 73.3 us
    pallas_call x34 -> x33, Pallas kernels: 75.6 us -> 73.3 us  [call(): pl.pallas_call(body, out_shape=tuple((jax.ShapeDtypeStruct(s, d) for s, d...]
  transfers between devices with their start and end apart: 47 -> 47, of which waited for: 16 -> 16; matrix products, arithmetic and copies ran while one was open for 3% -> 3% of each run, Pallas kernels for 39% -> 38%
where the time goes in v2:
time: 173 us; the launch traced here: 172 us
  Pallas kernels  73.3 us (42%)
  waiting for transfers between devices  47.9 us (28%)
  starting transfers between devices  36.7 us (21%)
  local copies, waits for them, and re-layouts  12.9 us (7%)
    pallas_call x33, Pallas kernels, call(): pl.pallas_call(body, out_shape=tuple((jax.ShapeDtypeStruct(s, d) for s, d...  73.3 us
    ppermute x47, waiting for transfers between devices, send(): return lax.ppermute(value, BOTH, pairs)  47.9 us
    ppermute x47, starting transfers between devices, send(): return lax.ppermute(value, BOTH, pairs)  36.7 us
    unnamed x42, local copies, waits for them, and re-layouts  6.48 us
  transfers between devices with their start and end apart: 47, of which 16 were waited for; matrix products, arithmetic and copies ran while one was open for 3% of the time, Pallas kernels for 38%

profile of v2, /device:TPU:0, one launch (start us, length us, event | category | flops | bytes accessed | tf_op | source)
XLA Modules:
  0.0 172.2 jit_solution(11319244249821017500)
XLA Ops:
  8.0 3.1 %collective-permute-start.2 = (bf16[1,160,384]{2,1,0:T(8,128)(2,1)S(1)}, bf16[1,160,384]{2,1,0:T(8,128)(2,1)S(1)}, u32[]{:S(2)}, u32[]{:S(2)}) collective-permute-start(bf16[1,160,384]{2,1,0:T(8,128)(2,1)S(1)} %meet_a_body.1.refs_0_), channel_id=1, source_target_pairs={{0,8},{1,9},{2,10},{3,11},{4,12},{5,13},{6,14},{7,15},{8,0},{9,1},... | collective-permute-start | bytes 368648 | tf_op jit(solution)/shard_map/ppermute | solution.py:25
  11.1 2.6 %collective-permute-start.3 = (bf16[1,160,384]{2,1,0:T(8,128)(2,1)S(1)}, bf16[1,160,384]{2,1,0:T(8,128)(2,1)S(1)}, u32[]{:S(2)}, u32[]{:S(2)}) collective-permute-start(bf16[1,160,384]{2,1,0:T(8,128)(2,1)S(1)} %meet_a_body.1.refs_0_), channel_id=1, source_target_pairs={{0,16},{1,17},{2,18},{3,19},{4,20},{5,21},{6,22},{7,23},{8,24},{9,... | collective-permute-start | bytes 368648 | tf_op jit(solution)/shard_map/ppermute | solution.py:25
  18.8 4.8 %collective-permute-done.3.refs_2_ = bf16[1,160,384]{2,1,0:T(8,128)(2,1)S(1)} collective-permute-done((bf16[1,160,384]{2,1,0:T(8,128)(2,1)S(1)}, bf16[1,160,384]{2,1,0:T(8,128)(2,1)S(1)}, u32[]{:S(2)}, u32[]{:S(2)}) %collective-permute-start.3) | collective-permute-done | bytes 122912 | tf_op jit(solution)/shard_map/ppermute | solution.py:25
  35.0 3.6 %collective-permute-done.7.refs_2_ = bf16[1,144,384]{2,1,0:T(8,128)(2,1)S(1)} collective-permute-done((bf16[1,144,384]{2,1,0:T(8,128)(2,1)S(1)}, bf16[1,144,384]{2,1,0:T(8,128)(2,1)S(1)}, u32[]{:S(2)}, u32[]{:S(2)}) %collective-permute-start.7) | collective-permute-done | bytes 110624 | tf_op jit(solution)/shard_map/ppermute | solution.py:25
  46.5 2.8 %forward_body.3 = (f32[8,32,480]{2,1,0:T(8,128)S(1)}, f32[8,1,480]{2,1,0:T(1,128)S(1)}) custom-call(bf16[16,32,480]{2,1,0:T(8,128)(2,1)S(1)} %get-tuple-element.366.qt, bf16[16,32,480]{2,1,0:T(8,128)(2,1)S(1)} %get-tuple-element.367.kt, bf16[16,32,480]{2,1,0:T(8,128)(2,1)S(1)} %get-tuple-element.368.vt, f32[480,512]{1,0:T(8,128)S(1)} %get-tuple-element.278.bias), custom_call_target="tpu_custom_call" | custom-call | flops 10000000000 | bytes 15000000 | tf_op jit(solution)/shard_map/forward_body/pallas_call | solution.py:59
  49.3 4.9 %collective-permute-done.14.refs_2_ = bf16[4,160,384]{2,1,0:T(8,128)(2,1)S(1)} collective-permute-done((bf16[4,160,384]{2,1,0:T(8,128)(2,1)S(1)}, bf16[4,160,384]{2,1,0:T(8,128)(2,1)S(1)}, u32[]{:S(2)}, u32[]{:S(2)}) %collective-permute-start.14) | collective-permute-done | bytes 491552 | tf_op jit(solution)/shard_map/ppermute | solution.py:25
  54.8 2.8 %forward_body.4 = (f32[8,32,480]{2,1,0:T(8,128)S(1)}, f32[8,1,480]{2,1,0:T(1,128)S(1)}) custom-call(bf16[16,32,480]{2,1,0:T(8,128)(2,1)S(1)} %get-tuple-element.366.qt, bf16[16,32,480]{2,1,0:T(8,128)(2,1)S(1)} %get-tuple-element.367.kt, bf16[16,32,480]{2,1,0:T(8,128)(2,1)S(1)} %get-tuple-element.368.vt, f32[480,512]{1,0:T(8,128)S(1)} %get-tuple-element.278.bias), custom_call_target="tpu_custom_call" | custom-call | flops 10000000000 | bytes 15000000 | tf_op jit(solution)/shard_map/forward_body/pallas_call | solution.py:59
  59.1 5.8 %forward_body.5 = (f32[16,32,480]{2,1,0:T(8,128)S(1)}, f32[16,1,480]{2,1,0:T(1,128)S(1)}) custom-call(bf16[16,32,480]{2,1,0:T(8,128)(2,1)S(1)} %get-tuple-element.334.qt, bf16[16,32,480]{2,1,0:T(8,128)(2,1)S(1)} %get-tuple-element.335.kt, bf16[16,32,480]{2,1,0:T(8,128)(2,1)S(1)} %get-tuple-element.336.vt, f32[480,512]{1,0:T(8,128)S(1)} %get-tuple-element.278.bias), custom_call_target="tpu_custom_call" | custom-call | flops 10000000000 | bytes 15000000 | tf_op jit(solution)/shard_map/forward_body/pallas_call | solution.py:59
  65.5 6.8 %collective-permute-done.21.refs_6_ = bf16[4,144,384]{2,1,0:T(8,128)(2,1)S(1)} collective-permute-done((bf16[4,144,384]{2,1,0:T(8,128)(2,1)S(1)}, bf16[4,144,384]{2,1,0:T(8,128)(2,1)S(1)}, u32[]{:S(2)}, u32[]{:S(2)}) %collective-permute-start.21) | collective-permute-done | bytes 442400 | tf_op jit(solution)/shard_map/ppermute | solution.py:25
  74.1 4.9 %feed_body.1 = (bf16[480,768]{1,0:T(8,128)(2,1)S(1)}, f32[480,768]{1,0:T(8,128)S(1)}, f32[480,1]{1,0:T(8,128)S(1)}, bf16[480,768]{1,0:T(8,128)(2,1)S(1)}, bf16[4...) custom-call(bf16[480,768]{1,0:T(8,128)(2,1)S(1)} %get-tuple-element., ...), custom_call_target="tpu_custom_call" | custom-call | flops 10000000000 | bytes 15000000 | tf_op jit(solution)/shard_map/feed_body/pallas_call | solution.py:59
  79.7 6.8 %feed_back_body.1 = (f32[480,768]{1,0:T(8,128)S(1)}, bf16[16,32,480]{2,1,0:T(8,128)(2,1)S(1)}, bf16[16,32,480]{2,1,0:T(8,128)(2,1)S(1)}, f32[16,384]{1,0:T(8,128...) custom-call(s32[2]{0:T(128)S(1)} %pad_add_fusion.info, ...), custom_call_target="tpu_custom_call" | custom-call | flops 14000000000 | bytes 21000000 | tf_op jit(solution)/shard_map/feed_back_body/pallas_call | solution.py:59
  87.9 6.0 %backward_body.4 = (bf16[192,480]{1,0:T(8,128)(2,1)S(1)}, bf16[192,480]{1,0:T(8,128)(2,1)S(1)}, bf16[192,480]{1,0:T(8,128)(2,1)S(1)}) custom-call(bf16[16,32,480]{2,1,0:T(8,128)(2,1)S(1)} %get-tuple-element.334.qt, bf16[16,32,480]{2,1,0:T(8,128)(2,1)S(1)} %get-tuple-element.335.kt, bf16[16,32,480]{2,1,0:T(8,128)(2,1)S(1)} %get-tuple-element.336.vt, ...), custom_call_target="tpu_custom_call" | custom-call | flops 30000001024 | bytes 45000000 | tf_op jit(solution)/shard_map/backward_body/pallas_call | solution.py:59
  95.7 6.0 %backward_body.5 = (bf16[192,480]{1,0:T(8,128)(2,1)S(1)}, bf16[192,480]{1,0:T(8,128)(2,1)S(1)}, bf16[192,480]{1,0:T(8,128)(2,1)S(1)}) custom-call(bf16[16,32,480]{2,1,0:T(8,128)(2,1)S(1)} %get-tuple-element.334.qt, bf16[16,32,480]{2,1,0:T(8,128)(2,1)S(1)} %get-tuple-element.335.kt, bf16[16,32,480]{2,1,0:T(8,128)(2,1)S(1)} %get-tuple-element.336.vt, ...), custom_call_target="tpu_custom_call" | custom-call | flops 30000001024 | bytes 45000000 | tf_op jit(solution)/shard_map/backward_body/pallas_call | solution.py:59
  101.7 2.8 %weigh_body.2 = (f32[768,480]{1,0:T(8,128)S(1)}, f32[2,384]{1,0:T(2,128)S(1)}, bf16[2,4,144,384]{3,2,1,0:T(8,128)(2,1)S(1)}, bf16[2,4,144,384]{3,2,1,0:T(8,128)(2,1)S(1)}) custom-call(bf16[768,480]{1,0:T(8,128)(2,1)S(1)} %get-tuple-element.377.nt_r, bf16[192,480]{1,0:T(8,128)(2,1)S(1)} %get-tuple-element.342.qa, bf16[192,480]{1,0:T(8,128)(2,1)S(1)} %get-tuple-element.343.ka, ...), custom_call_target="tpu_custom_call" | custom-call | flops 200000000 | bytes 300000 | tf_op jit(solution)/shard_map/weigh_body/pallas_call | solution.py:59
  105.1 6.0 %backward_body.6 = (bf16[192,480]{1,0:T(8,128)(2,1)S(1)}, bf16[192,480]{1,0:T(8,128)(2,1)S(1)}, bf16[192,480]{1,0:T(8,128)(2,1)S(1)}) custom-call(bf16[16,32,480]{2,1,0:T(8,128)(2,1)S(1)} %get-tuple-element.366.qt, bf16[16,32,480]{2,1,0:T(8,128)(2,1)S(1)} %get-tuple-element.367.kt, bf16[16,32,480]{2,1,0:T(8,128)(2,1)S(1)} %get-tuple-element.368.vt, ...), custom_call_target="tpu_custom_call" | custom-call | flops 30000001024 | bytes 45000000 | tf_op jit(solution)/shard_map/backward_body/pallas_call | solution.py:59
  111.9 6.0 %backward_body.7 = (bf16[192,480]{1,0:T(8,128)(2,1)S(1)}, bf16[192,480]{1,0:T(8,128)(2,1)S(1)}, bf16[192,480]{1,0:T(8,128)(2,1)S(1)}) custom-call(bf16[16,32,480]{2,1,0:T(8,128)(2,1)S(1)} %get-tuple-element.366.qt, bf16[16,32,480]{2,1,0:T(8,128)(2,1)S(1)} %get-tuple-element.367.kt, bf16[16,32,480]{2,1,0:T(8,128)(2,1)S(1)} %get-tuple-element.368.vt, ...), custom_call_target="tpu_custom_call" | custom-call | flops 30000001024 | bytes 45000000 | tf_op jit(solution)/shard_map/backward_body/pallas_call | solution.py:59
  119.5 2.8 %weigh_body.3 = (f32[768,480]{1,0:T(8,128)S(1)}, f32[2,384]{1,0:T(2,128)S(1)}, bf16[2,4,144,384]{3,2,1,0:T(8,128)(2,1)S(1)}, bf16[2,4,144,384]{3,2,1,0:T(8,128)(2,1)S(1)}) custom-call(bf16[768,480]{1,0:T(8,128)(2,1)S(1)} %get-tuple-element.377.nt_r, bf16[192,480]{1,0:T(8,128)(2,1)S(1)} %get-tuple-element.378.qa, bf16[192,480]{1,0:T(8,128)(2,1)S(1)} %get-tuple-element.379.ka, ...), custom_call_target="tpu_custom_call" | custom-call | flops 200000000 | bytes 300000 | tf_op jit(solution)/shard_map/weigh_body/pallas_call | solution.py:59
  122.4 3.0 %finish_body.1 = (bf16[480,768]{1,0:T(8,128)(2,1)S(1)}, f32[8,384]{1,0:T(8,128)S(1)}) custom-call(s32[2]{0:T(128)S(1)} %pad_add_fusion.info, f32[768,480]{1,0:T(8,128)S(1)} %get-tuple-element.388.dn0, f32[768,480]{1,0:T(8,128)S(1)} %get-tuple-element.389.dn1, bf16[480,768]{1,0:T(8,128)(2,1)S(1)} %get-tuple-element.296.x_r, ...), custom_call_target="tpu_custom_call" | custom-call | flops 40000000000 | bytes 60000000 | tf_op jit(solution)/shard_map/finish_body/pallas_call | solution.py:59
  127.0 3.6 %collective-permute-done.32.passed = bf16[608,384]{1,0:T(8,128)(2,1)S(1)} collective-permute-done((bf16[608,384]{1,0:T(8,128)(2,1)S(1)}, bf16[608,384]{1,0:T(8,128)(2,1)S(1)}, u32[]{:S(2)}, u32[]{:S(2)}) %collective-permute-start.32) | collective-permute-done | bytes 466976 | tf_op jit(solution)/shard_map/ppermute | solution.py:25
  133.6 2.7 %collective-permute-start.35 = (bf16[320,384]{1,0:T(8,128)(2,1)S(1)}, bf16[320,384]{1,0:T(8,128)(2,1)S(1)}, u32[]{:S(2)}, u32[]{:S(2)}) collective-permute-start(bf16[320,384]{1,0:T(8,128)(2,1)S(1)} %get-tuple-element.412), channel_id=1, source_target_pairs={{0,16},{1,17},{2,18},{3,19},{4,20},{5,21},{6,22},{7,23},{8,24},{9,... | collective-permute-start | bytes 737288 | tf_op jit(solution)/shard_map/ppermute | solution.py:25
  136.8 2.5 %join_body.2 = bf16[2,832,768]{2,1,0:T(8,128)(2,1)} custom-call(s32[2]{0:T(128)S(1)} %pad_add_fusion.info, s32[2,832]{1,0:T(2,128)S(1)} %copy-done.18, bf16[480,768]{1,0:T(8,128)(2,1)S(1)} %get-tuple-element.413.own, bf16[480,768]{1,0:T(8,128)(2,1)S(1)} %copy-done.13, bf16[480,768]{1,0:T(8,128)(2,1)S(1)} %collective-permute-done.26.across, ...), custom_call_target="tpu_custom_call" | custom-call | flops 40000000000 | bytes 60000000 | tf_op jit(solution)/shard_map/join_body/pallas_call | solution.py:59
  139.3 8.2 %collective-permute-done.35.got = bf16[320,384]{1,0:T(8,128)(2,1)S(1)} collective-permute-done((bf16[320,384]{1,0:T(8,128)(2,1)S(1)}, bf16[320,384]{1,0:T(8,128)(2,1)S(1)}, u32[]{:S(2)}, u32[]{:S(2)}) %collective-permute-start.35) | collective-permute-done | bytes 245792 | tf_op jit(solution)/shard_map/ppermute | solution.py:25
  152.9 6.0 %collective-permute-done.42.across = bf16[480,768]{1,0:T(8,128)(2,1)S(1)} collective-permute-done((bf16[480,768]{1,0:T(8,128)(2,1)S(1)}, bf16[480,768]{1,0:T(8,128)(2,1)S(1)}, u32[]{:S(2)}, u32[]{:S(2)}) %collective-permute-start.42) | collective-permute-done | bytes 737312 | tf_op jit(solution)/shard_map/ppermute | solution.py:25
  161.2 2.5 %join_body.3 = bf16[2,832,768]{2,1,0:T(8,128)(2,1)} custom-call(s32[2]{0:T(128)S(1)} %pad_add_fusion.info, s32[2,832]{1,0:T(2,128)S(1)} %copy-done.19, bf16[480,768]{1,0:T(8,128)(2,1)S(1)} %get-tuple-element.401.own, bf16[480,768]{1,0:T(8,128)(2,1)S(1)} %collective-permute-done.34.beside, bf16[480,768]{1,0:T(8,128)(2,1)S(1)} %collective-permute-done.42.across, ...), custom_call_target="tpu_custom_call" | custom-call | flops 40000000000 | bytes 60000000 | tf_op jit(solution)/shard_map/join_body/pallas_call | solution.py:59
  (169 shorter events, 64.2 us)
Async XLA Ops:
  8.0 10.7 %collective-permute-start.2 = (bf16[1,160,384]{2,1,0:T(8,128)(2,1)S(1)}, bf16[1,160,384]{2,1,0:T(8,128)(2,1)S(1)}, u32[]{:S(2)}, u32[]{:S(2)}) collective-permute-start(bf16[1,160,384]{2,1,0:T(8,128)(2,1)S(1)} %meet_a_body.1.refs_0_), channel_id=1, source_target_pairs={{0,8},{1,9},{2,10},{3,11},{4,12},{5,13},{6,14},{7,15},{8,0},{9,1},... | collective-permute-start | bytes 368648 | tf_op jit(solution)/shard_map/ppermute | solution.py:25
  11.1 12.4 %collective-permute-start.3 = (bf16[1,160,384]{2,1,0:T(8,128)(2,1)S(1)}, bf16[1,160,384]{2,1,0:T(8,128)(2,1)S(1)}, u32[]{:S(2)}, u32[]{:S(2)}) collective-permute-start(bf16[1,160,384]{2,1,0:T(8,128)(2,1)S(1)} %meet_a_body.1.refs_0_), channel_id=1, source_target_pairs={{0,16},{1,17},{2,18},{3,19},{4,20},{5,21},{6,22},{7,23},{8,24},{9,... | collective-permute-start | bytes 368648 | tf_op jit(solution)/shard_map/ppermute | solution.py:25
  13.7 9.8 %collective-permute-start.4 = (bf16[1,160,384]{2,1,0:T(8,128)(2,1)S(1)}, bf16[1,160,384]{2,1,0:T(8,128)(2,1)S(1)}, u32[]{:S(2)}, u32[]{:S(2)}) collective-permute-start(bf16[1,160,384]{2,1,0:T(8,128)(2,1)S(1)} %meet_a_body.1.refs_0_), channel_id=1, source_target_pairs={{0,24},{1,25},{2,26},{3,27},{4,28},{5,29},{6,30},{7,31},{8,16},{9,... | collective-permute-start | bytes 368648 | tf_op jit(solution)/shard_map/ppermute | solution.py:25
  23.6 15.1 %collective-permute-start.10 = (bf16[4,160,384]{2,1,0:T(8,128)(2,1)S(1)}, bf16[4,160,384]{2,1,0:T(8,128)(2,1)S(1)}, u32[]{:S(2)}, u32[]{:S(2)}) collective-permute-start(bf16[4,160,384]{2,1,0:T(8,128)(2,1)S(1)} %stack_body.2.refs_0_), channel_id=1, source_target_pairs={{0,2},{1,3},{2,0},{3,1},{4,6},{5,7},{6,4},{7,5},{8,10},{9,11},{10,... | collective-permute-start | bytes 1474568 | tf_op jit(solution)/shard_map/ppermute | solution.py:25
  25.2 13.5 %collective-permute-start.9 = (bf16[4,160,384]{2,1,0:T(8,128)(2,1)S(1)}, bf16[4,160,384]{2,1,0:T(8,128)(2,1)S(1)}, u32[]{:S(2)}, u32[]{:S(2)}) collective-permute-start(bf16[4,160,384]{2,1,0:T(8,128)(2,1)S(1)} %stack_body.2.refs_0_), channel_id=1, source_target_pairs={{0,4},{1,5},{2,6},{3,7},{4,0},{5,1},{6,2},{7,3},{8,12},{9,13},{10,... | collective-permute-start | bytes 1474568 | tf_op jit(solution)/shard_map/ppermute | solution.py:25
  26.6 8.4 %collective-permute-start.6 = (bf16[1,144,384]{2,1,0:T(8,128)(2,1)S(1)}, bf16[1,144,384]{2,1,0:T(8,128)(2,1)S(1)}, u32[]{:S(2)}, u32[]{:S(2)}) collective-permute-start(bf16[1,144,384]{2,1,0:T(8,128)(2,1)S(1)} %meet_b_body.1.refs_0_), channel_id=1, source_target_pairs={{0,8},{1,9},{2,10},{3,11},{4,12},{5,13},{6,14},{7,15},{8,0},{9,1},... | collective-permute-start | bytes 331784 | tf_op jit(solution)/shard_map/ppermute | solution.py:25
  28.7 9.9 %collective-permute-start.7 = (bf16[1,144,384]{2,1,0:T(8,128)(2,1)S(1)}, bf16[1,144,384]{2,1,0:T(8,128)(2,1)S(1)}, u32[]{:S(2)}, u32[]{:S(2)}) collective-permute-start(bf16[1,144,384]{2,1,0:T(8,128)(2,1)S(1)} %meet_b_body.1.refs_0_), channel_id=1, source_target_pairs={{0,16},{1,17},{2,18},{3,19},{4,20},{5,21},{6,22},{7,23},{8,24},{9,... | collective-permute-start | bytes 331784 | tf_op jit(solution)/shard_map/ppermute | solution.py:25
  29.7 8.9 %collective-permute-start.8 = (bf16[1,144,384]{2,1,0:T(8,128)(2,1)S(1)}, bf16[1,144,384]{2,1,0:T(8,128)(2,1)S(1)}, u32[]{:S(2)}, u32[]{:S(2)}) collective-permute-start(bf16[1,144,384]{2,1,0:T(8,128)(2,1)S(1)} %meet_b_body.1.refs_0_), channel_id=1, source_target_pairs={{0,24},{1,25},{2,26},{3,27},{4,28},{5,29},{6,30},{7,31},{8,16},{9,... | collective-permute-start | bytes 331784 | tf_op jit(solution)/shard_map/ppermute | solution.py:25
  39.2 15.0 %collective-permute-start.14 = (bf16[4,160,384]{2,1,0:T(8,128)(2,1)S(1)}, bf16[4,160,384]{2,1,0:T(8,128)(2,1)S(1)}, u32[]{:S(2)}, u32[]{:S(2)}) collective-permute-start(bf16[4,160,384]{2,1,0:T(8,128)(2,1)S(1)} %stack_body.2.refs_0_), channel_id=1, source_target_pairs={{0,6},{1,7},{2,4},{3,5},{4,2},{5,3},{6,0},{7,1},{8,14},{9,15},{10,... | collective-permute-start | bytes 1474568 | tf_op jit(solution)/shard_map/ppermute | solution.py:25
  43.0 21.9 %collective-permute-start.17 = (bf16[4,144,384]{2,1,0:T(8,128)(2,1)S(1)}, bf16[4,144,384]{2,1,0:T(8,128)(2,1)S(1)}, u32[]{:S(2)}, u32[]{:S(2)}) collective-permute-start(bf16[4,144,384]{2,1,0:T(8,128)(2,1)S(1)} %stack_body.3.refs_0_), channel_id=1, source_target_pairs={{0,4},{1,5},{2,6},{3,7},{4,0},{5,1},{6,2},{7,3},{8,12},{9,13},{10,... | collective-permute-start | bytes 1327112 | tf_op jit(solution)/shard_map/ppermute | solution.py:25
  43.6 21.3 %collective-permute-start.18 = (bf16[4,144,384]{2,1,0:T(8,128)(2,1)S(1)}, bf16[4,144,384]{2,1,0:T(8,128)(2,1)S(1)}, u32[]{:S(2)}, u32[]{:S(2)}) collective-permute-start(bf16[4,144,384]{2,1,0:T(8,128)(2,1)S(1)} %stack_body.3.refs_0_), channel_id=1, source_target_pairs={{0,2},{1,3},{2,0},{3,1},{4,6},{5,7},{6,4},{7,5},{8,10},{9,11},{10,... | collective-permute-start | bytes 1327112 | tf_op jit(solution)/shard_map/ppermute | solution.py:25
  44.5 27.8 %collective-permute-start.21 = (bf16[4,144,384]{2,1,0:T(8,128)(2,1)S(1)}, bf16[4,144,384]{2,1,0:T(8,128)(2,1)S(1)}, u32[]{:S(2)}, u32[]{:S(2)}) collective-permute-start(bf16[4,144,384]{2,1,0:T(8,128)(2,1)S(1)} %stack_body.3.refs_0_), channel_id=1, source_target_pairs={{0,6},{1,7},{2,4},{3,5},{4,2},{5,3},{6,0},{7,1},{8,14},{9,15},{10,... | collective-permute-start | bytes 1327112 | tf_op jit(solution)/shard_map/ppermute | solution.py:25
  79.2 25.3 %collective-permute-start.26 = (bf16[480,768]{1,0:T(8,128)(2,1)S(1)}, bf16[480,768]{1,0:T(8,128)(2,1)S(1)}, u32[]{:S(2)}, u32[]{:S(2)}) collective-permute-start(bf16[480,768]{1,0:T(8,128)(2,1)S(1)} %get-tuple-element.413.own), channel_id=1, source_target_pairs={{0,2},{1,3},{2,0},{3,1},{4,6},{5,7},{6,4},{7,5},{8,10},{9,11},{10,... | collective-permute-start | bytes 2211848 | tf_op jit(solution)/shard_map/ppermute | solution.py:25
  94.1 23.9 %collective-permute-start.29 = (bf16[1184,384]{1,0:T(8,128)(2,1)S(1)}, bf16[1184,384]{1,0:T(8,128)(2,1)S(1)}, u32[]{:S(2)}, u32[]{:S(2)}) collective-permute-start(bf16[1184,384]{1,0:T(8,128)(2,1)S(1)} %get-tuple-element.376), channel_id=1, source_target_pairs={{0,2},{1,3},{2,0},{3,1},{4,6},{5,7},{6,4},{7,5},{8,10},{9,11},{10,... | collective-permute-start | bytes 2727944 | tf_op jit(solution)/shard_map/ppermute | solution.py:25
  111.3 15.7 %collective-permute-start.31 = (bf16[576,384]{1,0:T(8,128)(2,1)S(1)}, bf16[576,384]{1,0:T(8,128)(2,1)S(1)}, u32[]{:S(2)}, u32[]{:S(2)}) collective-permute-start(bf16[576,384]{1,0:T(8,128)(2,1)S(1)} %get-tuple-element.396), channel_id=1, source_target_pairs={{0,2},{1,3},{2,0},{3,1},{4,6},{5,7},{6,4},{7,5},{8,10},{9,11},{10,... | collective-permute-start | bytes 1327112 | tf_op jit(solution)/shard_map/ppermute | solution.py:25
  118.2 12.3 %collective-permute-start.32 = (bf16[608,384]{1,0:T(8,128)(2,1)S(1)}, bf16[608,384]{1,0:T(8,128)(2,1)S(1)}, u32[]{:S(2)}, u32[]{:S(2)}) collective-permute-start(bf16[608,384]{1,0:T(8,128)(2,1)S(1)} %get-tuple-element.399), channel_id=1, source_target_pairs={{0,4},{1,5},{2,6},{3,7},{4,0},{5,1},{6,2},{7,3},{8,12},{9,13},{10,... | collective-permute-start | bytes 1400840 | tf_op jit(solution)/shard_map/ppermute | solution.py:25
  131.1 16.5 %collective-permute-start.37 = (bf16[576,384]{1,0:T(8,128)(2,1)S(1)}, bf16[576,384]{1,0:T(8,128)(2,1)S(1)}, u32[]{:S(2)}, u32[]{:S(2)}) collective-permute-start(bf16[576,384]{1,0:T(8,128)(2,1)S(1)} %get-tuple-element.422), channel_id=1, source_target_pairs={{0,2},{1,3},{2,0},{3,1},{4,6},{5,7},{6,4},{7,5},{8,10},{9,11},{10,... | collective-permute-start | bytes 1327112 | tf_op jit(solution)/shard_map/ppermute | solution.py:25
  132.6 26.4 %collective-permute-start.42 = (bf16[480,768]{1,0:T(8,128)(2,1)S(1)}, bf16[480,768]{1,0:T(8,128)(2,1)S(1)}, u32[]{:S(2)}, u32[]{:S(2)}) collective-permute-start(bf16[480,768]{1,0:T(8,128)(2,1)S(1)} %get-tuple-element.401.own), channel_id=1, source_target_pairs={{0,2},{1,3},{2,0},{3,1},{4,6},{5,7},{6,4},{7,5},{8,10},{9,11},{10,... | collective-permute-start | bytes 2211848 | tf_op jit(solution)/shard_map/ppermute | solution.py:25
  133.6 13.9 %collective-permute-start.35 = (bf16[320,384]{1,0:T(8,128)(2,1)S(1)}, bf16[320,384]{1,0:T(8,128)(2,1)S(1)}, u32[]{:S(2)}, u32[]{:S(2)}) collective-permute-start(bf16[320,384]{1,0:T(8,128)(2,1)S(1)} %get-tuple-element.412), channel_id=1, source_target_pairs={{0,16},{1,17},{2,18},{3,19},{4,20},{5,21},{6,22},{7,23},{8,24},{9,... | collective-permute-start | bytes 737288 | tf_op jit(solution)/shard_map/ppermute | solution.py:25
  136.2 11.9 %collective-permute-start.36 = (bf16[592,384]{1,0:T(8,128)(2,1)S(1)}, bf16[592,384]{1,0:T(8,128)(2,1)S(1)}, u32[]{:S(2)}, u32[]{:S(2)}) collective-permute-start(bf16[592,384]{1,0:T(8,128)(2,1)S(1)} %get-tuple-element.421), channel_id=1, source_target_pairs={{0,4},{1,5},{2,6},{3,7},{4,0},{5,1},{6,2},{7,3},{8,12},{9,13},{10,... | collective-permute-start | bytes 1363976 | tf_op jit(solution)/shard_map/ppermute | solution.py:25
  148.4 10.6 %collective-permute-start.41 = (bf16[176,384]{1,0:T(8,128)(2,1)S(1)}, bf16[176,384]{1,0:T(8,128)(2,1)S(1)}, u32[]{:S(2)}, u32[]{:S(2)}) collective-permute-start(bf16[176,384]{1,0:T(8,128)(2,1)S(1)} %get-tuple-element.440), channel_id=1, source_target_pairs={{0,8},{1,9},{2,10},{3,11},{4,12},{5,13},{6,14},{7,15},{8,0},{9,1},... | collective-permute-start | bytes 405512 | tf_op jit(solution)/shard_map/ppermute | solution.py:25
  148.5 16.6 %collective-permute-start.38 = (bf16[160,384]{1,0:T(8,128)(2,1)S(1)}, bf16[160,384]{1,0:T(8,128)(2,1)S(1)}, u32[]{:S(2)}, u32[]{:S(2)}) collective-permute-start(bf16[160,384]{1,0:T(8,128)(2,1)S(1)} %get-tuple-element.435), channel_id=1, source_target_pairs={{0,8},{1,9},{2,10},{3,11},{4,12},{5,13},{6,14},{7,15},{8,0},{9,1},... | collective-permute-start | bytes 368648 | tf_op jit(solution)/shard_map/ppermute | solution.py:25
  150.5 14.6 %collective-permute-start.39 = (bf16[160,384]{1,0:T(8,128)(2,1)S(1)}, bf16[160,384]{1,0:T(8,128)(2,1)S(1)}, u32[]{:S(2)}, u32[]{:S(2)}) collective-permute-start(bf16[160,384]{1,0:T(8,128)(2,1)S(1)} %get-tuple-element.436), channel_id=1, source_target_pairs={{0,16},{1,17},{2,18},{3,19},{4,20},{5,21},{6,22},{7,23},{8,24},{9,... | collective-permute-start | bytes 368648 | tf_op jit(solution)/shard_map/ppermute | solution.py:25
  150.8 14.2 %collective-permute-start.40 = (bf16[160,384]{1,0:T(8,128)(2,1)S(1)}, bf16[160,384]{1,0:T(8,128)(2,1)S(1)}, u32[]{:S(2)}, u32[]{:S(2)}) collective-permute-start(bf16[160,384]{1,0:T(8,128)(2,1)S(1)} %get-tuple-element.437), channel_id=1, source_target_pairs={{0,24},{1,25},{2,26},{3,27},{4,28},{5,29},{6,30},{7,31},{8,16},{9,... | collective-permute-start | bytes 368648 | tf_op jit(solution)/shard_map/ppermute | solution.py:25
  (43 other events, 233.3 us)

commit v3 on v2

--- a/solution.py
+++ b/solution.py
@@ -833,7 +833,7 @@
         theirs, gain1, b_query, w_query, w_key, w_value = fence(theirs, gain1, b_query, w_query, w_key, w_value)
         mine = jnp.stack([part(w, core) for w in (w_query, w_key, w_value)])
         small = jnp.stack([gain1, shift1, b_out, gain2, shift2, b_down])
-        units = jnp.stack([b_query, b_value, b_up])
+        units = jnp.concatenate([b_query, b_value, b_up]).reshape(3, wc)
         units_pair = to(units, 0, 1)
         feature = lax.iota(jnp.int32, width)
         target = (((feature // half) ^ (f * 2 + core)) * half + feature % half)[None]

time: 173 us -> 171 us (0.988)
  local copies, waits for them, and re-layouts: 12.9 us -> 11 us
    another operation x3 -> x0, local copies, waits for them, and re-layouts: 1.97 us -> none  [per_device(): units = jnp.stack([b_query, b_value, b_up])]
where the time goes in v3:
time: 171 us
  Pallas kernels  73.3 us (43%)
  waiting for transfers between devices  47.9 us (28%)
  starting transfers between devices  36.6 us (21%)
  local copies, waits for them, and re-layouts  11 us (6%)
    pallas_call x33, Pallas kernels, call(): pl.pallas_call(body, out_shape=tuple((jax.ShapeDtypeStruct(s, d) for s, d...  73.3 us
    ppermute x47, waiting for transfers between devices, send(): return lax.ppermute(value, BOTH, pairs)  47.9 us
    ppermute x47, starting transfers between devices, send(): return lax.ppermute(value, BOTH, pairs)  36.6 us
    unnamed x42, local copies, waits for them, and re-layouts  6.48 us
  transfers between devices with their start and end apart: 47, of which 16 were waited for; matrix products, arithmetic and copies ran while one was open for 3% of the time, Pallas kernels for 38%

profile of v3, /device:TPU:0, one launch (start us, length us, event | category | flops | bytes accessed | tf_op | source)
XLA Modules:
  0.0 171.0 jit_solution(916010652992185364)
XLA Ops:
  6.8 3.1 %collective-permute-start.2 = (bf16[1,160,384]{2,1,0:T(8,128)(2,1)S(1)}, bf16[1,160,384]{2,1,0:T(8,128)(2,1)S(1)}, u32[]{:S(2)}, u32[]{:S(2)}) collective-permute-start(bf16[1,160,384]{2,1,0:T(8,128)(2,1)S(1)} %meet_a_body.1.refs_0_), channel_id=1, source_target_pairs={{0,8},{1,9},{2,10},{3,11},{4,12},{5,13},{6,14},{7,15},{8,0},{9,1},... | collective-permute-start | bytes 368648 | tf_op jit(solution)/shard_map/ppermute | solution.py:25
  9.9 2.6 %collective-permute-start.3 = (bf16[1,160,384]{2,1,0:T(8,128)(2,1)S(1)}, bf16[1,160,384]{2,1,0:T(8,128)(2,1)S(1)}, u32[]{:S(2)}, u32[]{:S(2)}) collective-permute-start(bf16[1,160,384]{2,1,0:T(8,128)(2,1)S(1)} %meet_a_body.1.refs_0_), channel_id=1, source_target_pairs={{0,16},{1,17},{2,18},{3,19},{4,20},{5,21},{6,22},{7,23},{8,24},{9,... | collective-permute-start | bytes 368648 | tf_op jit(solution)/shard_map/ppermute | solution.py:25
  17.6 4.8 %collective-permute-done.3.refs_2_ = bf16[1,160,384]{2,1,0:T(8,128)(2,1)S(1)} collective-permute-done((bf16[1,160,384]{2,1,0:T(8,128)(2,1)S(1)}, bf16[1,160,384]{2,1,0:T(8,128)(2,1)S(1)}, u32[]{:S(2)}, u32[]{:S(2)}) %collective-permute-start.3) | collective-permute-done | bytes 122912 | tf_op jit(solution)/shard_map/ppermute | solution.py:25
  33.8 3.6 %collective-permute-done.7.refs_2_ = bf16[1,144,384]{2,1,0:T(8,128)(2,1)S(1)} collective-permute-done((bf16[1,144,384]{2,1,0:T(8,128)(2,1)S(1)}, bf16[1,144,384]{2,1,0:T(8,128)(2,1)S(1)}, u32[]{:S(2)}, u32[]{:S(2)}) %collective-permute-start.7) | collective-permute-done | bytes 110624 | tf_op jit(solution)/shard_map/ppermute | solution.py:25
  45.3 2.8 %forward_body.3 = (f32[8,32,480]{2,1,0:T(8,128)S(1)}, f32[8,1,480]{2,1,0:T(1,128)S(1)}) custom-call(bf16[16,32,480]{2,1,0:T(8,128)(2,1)S(1)} %get-tuple-element.366.qt, bf16[16,32,480]{2,1,0:T(8,128)(2,1)S(1)} %get-tuple-element.367.kt, bf16[16,32,480]{2,1,0:T(8,128)(2,1)S(1)} %get-tuple-element.368.vt, f32[480,512]{1,0:T(8,128)S(1)} %get-tuple-element.278.bias), custom_call_target="tpu_custom_call" | custom-call | flops 10000000000 | bytes 15000000 | tf_op jit(solution)/shard_map/forward_body/pallas_call | solution.py:59
  48.1 4.9 %collective-permute-done.14.refs_2_ = bf16[4,160,384]{2,1,0:T(8,128)(2,1)S(1)} collective-permute-done((bf16[4,160,384]{2,1,0:T(8,128)(2,1)S(1)}, bf16[4,160,384]{2,1,0:T(8,128)(2,1)S(1)}, u32[]{:S(2)}, u32[]{:S(2)}) %collective-permute-start.14) | collective-permute-done | bytes 491552 | tf_op jit(solution)/shard_map/ppermute | solution.py:25
  53.5 2.8 %forward_body.4 = (f32[8,32,480]{2,1,0:T(8,128)S(1)}, f32[8,1,480]{2,1,0:T(1,128)S(1)}) custom-call(bf16[16,32,480]{2,1,0:T(8,128)(2,1)S(1)} %get-tuple-element.366.qt, bf16[16,32,480]{2,1,0:T(8,128)(2,1)S(1)} %get-tuple-element.367.kt, bf16[16,32,480]{2,1,0:T(8,128)(2,1)S(1)} %get-tuple-element.368.vt, f32[480,512]{1,0:T(8,128)S(1)} %get-tuple-element.278.bias), custom_call_target="tpu_custom_call" | custom-call | flops 10000000000 | bytes 15000000 | tf_op jit(solution)/shard_map/forward_body/pallas_call | solution.py:59
  57.9 5.8 %forward_body.5 = (f32[16,32,480]{2,1,0:T(8,128)S(1)}, f32[16,1,480]{2,1,0:T(1,128)S(1)}) custom-call(bf16[16,32,480]{2,1,0:T(8,128)(2,1)S(1)} %get-tuple-element.334.qt, bf16[16,32,480]{2,1,0:T(8,128)(2,1)S(1)} %get-tuple-element.335.kt, bf16[16,32,480]{2,1,0:T(8,128)(2,1)S(1)} %get-tuple-element.336.vt, f32[480,512]{1,0:T(8,128)S(1)} %get-tuple-element.278.bias), custom_call_target="tpu_custom_call" | custom-call | flops 10000000000 | bytes 15000000 | tf_op jit(solution)/shard_map/forward_body/pallas_call | solution.py:59
  64.3 6.8 %collective-permute-done.21.refs_6_ = bf16[4,144,384]{2,1,0:T(8,128)(2,1)S(1)} collective-permute-done((bf16[4,144,384]{2,1,0:T(8,128)(2,1)S(1)}, bf16[4,144,384]{2,1,0:T(8,128)(2,1)S(1)}, u32[]{:S(2)}, u32[]{:S(2)}) %collective-permute-start.21) | collective-permute-done | bytes 442400 | tf_op jit(solution)/shard_map/ppermute | solution.py:25
  72.9 4.9 %feed_body.1 = (bf16[480,768]{1,0:T(8,128)(2,1)S(1)}, f32[480,768]{1,0:T(8,128)S(1)}, f32[480,1]{1,0:T(8,128)S(1)}, bf16[480,768]{1,0:T(8,128)(2,1)S(1)}, bf16[4...) custom-call(bf16[480,768]{1,0:T(8,128)(2,1)S(1)} %get-tuple-element., ...), custom_call_target="tpu_custom_call" | custom-call | flops 10000000000 | bytes 15000000 | tf_op jit(solution)/shard_map/feed_body/pallas_call | solution.py:59
  78.5 6.8 %feed_back_body.1 = (f32[480,768]{1,0:T(8,128)S(1)}, bf16[16,32,480]{2,1,0:T(8,128)(2,1)S(1)}, bf16[16,32,480]{2,1,0:T(8,128)(2,1)S(1)}, f32[16,384]{1,0:T(8,128...) custom-call(s32[2]{0:T(128)S(1)} %pad_add_fusion.info, ...), custom_call_target="tpu_custom_call" | custom-call | flops 14000000000 | bytes 21000000 | tf_op jit(solution)/shard_map/feed_back_body/pallas_call | solution.py:59
  86.7 6.0 %backward_body.4 = (bf16[192,480]{1,0:T(8,128)(2,1)S(1)}, bf16[192,480]{1,0:T(8,128)(2,1)S(1)}, bf16[192,480]{1,0:T(8,128)(2,1)S(1)}) custom-call(bf16[16,32,480]{2,1,0:T(8,128)(2,1)S(1)} %get-tuple-element.334.qt, bf16[16,32,480]{2,1,0:T(8,128)(2,1)S(1)} %get-tuple-element.335.kt, bf16[16,32,480]{2,1,0:T(8,128)(2,1)S(1)} %get-tuple-element.336.vt, ...), custom_call_target="tpu_custom_call" | custom-call | flops 30000001024 | bytes 45000000 | tf_op jit(solution)/shard_map/backward_body/pallas_call | solution.py:59
  94.5 6.0 %backward_body.5 = (bf16[192,480]{1,0:T(8,128)(2,1)S(1)}, bf16[192,480]{1,0:T(8,128)(2,1)S(1)}, bf16[192,480]{1,0:T(8,128)(2,1)S(1)}) custom-call(bf16[16,32,480]{2,1,0:T(8,128)(2,1)S(1)} %get-tuple-element.334.qt, bf16[16,32,480]{2,1,0:T(8,128)(2,1)S(1)} %get-tuple-element.335.kt, bf16[16,32,480]{2,1,0:T(8,128)(2,1)S(1)} %get-tuple-element.336.vt, ...), custom_call_target="tpu_custom_call" | custom-call | flops 30000001024 | bytes 45000000 | tf_op jit(solution)/shard_map/backward_body/pallas_call | solution.py:59
  100.5 2.8 %weigh_body.2 = (f32[768,480]{1,0:T(8,128)S(1)}, f32[2,384]{1,0:T(2,128)S(1)}, bf16[2,4,144,384]{3,2,1,0:T(8,128)(2,1)S(1)}, bf16[2,4,144,384]{3,2,1,0:T(8,128)(2,1)S(1)}) custom-call(bf16[768,480]{1,0:T(8,128)(2,1)S(1)} %get-tuple-element.377.nt_r, bf16[192,480]{1,0:T(8,128)(2,1)S(1)} %get-tuple-element.342.qa, bf16[192,480]{1,0:T(8,128)(2,1)S(1)} %get-tuple-element.343.ka, ...), custom_call_target="tpu_custom_call" | custom-call | flops 200000000 | bytes 300000 | tf_op jit(solution)/shard_map/weigh_body/pallas_call | solution.py:59
  103.9 6.0 %backward_body.6 = (bf16[192,480]{1,0:T(8,128)(2,1)S(1)}, bf16[192,480]{1,0:T(8,128)(2,1)S(1)}, bf16[192,480]{1,0:T(8,128)(2,1)S(1)}) custom-call(bf16[16,32,480]{2,1,0:T(8,128)(2,1)S(1)} %get-tuple-element.366.qt, bf16[16,32,480]{2,1,0:T(8,128)(2,1)S(1)} %get-tuple-element.367.kt, bf16[16,32,480]{2,1,0:T(8,128)(2,1)S(1)} %get-tuple-element.368.vt, ...), custom_call_target="tpu_custom_call" | custom-call | flops 30000001024 | bytes 45000000 | tf_op jit(solution)/shard_map/backward_body/pallas_call | solution.py:59
  110.6 6.0 %backward_body.7 = (bf16[192,480]{1,0:T(8,128)(2,1)S(1)}, bf16[192,480]{1,0:T(8,128)(2,1)S(1)}, bf16[192,480]{1,0:T(8,128)(2,1)S(1)}) custom-call(bf16[16,32,480]{2,1,0:T(8,128)(2,1)S(1)} %get-tuple-element.366.qt, bf16[16,32,480]{2,1,0:T(8,128)(2,1)S(1)} %get-tuple-element.367.kt, bf16[16,32,480]{2,1,0:T(8,128)(2,1)S(1)} %get-tuple-element.368.vt, ...), custom_call_target="tpu_custom_call" | custom-call | flops 30000001024 | bytes 45000000 | tf_op jit(solution)/shard_map/backward_body/pallas_call | solution.py:59
  118.3 2.8 %weigh_body.3 = (f32[768,480]{1,0:T(8,128)S(1)}, f32[2,384]{1,0:T(2,128)S(1)}, bf16[2,4,144,384]{3,2,1,0:T(8,128)(2,1)S(1)}, bf16[2,4,144,384]{3,2,1,0:T(8,128)(2,1)S(1)}) custom-call(bf16[768,480]{1,0:T(8,128)(2,1)S(1)} %get-tuple-element.377.nt_r, bf16[192,480]{1,0:T(8,128)(2,1)S(1)} %get-tuple-element.378.qa, bf16[192,480]{1,0:T(8,128)(2,1)S(1)} %get-tuple-element.379.ka, ...), custom_call_target="tpu_custom_call" | custom-call | flops 200000000 | bytes 300000 | tf_op jit(solution)/shard_map/weigh_body/pallas_call | solution.py:59
  121.2 3.0 %finish_body.1 = (bf16[480,768]{1,0:T(8,128)(2,1)S(1)}, f32[8,384]{1,0:T(8,128)S(1)}) custom-call(s32[2]{0:T(128)S(1)} %pad_add_fusion.info, f32[768,480]{1,0:T(8,128)S(1)} %get-tuple-element.388.dn0, f32[768,480]{1,0:T(8,128)S(1)} %get-tuple-element.389.dn1, bf16[480,768]{1,0:T(8,128)(2,1)S(1)} %get-tuple-element.296.x_r, ...), custom_call_target="tpu_custom_call" | custom-call | flops 40000000000 | bytes 60000000 | tf_op jit(solution)/shard_map/finish_body/pallas_call | solution.py:59
  125.7 3.6 %collective-permute-done.32.passed = bf16[608,384]{1,0:T(8,128)(2,1)S(1)} collective-permute-done((bf16[608,384]{1,0:T(8,128)(2,1)S(1)}, bf16[608,384]{1,0:T(8,128)(2,1)S(1)}, u32[]{:S(2)}, u32[]{:S(2)}) %collective-permute-start.32) | collective-permute-done | bytes 466976 | tf_op jit(solution)/shard_map/ppermute | solution.py:25
  132.4 2.7 %collective-permute-start.35 = (bf16[320,384]{1,0:T(8,128)(2,1)S(1)}, bf16[320,384]{1,0:T(8,128)(2,1)S(1)}, u32[]{:S(2)}, u32[]{:S(2)}) collective-permute-start(bf16[320,384]{1,0:T(8,128)(2,1)S(1)} %get-tuple-element.412), channel_id=1, source_target_pairs={{0,16},{1,17},{2,18},{3,19},{4,20},{5,21},{6,22},{7,23},{8,24},{9,... | collective-permute-start | bytes 737288 | tf_op jit(solution)/shard_map/ppermute | solution.py:25
  135.6 2.5 %join_body.2 = bf16[2,832,768]{2,1,0:T(8,128)(2,1)} custom-call(s32[2]{0:T(128)S(1)} %pad_add_fusion.info, s32[2,832]{1,0:T(2,128)S(1)} %copy-done.18, bf16[480,768]{1,0:T(8,128)(2,1)S(1)} %get-tuple-element.413.own, bf16[480,768]{1,0:T(8,128)(2,1)S(1)} %copy-done.13, bf16[480,768]{1,0:T(8,128)(2,1)S(1)} %collective-permute-done.26.across, ...), custom_call_target="tpu_custom_call" | custom-call | flops 40000000000 | bytes 60000000 | tf_op jit(solution)/shard_map/join_body/pallas_call | solution.py:59
  138.0 8.2 %collective-permute-done.35.got = bf16[320,384]{1,0:T(8,128)(2,1)S(1)} collective-permute-done((bf16[320,384]{1,0:T(8,128)(2,1)S(1)}, bf16[320,384]{1,0:T(8,128)(2,1)S(1)}, u32[]{:S(2)}, u32[]{:S(2)}) %collective-permute-start.35) | collective-permute-done | bytes 245792 | tf_op jit(solution)/shard_map/ppermute | solution.py:25
  151.7 6.0 %collective-permute-done.42.across = bf16[480,768]{1,0:T(8,128)(2,1)S(1)} collective-permute-done((bf16[480,768]{1,0:T(8,128)(2,1)S(1)}, bf16[480,768]{1,0:T(8,128)(2,1)S(1)}, u32[]{:S(2)}, u32[]{:S(2)}) %collective-permute-start.42) | collective-permute-done | bytes 737312 | tf_op jit(solution)/shard_map/ppermute | solution.py:25
  160.0 2.5 %join_body.3 = bf16[2,832,768]{2,1,0:T(8,128)(2,1)} custom-call(s32[2]{0:T(128)S(1)} %pad_add_fusion.info, s32[2,832]{1,0:T(2,128)S(1)} %copy-done.19, bf16[480,768]{1,0:T(8,128)(2,1)S(1)} %get-tuple-element.401.own, bf16[480,768]{1,0:T(8,128)(2,1)S(1)} %collective-permute-done.34.beside, bf16[480,768]{1,0:T(8,128)(2,1)S(1)} %collective-permute-done.42.across, ...), custom_call_target="tpu_custom_call" | custom-call | flops 40000000000 | bytes 60000000 | tf_op jit(solution)/shard_map/join_body/pallas_call | solution.py:59
  (167 shorter events, 62.9 us)
Async XLA Ops:
  6.8 10.7 %collective-permute-start.2 = (bf16[1,160,384]{2,1,0:T(8,128)(2,1)S(1)}, bf16[1,160,384]{2,1,0:T(8,128)(2,1)S(1)}, u32[]{:S(2)}, u32[]{:S(2)}) collective-permute-start(bf16[1,160,384]{2,1,0:T(8,128)(2,1)S(1)} %meet_a_body.1.refs_0_), channel_id=1, source_target_pairs={{0,8},{1,9},{2,10},{3,11},{4,12},{5,13},{6,14},{7,15},{8,0},{9,1},... | collective-permute-start | bytes 368648 | tf_op jit(solution)/shard_map/ppermute | solution.py:25
  9.9 12.4 %collective-permute-start.3 = (bf16[1,160,384]{2,1,0:T(8,128)(2,1)S(1)}, bf16[1,160,384]{2,1,0:T(8,128)(2,1)S(1)}, u32[]{:S(2)}, u32[]{:S(2)}) collective-permute-start(bf16[1,160,384]{2,1,0:T(8,128)(2,1)S(1)} %meet_a_body.1.refs_0_), channel_id=1, source_target_pairs={{0,16},{1,17},{2,18},{3,19},{4,20},{5,21},{6,22},{7,23},{8,24},{9,... | collective-permute-start | bytes 368648 | tf_op jit(solution)/shard_map/ppermute | solution.py:25
  12.5 9.8 %collective-permute-start.4 = (bf16[1,160,384]{2,1,0:T(8,128)(2,1)S(1)}, bf16[1,160,384]{2,1,0:T(8,128)(2,1)S(1)}, u32[]{:S(2)}, u32[]{:S(2)}) collective-permute-start(bf16[1,160,384]{2,1,0:T(8,128)(2,1)S(1)} %meet_a_body.1.refs_0_), channel_id=1, source_target_pairs={{0,24},{1,25},{2,26},{3,27},{4,28},{5,29},{6,30},{7,31},{8,16},{9,... | collective-permute-start | bytes 368648 | tf_op jit(solution)/shard_map/ppermute | solution.py:25
  22.4 15.0 %collective-permute-start.10 = (bf16[4,160,384]{2,1,0:T(8,128)(2,1)S(1)}, bf16[4,160,384]{2,1,0:T(8,128)(2,1)S(1)}, u32[]{:S(2)}, u32[]{:S(2)}) collective-permute-start(bf16[4,160,384]{2,1,0:T(8,128)(2,1)S(1)} %stack_body.2.refs_0_), channel_id=1, source_target_pairs={{0,2},{1,3},{2,0},{3,1},{4,6},{5,7},{6,4},{7,5},{8,10},{9,11},{10,... | collective-permute-start | bytes 1474568 | tf_op jit(solution)/shard_map/ppermute | solution.py:25
  24.0 13.4 %collective-permute-start.9 = (bf16[4,160,384]{2,1,0:T(8,128)(2,1)S(1)}, bf16[4,160,384]{2,1,0:T(8,128)(2,1)S(1)}, u32[]{:S(2)}, u32[]{:S(2)}) collective-permute-start(bf16[4,160,384]{2,1,0:T(8,128)(2,1)S(1)} %stack_body.2.refs_0_), channel_id=1, source_target_pairs={{0,4},{1,5},{2,6},{3,7},{4,0},{5,1},{6,2},{7,3},{8,12},{9,13},{10,... | collective-permute-start | bytes 1474568 | tf_op jit(solution)/shard_map/ppermute | solution.py:25
  25.5 8.4 %collective-permute-start.6 = (bf16[1,144,384]{2,1,0:T(8,128)(2,1)S(1)}, bf16[1,144,384]{2,1,0:T(8,128)(2,1)S(1)}, u32[]{:S(2)}, u32[]{:S(2)}) collective-permute-start(bf16[1,144,384]{2,1,0:T(8,128)(2,1)S(1)} %meet_b_body.1.refs_0_), channel_id=1, source_target_pairs={{0,8},{1,9},{2,10},{3,11},{4,12},{5,13},{6,14},{7,15},{8,0},{9,1},... | collective-permute-start | bytes 331784 | tf_op jit(solution)/shard_map/ppermute | solution.py:25
  27.5 9.9 %collective-permute-start.7 = (bf16[1,144,384]{2,1,0:T(8,128)(2,1)S(1)}, bf16[1,144,384]{2,1,0:T(8,128)(2,1)S(1)}, u32[]{:S(2)}, u32[]{:S(2)}) collective-permute-start(bf16[1,144,384]{2,1,0:T(8,128)(2,1)S(1)} %meet_b_body.1.refs_0_), channel_id=1, source_target_pairs={{0,16},{1,17},{2,18},{3,19},{4,20},{5,21},{6,22},{7,23},{8,24},{9,... | collective-permute-start | bytes 331784 | tf_op jit(solution)/shard_map/ppermute | solution.py:25
  28.5 8.9 %collective-permute-start.8 = (bf16[1,144,384]{2,1,0:T(8,128)(2,1)S(1)}, bf16[1,144,384]{2,1,0:T(8,128)(2,1)S(1)}, u32[]{:S(2)}, u32[]{:S(2)}) collective-permute-start(bf16[1,144,384]{2,1,0:T(8,128)(2,1)S(1)} %meet_b_body.1.refs_0_), channel_id=1, source_target_pairs={{0,24},{1,25},{2,26},{3,27},{4,28},{5,29},{6,30},{7,31},{8,16},{9,... | collective-permute-start | bytes 331784 | tf_op jit(solution)/shard_map/ppermute | solution.py:25
  38.0 15.0 %collective-permute-start.14 = (bf16[4,160,384]{2,1,0:T(8,128)(2,1)S(1)}, bf16[4,160,384]{2,1,0:T(8,128)(2,1)S(1)}, u32[]{:S(2)}, u32[]{:S(2)}) collective-permute-start(bf16[4,160,384]{2,1,0:T(8,128)(2,1)S(1)} %stack_body.2.refs_0_), channel_id=1, source_target_pairs={{0,6},{1,7},{2,4},{3,5},{4,2},{5,3},{6,0},{7,1},{8,14},{9,15},{10,... | collective-permute-start | bytes 1474568 | tf_op jit(solution)/shard_map/ppermute | solution.py:25
  41.7 21.9 %collective-permute-start.17 = (bf16[4,144,384]{2,1,0:T(8,128)(2,1)S(1)}, bf16[4,144,384]{2,1,0:T(8,128)(2,1)S(1)}, u32[]{:S(2)}, u32[]{:S(2)}) collective-permute-start(bf16[4,144,384]{2,1,0:T(8,128)(2,1)S(1)} %stack_body.3.refs_0_), channel_id=1, source_target_pairs={{0,4},{1,5},{2,6},{3,7},{4,0},{5,1},{6,2},{7,3},{8,12},{9,13},{10,... | collective-permute-start | bytes 1327112 | tf_op jit(solution)/shard_map/ppermute | solution.py:25
  42.3 21.3 %collective-permute-start.18 = (bf16[4,144,384]{2,1,0:T(8,128)(2,1)S(1)}, bf16[4,144,384]{2,1,0:T(8,128)(2,1)S(1)}, u32[]{:S(2)}, u32[]{:S(2)}) collective-permute-start(bf16[4,144,384]{2,1,0:T(8,128)(2,1)S(1)} %stack_body.3.refs_0_), channel_id=1, source_target_pairs={{0,2},{1,3},{2,0},{3,1},{4,6},{5,7},{6,4},{7,5},{8,10},{9,11},{10,... | collective-permute-start | bytes 1327112 | tf_op jit(solution)/shard_map/ppermute | solution.py:25
  43.3 27.8 %collective-permute-start.21 = (bf16[4,144,384]{2,1,0:T(8,128)(2,1)S(1)}, bf16[4,144,384]{2,1,0:T(8,128)(2,1)S(1)}, u32[]{:S(2)}, u32[]{:S(2)}) collective-permute-start(bf16[4,144,384]{2,1,0:T(8,128)(2,1)S(1)} %stack_body.3.refs_0_), channel_id=1, source_target_pairs={{0,6},{1,7},{2,4},{3,5},{4,2},{5,3},{6,0},{7,1},{8,14},{9,15},{10,... | collective-permute-start | bytes 1327112 | tf_op jit(solution)/shard_map/ppermute | solution.py:25
  78.0 25.3 %collective-permute-start.26 = (bf16[480,768]{1,0:T(8,128)(2,1)S(1)}, bf16[480,768]{1,0:T(8,128)(2,1)S(1)}, u32[]{:S(2)}, u32[]{:S(2)}) collective-permute-start(bf16[480,768]{1,0:T(8,128)(2,1)S(1)} %get-tuple-element.413.own), channel_id=1, source_target_pairs={{0,2},{1,3},{2,0},{3,1},{4,6},{5,7},{6,4},{7,5},{8,10},{9,11},{10,... | collective-permute-start | bytes 2211848 | tf_op jit(solution)/shard_map/ppermute | solution.py:25
  92.9 23.9 %collective-permute-start.29 = (bf16[1184,384]{1,0:T(8,128)(2,1)S(1)}, bf16[1184,384]{1,0:T(8,128)(2,1)S(1)}, u32[]{:S(2)}, u32[]{:S(2)}) collective-permute-start(bf16[1184,384]{1,0:T(8,128)(2,1)S(1)} %get-tuple-element.376), channel_id=1, source_target_pairs={{0,2},{1,3},{2,0},{3,1},{4,6},{5,7},{6,4},{7,5},{8,10},{9,11},{10,... | collective-permute-start | bytes 2727944 | tf_op jit(solution)/shard_map/ppermute | solution.py:25
  110.1 15.7 %collective-permute-start.31 = (bf16[576,384]{1,0:T(8,128)(2,1)S(1)}, bf16[576,384]{1,0:T(8,128)(2,1)S(1)}, u32[]{:S(2)}, u32[]{:S(2)}) collective-permute-start(bf16[576,384]{1,0:T(8,128)(2,1)S(1)} %get-tuple-element.396), channel_id=1, source_target_pairs={{0,2},{1,3},{2,0},{3,1},{4,6},{5,7},{6,4},{7,5},{8,10},{9,11},{10,... | collective-permute-start | bytes 1327112 | tf_op jit(solution)/shard_map/ppermute | solution.py:25
  117.0 12.3 %collective-permute-start.32 = (bf16[608,384]{1,0:T(8,128)(2,1)S(1)}, bf16[608,384]{1,0:T(8,128)(2,1)S(1)}, u32[]{:S(2)}, u32[]{:S(2)}) collective-permute-start(bf16[608,384]{1,0:T(8,128)(2,1)S(1)} %get-tuple-element.399), channel_id=1, source_target_pairs={{0,4},{1,5},{2,6},{3,7},{4,0},{5,1},{6,2},{7,3},{8,12},{9,13},{10,... | collective-permute-start | bytes 1400840 | tf_op jit(solution)/shard_map/ppermute | solution.py:25
  129.9 16.5 %collective-permute-start.37 = (bf16[576,384]{1,0:T(8,128)(2,1)S(1)}, bf16[576,384]{1,0:T(8,128)(2,1)S(1)}, u32[]{:S(2)}, u32[]{:S(2)}) collective-permute-start(bf16[576,384]{1,0:T(8,128)(2,1)S(1)} %get-tuple-element.422), channel_id=1, source_target_pairs={{0,2},{1,3},{2,0},{3,1},{4,6},{5,7},{6,4},{7,5},{8,10},{9,11},{10,... | collective-permute-start | bytes 1327112 | tf_op jit(solution)/shard_map/ppermute | solution.py:25
  131.4 26.4 %collective-permute-start.42 = (bf16[480,768]{1,0:T(8,128)(2,1)S(1)}, bf16[480,768]{1,0:T(8,128)(2,1)S(1)}, u32[]{:S(2)}, u32[]{:S(2)}) collective-permute-start(bf16[480,768]{1,0:T(8,128)(2,1)S(1)} %get-tuple-element.401.own), channel_id=1, source_target_pairs={{0,2},{1,3},{2,0},{3,1},{4,6},{5,7},{6,4},{7,5},{8,10},{9,11},{10,... | collective-permute-start | bytes 2211848 | tf_op jit(solution)/shard_map/ppermute | solution.py:25
  132.4 13.9 %collective-permute-start.35 = (bf16[320,384]{1,0:T(8,128)(2,1)S(1)}, bf16[320,384]{1,0:T(8,128)(2,1)S(1)}, u32[]{:S(2)}, u32[]{:S(2)}) collective-permute-start(bf16[320,384]{1,0:T(8,128)(2,1)S(1)} %get-tuple-element.412), channel_id=1, source_target_pairs={{0,16},{1,17},{2,18},{3,19},{4,20},{5,21},{6,22},{7,23},{8,24},{9,... | collective-permute-start | bytes 737288 | tf_op jit(solution)/shard_map/ppermute | solution.py:25
  135.0 11.9 %collective-permute-start.36 = (bf16[592,384]{1,0:T(8,128)(2,1)S(1)}, bf16[592,384]{1,0:T(8,128)(2,1)S(1)}, u32[]{:S(2)}, u32[]{:S(2)}) collective-permute-start(bf16[592,384]{1,0:T(8,128)(2,1)S(1)} %get-tuple-element.421), channel_id=1, source_target_pairs={{0,4},{1,5},{2,6},{3,7},{4,0},{5,1},{6,2},{7,3},{8,12},{9,13},{10,... | collective-permute-start | bytes 1363976 | tf_op jit(solution)/shard_map/ppermute | solution.py:25
  147.2 10.6 %collective-permute-start.41 = (bf16[176,384]{1,0:T(8,128)(2,1)S(1)}, bf16[176,384]{1,0:T(8,128)(2,1)S(1)}, u32[]{:S(2)}, u32[]{:S(2)}) collective-permute-start(bf16[176,384]{1,0:T(8,128)(2,1)S(1)} %get-tuple-element.440), channel_id=1, source_target_pairs={{0,8},{1,9},{2,10},{3,11},{4,12},{5,13},{6,14},{7,15},{8,0},{9,1},... | collective-permute-start | bytes 405512 | tf_op jit(solution)/shard_map/ppermute | solution.py:25
  147.2 16.6 %collective-permute-start.38 = (bf16[160,384]{1,0:T(8,128)(2,1)S(1)}, bf16[160,384]{1,0:T(8,128)(2,1)S(1)}, u32[]{:S(2)}, u32[]{:S(2)}) collective-permute-start(bf16[160,384]{1,0:T(8,128)(2,1)S(1)} %get-tuple-element.435), channel_id=1, source_target_pairs={{0,8},{1,9},{2,10},{3,11},{4,12},{5,13},{6,14},{7,15},{8,0},{9,1},... | collective-permute-start | bytes 368648 | tf_op jit(solution)/shard_map/ppermute | solution.py:25
  149.2 14.6 %collective-permute-start.39 = (bf16[160,384]{1,0:T(8,128)(2,1)S(1)}, bf16[160,384]{1,0:T(8,128)(2,1)S(1)}, u32[]{:S(2)}, u32[]{:S(2)}) collective-permute-start(bf16[160,384]{1,0:T(8,128)(2,1)S(1)} %get-tuple-element.436), channel_id=1, source_target_pairs={{0,16},{1,17},{2,18},{3,19},{4,20},{5,21},{6,22},{7,23},{8,24},{9,... | collective-permute-start | bytes 368648 | tf_op jit(solution)/shard_map/ppermute | solution.py:25
  149.6 14.2 %collective-permute-start.40 = (bf16[160,384]{1,0:T(8,128)(2,1)S(1)}, bf16[160,384]{1,0:T(8,128)(2,1)S(1)}, u32[]{:S(2)}, u32[]{:S(2)}) collective-permute-start(bf16[160,384]{1,0:T(8,128)(2,1)S(1)} %get-tuple-element.437), channel_id=1, source_target_pairs={{0,24},{1,25},{2,26},{3,27},{4,28},{5,29},{6,30},{7,31},{8,16},{9,... | collective-permute-start | bytes 368648 | tf_op jit(solution)/shard_map/ppermute | solution.py:25
  (43 other events, 232.0 us)

commit v4 on v3

--- a/solution.py
+++ b/solution.py
@@ -917,12 +917,6 @@
         grad_window, a_sums, got0, a_far1, b_x = fence(grad_window, a_sums, got0, a_far1, b_x)
 
         gw_y, gw_c, a_sums_got = to(grad_window, 0, 2), to(grad_window, 0, 1), to(a_sums, 0, 1)
-        a_sums_got, gw_c, keep0 = fence(a_sums_got, gw_c, keep0)
-        a_x, a_sums = call(
-            near_a_body, [((n_near + 16, cols), BF16), f32_8], [keep0, got0, a_far1, a_sums, a_sums_got]
-        )
-        a_x, b_keep = fence(a_x, b_keep)
-        a_x = to(a_x, 1, 0)
         b_own, b_z2, b_sums = call(
             high_b_body,
             [((2, 3 * half, cols), F32), ((n_two + 32, cols), BF16), f32_16],
@@ -931,7 +925,11 @@
         b_z2, result = fence(b_z2, result)
         b_z2 = to(b_z2, 4, 0)
         out_hidden = join(result, res_c, res_y, res_yc)
-        b_z2, out_hidden = fence(b_z2, out_hidden)
+        a_sums_got, gw_c, keep0, out_hidden = fence(a_sums_got, gw_c, keep0, out_hidden)
+        a_x, a_sums = call(
+            near_a_body, [((n_near + 16, cols), BF16), f32_8], [keep0, got0, a_far1, a_sums, a_sums_got]
+        )
+        a_x = to(a_x, 1, 0)
 
         def last(own, sums, got, kind):
             return call(last_body, [((3, half, wc), F32)] * 2 + [kind], [side, own, sums] + got, (), 1, us=20)

time: 171 us -> 173 us (1.012)
  Pallas kernels: 73.3 us -> 75.2 us
    pallas_call x33, Pallas kernels: 73.3 us -> 75.2 us  [call(): pl.pallas_call(body, out_shape=tuple((jax.ShapeDtypeStruct(s, d) for s, d...]
  transfers between devices with their start and end apart: 47 -> 47, of which waited for: 16 -> 15; matrix products, arithmetic and copies ran while one was open for 3% -> 3% of each run, Pallas kernels for 38% -> 39%
where the time goes in v4:
time: 173 us; the launch traced here: 172 us
  Pallas kernels  75.2 us (43%)
  waiting for transfers between devices  47.5 us (27%)
  starting transfers between devices  36.3 us (21%)
  local copies, waits for them, and re-layouts  11 us (6%)
    pallas_call x33, Pallas kernels, call(): pl.pallas_call(body, out_shape=tuple((jax.ShapeDtypeStruct(s, d) for s, d...  75.2 us
    ppermute x47, waiting for transfers between devices, send(): return lax.ppermute(value, BOTH, pairs)  47.5 us
    ppermute x47, starting transfers between devices, send(): return lax.ppermute(value, BOTH, pairs)  36.3 us
    unnamed x42, local copies, waits for them, and re-layouts  6.47 us
  transfers between devices with their start and end apart: 47, of which 15 were waited for; matrix products, arithmetic and copies ran while one was open for 3% of the time, Pallas kernels for 39%

profile of v4, /device:TPU:0, one launch (start us, length us, event | category | flops | bytes accessed | tf_op | source)
XLA Modules:
  0.0 172.2 jit_solution(11667460576566942523)
XLA Ops:
  6.8 3.1 %collective-permute-start.2 = (bf16[1,160,384]{2,1,0:T(8,128)(2,1)S(1)}, bf16[1,160,384]{2,1,0:T(8,128)(2,1)S(1)}, u32[]{:S(2)}, u32[]{:S(2)}) collective-permute-start(bf16[1,160,384]{2,1,0:T(8,128)(2,1)S(1)} %meet_a_body.1.refs_0_), channel_id=1, source_target_pairs={{0,8},{1,9},{2,10},{3,11},{4,12},{5,13},{6,14},{7,15},{8,0},{9,1},... | collective-permute-start | bytes 368648 | tf_op jit(solution)/shard_map/ppermute | solution.py:25
  9.9 2.6 %collective-permute-start.3 = (bf16[1,160,384]{2,1,0:T(8,128)(2,1)S(1)}, bf16[1,160,384]{2,1,0:T(8,128)(2,1)S(1)}, u32[]{:S(2)}, u32[]{:S(2)}) collective-permute-start(bf16[1,160,384]{2,1,0:T(8,128)(2,1)S(1)} %meet_a_body.1.refs_0_), channel_id=1, source_target_pairs={{0,16},{1,17},{2,18},{3,19},{4,20},{5,21},{6,22},{7,23},{8,24},{9,... | collective-permute-start | bytes 368648 | tf_op jit(solution)/shard_map/ppermute | solution.py:25
  17.6 4.8 %collective-permute-done.3.refs_2_ = bf16[1,160,384]{2,1,0:T(8,128)(2,1)S(1)} collective-permute-done((bf16[1,160,384]{2,1,0:T(8,128)(2,1)S(1)}, bf16[1,160,384]{2,1,0:T(8,128)(2,1)S(1)}, u32[]{:S(2)}, u32[]{:S(2)}) %collective-permute-start.3) | collective-permute-done | bytes 122912 | tf_op jit(solution)/shard_map/ppermute | solution.py:25
  33.8 3.6 %collective-permute-done.7.refs_2_ = bf16[1,144,384]{2,1,0:T(8,128)(2,1)S(1)} collective-permute-done((bf16[1,144,384]{2,1,0:T(8,128)(2,1)S(1)}, bf16[1,144,384]{2,1,0:T(8,128)(2,1)S(1)}, u32[]{:S(2)}, u32[]{:S(2)}) %collective-permute-start.7) | collective-permute-done | bytes 110624 | tf_op jit(solution)/shard_map/ppermute | solution.py:25
  45.3 2.8 %forward_body.3 = (f32[8,32,480]{2,1,0:T(8,128)S(1)}, f32[8,1,480]{2,1,0:T(1,128)S(1)}) custom-call(bf16[16,32,480]{2,1,0:T(8,128)(2,1)S(1)} %get-tuple-element.363.qt, bf16[16,32,480]{2,1,0:T(8,128)(2,1)S(1)} %get-tuple-element.364.kt, bf16[16,32,480]{2,1,0:T(8,128)(2,1)S(1)} %get-tuple-element.365.vt, f32[480,512]{1,0:T(8,128)S(1)} %get-tuple-element.275.bias), custom_call_target="tpu_custom_call" | custom-call | flops 10000000000 | bytes 15000000 | tf_op jit(solution)/shard_map/forward_body/pallas_call | solution.py:59
  48.1 4.9 %collective-permute-done.14.refs_2_ = bf16[4,160,384]{2,1,0:T(8,128)(2,1)S(1)} collective-permute-done((bf16[4,160,384]{2,1,0:T(8,128)(2,1)S(1)}, bf16[4,160,384]{2,1,0:T(8,128)(2,1)S(1)}, u32[]{:S(2)}, u32[]{:S(2)}) %collective-permute-start.14) | collective-permute-done | bytes 491552 | tf_op jit(solution)/shard_map/ppermute | solution.py:25
  53.5 2.8 %forward_body.4 = (f32[8,32,480]{2,1,0:T(8,128)S(1)}, f32[8,1,480]{2,1,0:T(1,128)S(1)}) custom-call(bf16[16,32,480]{2,1,0:T(8,128)(2,1)S(1)} %get-tuple-element.363.qt, bf16[16,32,480]{2,1,0:T(8,128)(2,1)S(1)} %get-tuple-element.364.kt, bf16[16,32,480]{2,1,0:T(8,128)(2,1)S(1)} %get-tuple-element.365.vt, f32[480,512]{1,0:T(8,128)S(1)} %get-tuple-element.275.bias), custom_call_target="tpu_custom_call" | custom-call | flops 10000000000 | bytes 15000000 | tf_op jit(solution)/shard_map/forward_body/pallas_call | solution.py:59
  57.9 5.8 %forward_body.5 = (f32[16,32,480]{2,1,0:T(8,128)S(1)}, f32[16,1,480]{2,1,0:T(1,128)S(1)}) custom-call(bf16[16,32,480]{2,1,0:T(8,128)(2,1)S(1)} %get-tuple-element.331.qt, bf16[16,32,480]{2,1,0:T(8,128)(2,1)S(1)} %get-tuple-element.332.kt, bf16[16,32,480]{2,1,0:T(8,128)(2,1)S(1)} %get-tuple-element.333.vt, f32[480,512]{1,0:T(8,128)S(1)} %get-tuple-element.275.bias), custom_call_target="tpu_custom_call" | custom-call | flops 10000000000 | bytes 15000000 | tf_op jit(solution)/shard_map/forward_body/pallas_call | solution.py:59
  64.3 6.8 %collective-permute-done.21.refs_6_ = bf16[4,144,384]{2,1,0:T(8,128)(2,1)S(1)} collective-permute-done((bf16[4,144,384]{2,1,0:T(8,128)(2,1)S(1)}, bf16[4,144,384]{2,1,0:T(8,128)(2,1)S(1)}, u32[]{:S(2)}, u32[]{:S(2)}) %collective-permute-start.21) | collective-permute-done | bytes 442400 | tf_op jit(solution)/shard_map/ppermute | solution.py:25
  72.9 4.9 %feed_body.1 = (bf16[480,768]{1,0:T(8,128)(2,1)S(1)}, f32[480,768]{1,0:T(8,128)S(1)}, f32[480,1]{1,0:T(8,128)S(1)}, bf16[480,768]{1,0:T(8,128)(2,1)S(1)}, bf16[4...) custom-call(bf16[480,768]{1,0:T(8,128)(2,1)S(1)} %get-tuple-element., ...), custom_call_target="tpu_custom_call" | custom-call | flops 10000000000 | bytes 15000000 | tf_op jit(solution)/shard_map/feed_body/pallas_call | solution.py:59
  78.5 6.8 %feed_back_body.1 = (f32[480,768]{1,0:T(8,128)S(1)}, bf16[16,32,480]{2,1,0:T(8,128)(2,1)S(1)}, bf16[16,32,480]{2,1,0:T(8,128)(2,1)S(1)}, f32[16,384]{1,0:T(8,128...) custom-call(s32[2]{0:T(128)S(1)} %pad_add_fusion.info, ...), custom_call_target="tpu_custom_call" | custom-call | flops 14000000000 | bytes 21000000 | tf_op jit(solution)/shard_map/feed_back_body/pallas_call | solution.py:59
  86.7 6.0 %backward_body.4 = (bf16[192,480]{1,0:T(8,128)(2,1)S(1)}, bf16[192,480]{1,0:T(8,128)(2,1)S(1)}, bf16[192,480]{1,0:T(8,128)(2,1)S(1)}) custom-call(bf16[16,32,480]{2,1,0:T(8,128)(2,1)S(1)} %get-tuple-element.331.qt, bf16[16,32,480]{2,1,0:T(8,128)(2,1)S(1)} %get-tuple-element.332.kt, bf16[16,32,480]{2,1,0:T(8,128)(2,1)S(1)} %get-tuple-element.333.vt, ...), custom_call_target="tpu_custom_call" | custom-call | flops 30000001024 | bytes 45000000 | tf_op jit(solution)/shard_map/backward_body/pallas_call | solution.py:59
  94.5 6.0 %backward_body.5 = (bf16[192,480]{1,0:T(8,128)(2,1)S(1)}, bf16[192,480]{1,0:T(8,128)(2,1)S(1)}, bf16[192,480]{1,0:T(8,128)(2,1)S(1)}) custom-call(bf16[16,32,480]{2,1,0:T(8,128)(2,1)S(1)} %get-tuple-element.331.qt, bf16[16,32,480]{2,1,0:T(8,128)(2,1)S(1)} %get-tuple-element.332.kt, bf16[16,32,480]{2,1,0:T(8,128)(2,1)S(1)} %get-tuple-element.333.vt, ...), custom_call_target="tpu_custom_call" | custom-call | flops 30000001024 | bytes 45000000 | tf_op jit(solution)/shard_map/backward_body/pallas_call | solution.py:59
  100.5 2.8 %weigh_body.2 = (f32[768,480]{1,0:T(8,128)S(1)}, f32[2,384]{1,0:T(2,128)S(1)}, bf16[2,4,144,384]{3,2,1,0:T(8,128)(2,1)S(1)}, bf16[2,4,144,384]{3,2,1,0:T(8,128)(2,1)S(1)}) custom-call(bf16[768,480]{1,0:T(8,128)(2,1)S(1)} %get-tuple-element.374.nt_r, bf16[192,480]{1,0:T(8,128)(2,1)S(1)} %get-tuple-element.339.qa, bf16[192,480]{1,0:T(8,128)(2,1)S(1)} %get-tuple-element.340.ka, ...), custom_call_target="tpu_custom_call" | custom-call | flops 200000000 | bytes 300000 | tf_op jit(solution)/shard_map/weigh_body/pallas_call | solution.py:59
  103.9 6.0 %backward_body.6 = (bf16[192,480]{1,0:T(8,128)(2,1)S(1)}, bf16[192,480]{1,0:T(8,128)(2,1)S(1)}, bf16[192,480]{1,0:T(8,128)(2,1)S(1)}) custom-call(bf16[16,32,480]{2,1,0:T(8,128)(2,1)S(1)} %get-tuple-element.363.qt, bf16[16,32,480]{2,1,0:T(8,128)(2,1)S(1)} %get-tuple-element.364.kt, bf16[16,32,480]{2,1,0:T(8,128)(2,1)S(1)} %get-tuple-element.365.vt, ...), custom_call_target="tpu_custom_call" | custom-call | flops 30000001024 | bytes 45000000 | tf_op jit(solution)/shard_map/backward_body/pallas_call | solution.py:59
  112.8 5.9 %backward_body.7 = (bf16[192,480]{1,0:T(8,128)(2,1)S(1)}, bf16[192,480]{1,0:T(8,128)(2,1)S(1)}, bf16[192,480]{1,0:T(8,128)(2,1)S(1)}) custom-call(bf16[16,32,480]{2,1,0:T(8,128)(2,1)S(1)} %get-tuple-element.363.qt, bf16[16,32,480]{2,1,0:T(8,128)(2,1)S(1)} %get-tuple-element.364.kt, bf16[16,32,480]{2,1,0:T(8,128)(2,1)S(1)} %get-tuple-element.365.vt, ...), custom_call_target="tpu_custom_call" | custom-call | flops 30000001024 | bytes 45000000 | tf_op jit(solution)/shard_map/backward_body/pallas_call | solution.py:59
  120.2 2.8 %weigh_body.3 = (f32[768,480]{1,0:T(8,128)S(1)}, f32[2,384]{1,0:T(2,128)S(1)}, bf16[2,4,144,384]{3,2,1,0:T(8,128)(2,1)S(1)}, bf16[2,4,144,384]{3,2,1,0:T(8,128)(2,1)S(1)}) custom-call(bf16[768,480]{1,0:T(8,128)(2,1)S(1)} %get-tuple-element.374.nt_r, bf16[192,480]{1,0:T(8,128)(2,1)S(1)} %get-tuple-element.375.qa, bf16[192,480]{1,0:T(8,128)(2,1)S(1)} %get-tuple-element.376.ka, ...), custom_call_target="tpu_custom_call" | custom-call | flops 200000000 | bytes 300000 | tf_op jit(solution)/shard_map/weigh_body/pallas_call | solution.py:59
  123.1 3.0 %finish_body.1 = (bf16[480,768]{1,0:T(8,128)(2,1)S(1)}, f32[8,384]{1,0:T(8,128)S(1)}) custom-call(s32[2]{0:T(128)S(1)} %pad_add_fusion.info, f32[768,480]{1,0:T(8,128)S(1)} %get-tuple-element.385.dn0, f32[768,480]{1,0:T(8,128)S(1)} %get-tuple-element.386.dn1, bf16[480,768]{1,0:T(8,128)(2,1)S(1)} %get-tuple-element.293.x_r, ...), custom_call_target="tpu_custom_call" | custom-call | flops 40000000000 | bytes 60000000 | tf_op jit(solution)/shard_map/finish_body/pallas_call | solution.py:59
  126.3 4.9 %collective-permute-done.32.passed = bf16[608,384]{1,0:T(8,128)(2,1)S(1)} collective-permute-done((bf16[608,384]{1,0:T(8,128)(2,1)S(1)}, bf16[608,384]{1,0:T(8,128)(2,1)S(1)}, u32[]{:S(2)}, u32[]{:S(2)}) %collective-permute-start.32) | collective-permute-done | bytes 466976 | tf_op jit(solution)/shard_map/ppermute | solution.py:25
  132.2 2.6 %collective-permute-start.35 = (bf16[320,384]{1,0:T(8,128)(2,1)S(1)}, bf16[320,384]{1,0:T(8,128)(2,1)S(1)}, u32[]{:S(2)}, u32[]{:S(2)}) collective-permute-start(bf16[320,384]{1,0:T(8,128)(2,1)S(1)} %get-tuple-element.408), channel_id=1, source_target_pairs={{0,16},{1,17},{2,18},{3,19},{4,20},{5,21},{6,22},{7,23},{8,24},{9,... | collective-permute-start | bytes 737288 | tf_op jit(solution)/shard_map/ppermute | solution.py:25
  134.8 2.7 %join_body.2 = bf16[2,832,768]{2,1,0:T(8,128)(2,1)} custom-call(s32[2]{0:T(128)S(1)} %pad_add_fusion.info, s32[2,832]{1,0:T(2,128)S(1)} %copy-done.18, bf16[480,768]{1,0:T(8,128)(2,1)S(1)} %get-tuple-element.403.own, bf16[480,768]{1,0:T(8,128)(2,1)S(1)} %copy-done.13, bf16[480,768]{1,0:T(8,128)(2,1)S(1)} %collective-permute-done.26.across, ...), custom_call_target="tpu_custom_call" | custom-call | flops 40000000000 | bytes 60000000 | tf_op jit(solution)/shard_map/join_body/pallas_call | solution.py:59
  138.4 8.2 %collective-permute-done.35.got = bf16[320,384]{1,0:T(8,128)(2,1)S(1)} collective-permute-done((bf16[320,384]{1,0:T(8,128)(2,1)S(1)}, bf16[320,384]{1,0:T(8,128)(2,1)S(1)}, u32[]{:S(2)}, u32[]{:S(2)}) %collective-permute-start.35) | collective-permute-done | bytes 245792 | tf_op jit(solution)/shard_map/ppermute | solution.py:25
  146.6 3.6 %collective-permute-done.36.passed = bf16[592,384]{1,0:T(8,128)(2,1)S(1)} collective-permute-done((bf16[592,384]{1,0:T(8,128)(2,1)S(1)}, bf16[592,384]{1,0:T(8,128)(2,1)S(1)}, u32[]{:S(2)}, u32[]{:S(2)}) %collective-permute-start.36) | collective-permute-done | bytes 454688 | tf_op jit(solution)/shard_map/ppermute | solution.py:25
  156.0 3.0 %collective-permute-done.41.refs_0_ = bf16[176,384]{1,0:T(8,128)(2,1)S(1)} collective-permute-done((bf16[176,384]{1,0:T(8,128)(2,1)S(1)}, bf16[176,384]{1,0:T(8,128)(2,1)S(1)}, u32[]{:S(2)}, u32[]{:S(2)}) %collective-permute-start.41) | collective-permute-done | bytes 135200 | tf_op jit(solution)/shard_map/ppermute | solution.py:25
  (167 shorter events, 64.7 us)
Async XLA Ops:
  6.8 10.7 %collective-permute-start.2 = (bf16[1,160,384]{2,1,0:T(8,128)(2,1)S(1)}, bf16[1,160,384]{2,1,0:T(8,128)(2,1)S(1)}, u32[]{:S(2)}, u32[]{:S(2)}) collective-permute-start(bf16[1,160,384]{2,1,0:T(8,128)(2,1)S(1)} %meet_a_body.1.refs_0_), channel_id=1, source_target_pairs={{0,8},{1,9},{2,10},{3,11},{4,12},{5,13},{6,14},{7,15},{8,0},{9,1},... | collective-permute-start | bytes 368648 | tf_op jit(solution)/shard_map/ppermute | solution.py:25
  9.9 12.4 %collective-permute-start.3 = (bf16[1,160,384]{2,1,0:T(8,128)(2,1)S(1)}, bf16[1,160,384]{2,1,0:T(8,128)(2,1)S(1)}, u32[]{:S(2)}, u32[]{:S(2)}) collective-permute-start(bf16[1,160,384]{2,1,0:T(8,128)(2,1)S(1)} %meet_a_body.1.refs_0_), channel_id=1, source_target_pairs={{0,16},{1,17},{2,18},{3,19},{4,20},{5,21},{6,22},{7,23},{8,24},{9,... | collective-permute-start | bytes 368648 | tf_op jit(solution)/shard_map/ppermute | solution.py:25
  12.5 9.8 %collective-permute-start.4 = (bf16[1,160,384]{2,1,0:T(8,128)(2,1)S(1)}, bf16[1,160,384]{2,1,0:T(8,128)(2,1)S(1)}, u32[]{:S(2)}, u32[]{:S(2)}) collective-permute-start(bf16[1,160,384]{2,1,0:T(8,128)(2,1)S(1)} %meet_a_body.1.refs_0_), channel_id=1, source_target_pairs={{0,24},{1,25},{2,26},{3,27},{4,28},{5,29},{6,30},{7,31},{8,16},{9,... | collective-permute-start | bytes 368648 | tf_op jit(solution)/shard_map/ppermute | solution.py:25
  22.4 15.0 %collective-permute-start.10 = (bf16[4,160,384]{2,1,0:T(8,128)(2,1)S(1)}, bf16[4,160,384]{2,1,0:T(8,128)(2,1)S(1)}, u32[]{:S(2)}, u32[]{:S(2)}) collective-permute-start(bf16[4,160,384]{2,1,0:T(8,128)(2,1)S(1)} %stack_body.2.refs_0_), channel_id=1, source_target_pairs={{0,2},{1,3},{2,0},{3,1},{4,6},{5,7},{6,4},{7,5},{8,10},{9,11},{10,... | collective-permute-start | bytes 1474568 | tf_op jit(solution)/shard_map/ppermute | solution.py:25
  24.0 13.4 %collective-permute-start.9 = (bf16[4,160,384]{2,1,0:T(8,128)(2,1)S(1)}, bf16[4,160,384]{2,1,0:T(8,128)(2,1)S(1)}, u32[]{:S(2)}, u32[]{:S(2)}) collective-permute-start(bf16[4,160,384]{2,1,0:T(8,128)(2,1)S(1)} %stack_body.2.refs_0_), channel_id=1, source_target_pairs={{0,4},{1,5},{2,6},{3,7},{4,0},{5,1},{6,2},{7,3},{8,12},{9,13},{10,... | collective-permute-start | bytes 1474568 | tf_op jit(solution)/shard_map/ppermute | solution.py:25
  25.5 8.4 %collective-permute-start.6 = (bf16[1,144,384]{2,1,0:T(8,128)(2,1)S(1)}, bf16[1,144,384]{2,1,0:T(8,128)(2,1)S(1)}, u32[]{:S(2)}, u32[]{:S(2)}) collective-permute-start(bf16[1,144,384]{2,1,0:T(8,128)(2,1)S(1)} %meet_b_body.1.refs_0_), channel_id=1, source_target_pairs={{0,8},{1,9},{2,10},{3,11},{4,12},{5,13},{6,14},{7,15},{8,0},{9,1},... | collective-permute-start | bytes 331784 | tf_op jit(solution)/shard_map/ppermute | solution.py:25
  27.5 9.9 %collective-permute-start.7 = (bf16[1,144,384]{2,1,0:T(8,128)(2,1)S(1)}, bf16[1,144,384]{2,1,0:T(8,128)(2,1)S(1)}, u32[]{:S(2)}, u32[]{:S(2)}) collective-permute-start(bf16[1,144,384]{2,1,0:T(8,128)(2,1)S(1)} %meet_b_body.1.refs_0_), channel_id=1, source_target_pairs={{0,16},{1,17},{2,18},{3,19},{4,20},{5,21},{6,22},{7,23},{8,24},{9,... | collective-permute-start | bytes 331784 | tf_op jit(solution)/shard_map/ppermute | solution.py:25
  28.5 8.9 %collective-permute-start.8 = (bf16[1,144,384]{2,1,0:T(8,128)(2,1)S(1)}, bf16[1,144,384]{2,1,0:T(8,128)(2,1)S(1)}, u32[]{:S(2)}, u32[]{:S(2)}) collective-permute-start(bf16[1,144,384]{2,1,0:T(8,128)(2,1)S(1)} %meet_b_body.1.refs_0_), channel_id=1, source_target_pairs={{0,24},{1,25},{2,26},{3,27},{4,28},{5,29},{6,30},{7,31},{8,16},{9,... | collective-permute-start | bytes 331784 | tf_op jit(solution)/shard_map/ppermute | solution.py:25
  38.0 15.0 %collective-permute-start.14 = (bf16[4,160,384]{2,1,0:T(8,128)(2,1)S(1)}, bf16[4,160,384]{2,1,0:T(8,128)(2,1)S(1)}, u32[]{:S(2)}, u32[]{:S(2)}) collective-permute-start(bf16[4,160,384]{2,1,0:T(8,128)(2,1)S(1)} %stack_body.2.refs_0_), channel_id=1, source_target_pairs={{0,6},{1,7},{2,4},{3,5},{4,2},{5,3},{6,0},{7,1},{8,14},{9,15},{10,... | collective-permute-start | bytes 1474568 | tf_op jit(solution)/shard_map/ppermute | solution.py:25
  41.7 21.9 %collective-permute-start.17 = (bf16[4,144,384]{2,1,0:T(8,128)(2,1)S(1)}, bf16[4,144,384]{2,1,0:T(8,128)(2,1)S(1)}, u32[]{:S(2)}, u32[]{:S(2)}) collective-permute-start(bf16[4,144,384]{2,1,0:T(8,128)(2,1)S(1)} %stack_body.3.refs_0_), channel_id=1, source_target_pairs={{0,4},{1,5},{2,6},{3,7},{4,0},{5,1},{6,2},{7,3},{8,12},{9,13},{10,... | collective-permute-start | bytes 1327112 | tf_op jit(solution)/shard_map/ppermute | solution.py:25
  42.3 21.3 %collective-permute-start.18 = (bf16[4,144,384]{2,1,0:T(8,128)(2,1)S(1)}, bf16[4,144,384]{2,1,0:T(8,128)(2,1)S(1)}, u32[]{:S(2)}, u32[]{:S(2)}) collective-permute-start(bf16[4,144,384]{2,1,0:T(8,128)(2,1)S(1)} %stack_body.3.refs_0_), channel_id=1, source_target_pairs={{0,2},{1,3},{2,0},{3,1},{4,6},{5,7},{6,4},{7,5},{8,10},{9,11},{10,... | collective-permute-start | bytes 1327112 | tf_op jit(solution)/shard_map/ppermute | solution.py:25
  43.3 27.8 %collective-permute-start.21 = (bf16[4,144,384]{2,1,0:T(8,128)(2,1)S(1)}, bf16[4,144,384]{2,1,0:T(8,128)(2,1)S(1)}, u32[]{:S(2)}, u32[]{:S(2)}) collective-permute-start(bf16[4,144,384]{2,1,0:T(8,128)(2,1)S(1)} %stack_body.3.refs_0_), channel_id=1, source_target_pairs={{0,6},{1,7},{2,4},{3,5},{4,2},{5,3},{6,0},{7,1},{8,14},{9,15},{10,... | collective-permute-start | bytes 1327112 | tf_op jit(solution)/shard_map/ppermute | solution.py:25
  78.0 25.3 %collective-permute-start.26 = (bf16[480,768]{1,0:T(8,128)(2,1)S(1)}, bf16[480,768]{1,0:T(8,128)(2,1)S(1)}, u32[]{:S(2)}, u32[]{:S(2)}) collective-permute-start(bf16[480,768]{1,0:T(8,128)(2,1)S(1)} %get-tuple-element.403.own), channel_id=1, source_target_pairs={{0,2},{1,3},{2,0},{3,1},{4,6},{5,7},{6,4},{7,5},{8,10},{9,11},{10,... | collective-permute-start | bytes 2211848 | tf_op jit(solution)/shard_map/ppermute | solution.py:25
  92.9 25.8 %collective-permute-start.29 = (bf16[1184,384]{1,0:T(8,128)(2,1)S(1)}, bf16[1184,384]{1,0:T(8,128)(2,1)S(1)}, u32[]{:S(2)}, u32[]{:S(2)}) collective-permute-start(bf16[1184,384]{1,0:T(8,128)(2,1)S(1)} %get-tuple-element.373), channel_id=1, source_target_pairs={{0,2},{1,3},{2,0},{3,1},{4,6},{5,7},{6,4},{7,5},{8,10},{9,11},{10,... | collective-permute-start | bytes 2727944 | tf_op jit(solution)/shard_map/ppermute | solution.py:25
  110.7 15.5 %collective-permute-start.31 = (bf16[576,384]{1,0:T(8,128)(2,1)S(1)}, bf16[576,384]{1,0:T(8,128)(2,1)S(1)}, u32[]{:S(2)}, u32[]{:S(2)}) collective-permute-start(bf16[576,384]{1,0:T(8,128)(2,1)S(1)} %get-tuple-element.393), channel_id=1, source_target_pairs={{0,2},{1,3},{2,0},{3,1},{4,6},{5,7},{6,4},{7,5},{8,10},{9,11},{10,... | collective-permute-start | bytes 1327112 | tf_op jit(solution)/shard_map/ppermute | solution.py:25
  111.3 35.3 %collective-permute-start.37 = (bf16[576,384]{1,0:T(8,128)(2,1)}, bf16[576,384]{1,0:T(8,128)(2,1)}, u32[]{:S(2)}, u32[]{:S(2)}) collective-permute-start(bf16[576,384]{1,0:T(8,128)(2,1)} %get-tuple-element.416), channel_id=1, source_target_pairs={{0,2},{1,3},{2,0},{3,1},{4,6},{5,7},{6,4},{7,5},{8,10},{9,11},{10,... | collective-permute-start | bytes 1327112 | tf_op jit(solution)/shard_map/ppermute | solution.py:25
  119.0 12.2 %collective-permute-start.32 = (bf16[608,384]{1,0:T(8,128)(2,1)S(1)}, bf16[608,384]{1,0:T(8,128)(2,1)S(1)}, u32[]{:S(2)}, u32[]{:S(2)}) collective-permute-start(bf16[608,384]{1,0:T(8,128)(2,1)S(1)} %get-tuple-element.396), channel_id=1, source_target_pairs={{0,4},{1,5},{2,6},{3,7},{4,0},{5,1},{6,2},{7,3},{8,12},{9,13},{10,... | collective-permute-start | bytes 1400840 | tf_op jit(solution)/shard_map/ppermute | solution.py:25
  123.1 8.1 %collective-permute-start.30 = (bf16[2,4,144,384]{3,2,1,0:T(8,128)(2,1)S(1)}, bf16[2,4,144,384]{3,2,1,0:T(8,128)(2,1)S(1)}, u32[]{:S(2)}, u32[]{:S(2)}) collective-permute-start(bf16[2,4,144,384]{3,2,1,0:T(8,128)(2,1)S(1)} %get-tuple-element.392), channel_id=1, source_target_pairs={{0,1},{1,0},{2,3},{3,2},{4,5},{5,4},{6,7},{7,6},{8,9},{9,8},{10,11... | collective-permute-start | bytes 2654216 | tf_op jit(solution)/shard_map/ppermute | solution.py:25
  131.2 24.8 %collective-permute-start.42 = (bf16[480,768]{1,0:T(8,128)(2,1)S(1)}, bf16[480,768]{1,0:T(8,128)(2,1)S(1)}, u32[]{:S(2)}, u32[]{:S(2)}) collective-permute-start(bf16[480,768]{1,0:T(8,128)(2,1)S(1)} %get-tuple-element.398.own), channel_id=1, source_target_pairs={{0,2},{1,3},{2,0},{3,1},{4,6},{5,7},{6,4},{7,5},{8,10},{9,11},{10,... | collective-permute-start | bytes 2211848 | tf_op jit(solution)/shard_map/ppermute | solution.py:25
  132.2 14.3 %collective-permute-start.35 = (bf16[320,384]{1,0:T(8,128)(2,1)S(1)}, bf16[320,384]{1,0:T(8,128)(2,1)S(1)}, u32[]{:S(2)}, u32[]{:S(2)}) collective-permute-start(bf16[320,384]{1,0:T(8,128)(2,1)S(1)} %get-tuple-element.408), channel_id=1, source_target_pairs={{0,16},{1,17},{2,18},{3,19},{4,20},{5,21},{6,22},{7,23},{8,24},{9,... | collective-permute-start | bytes 737288 | tf_op jit(solution)/shard_map/ppermute | solution.py:25
  137.8 12.4 %collective-permute-start.36 = (bf16[592,384]{1,0:T(8,128)(2,1)S(1)}, bf16[592,384]{1,0:T(8,128)(2,1)S(1)}, u32[]{:S(2)}, u32[]{:S(2)}) collective-permute-start(bf16[592,384]{1,0:T(8,128)(2,1)S(1)} %get-tuple-element.415), channel_id=1, source_target_pairs={{0,4},{1,5},{2,6},{3,7},{4,0},{5,1},{6,2},{7,3},{8,12},{9,13},{10,... | collective-permute-start | bytes 1363976 | tf_op jit(solution)/shard_map/ppermute | solution.py:25
  151.5 13.6 %collective-permute-start.38 = (bf16[160,384]{1,0:T(8,128)(2,1)S(1)}, bf16[160,384]{1,0:T(8,128)(2,1)S(1)}, u32[]{:S(2)}, u32[]{:S(2)}) collective-permute-start(bf16[160,384]{1,0:T(8,128)(2,1)S(1)} %get-tuple-element.429), channel_id=1, source_target_pairs={{0,8},{1,9},{2,10},{3,11},{4,12},{5,13},{6,14},{7,15},{8,0},{9,1},... | collective-permute-start | bytes 368648 | tf_op jit(solution)/shard_map/ppermute | solution.py:25
  153.5 11.6 %collective-permute-start.39 = (bf16[160,384]{1,0:T(8,128)(2,1)S(1)}, bf16[160,384]{1,0:T(8,128)(2,1)S(1)}, u32[]{:S(2)}, u32[]{:S(2)}) collective-permute-start(bf16[160,384]{1,0:T(8,128)(2,1)S(1)} %get-tuple-element.430), channel_id=1, source_target_pairs={{0,16},{1,17},{2,18},{3,19},{4,20},{5,21},{6,22},{7,23},{8,24},{9,... | collective-permute-start | bytes 368648 | tf_op jit(solution)/shard_map/ppermute | solution.py:25
  154.3 10.8 %collective-permute-start.40 = (bf16[160,384]{1,0:T(8,128)(2,1)S(1)}, bf16[160,384]{1,0:T(8,128)(2,1)S(1)}, u32[]{:S(2)}, u32[]{:S(2)}) collective-permute-start(bf16[160,384]{1,0:T(8,128)(2,1)S(1)} %get-tuple-element.431), channel_id=1, source_target_pairs={{0,24},{1,25},{2,26},{3,27},{4,28},{5,29},{6,30},{7,31},{8,16},{9,... | collective-permute-start | bytes 368648 | tf_op jit(solution)/shard_map/ppermute | solution.py:25
  (43 other events, 237.9 us)
